TPU v7x, 256 devices: a whole 4x4x8 slice. The times are simulated.
256 devices in a mesh: geo: 4 (over y), region: 16 (over z, core), sub: 4 (over x).
Axes of the slice: x: 4, y: 4, z: 8, core: 2. Of those that a mesh axis runs over, the one named last changes fastest.
Arguments:
- features: bfloat16 [4, 32, 131072], P('geo', None, ('region', 'sub')), may hold values from -6 to 6
- lap_tiles: bfloat16 [4, 1024, 4, 128, 128], P('geo', ('region', 'sub')), may hold values from -0.25 to 0.25
- tile_cols: int32 [4, 1024, 4], P('geo', ('region', 'sub')), may hold values from 0 to 17
- coarse_owner: int32 [4, 131072, 1], P('geo', ('region', 'sub')), may hold values from 0 to 63; in each aligned block of 2048 rows (0 to 2047, 2048 to 4095, ..., all dimensions but the last counted through in order) at most 128 rows name the same one
- coarse_slot: int32 [4, 131072], P('geo', ('region', 'sub')), may hold values from 0 to 511
- pool_weight: float32 [4, 131072], P('geo', ('region', 'sub')), may hold values from 0.25 to 1
- weight_in: bfloat16 [3, 32, 32], replicated, may hold values from -0.625 to 0.625
- weight_mid: bfloat16 [32, 32], replicated, may hold values from -1 to 1
- weight_out: bfloat16 [3, 32, 32], replicated, may hold values from -0.625 to 0.625
- biases: float32 [2, 32], replicated, may hold values from -3 to 3
- out_grad: bfloat16 [4, 32, 131072], P('geo', None, ('region', 'sub')), may hold values from -6 to 6
Outputs:
- result: bfloat16 [4, 32, 131072], P('geo', None, ('region', 'sub'))
- input_grad: bfloat16 [4, 32, 131072], P('geo', None, ('region', 'sub'))
- weight_grads: float32 [7, 32, 32], replicated
- bias_grads: float32 [2, 32], replicated
Inputs may be any that keep to these rules, and one draw needn't show every extreme that they name: `coarse_owner`: among the 2048 fine vertices of one device (aligned blocks along the vertices, geometries in order) no owner is named more than 128 times, and in every draw some owner is named exactly 128 times. `tile_cols`: entry 0 reads the last tile of the device before, 1 to 16 the device's own tiles, 17 the first tile of the device after.
All inputs are finite; a program needn't handle non-finite values.
Results may differ from a plain program's by a relative error of at most 0.02.
Values may be sent and summed in bfloat16 or wider, within the bound.
No kernel may reach another device: no remote copies, remote signals or barrier semaphores. Data moves between devices by JAX's collectives and lax.ppermute only.
A program may use at most 64 MiB of HBM per device.

v0:
```python
import math

import jax
import jax.numpy as jnp
from jax import lax
from jax.sharding import PartitionSpec as P


def with_halo(block, sides, width):
    for axis, dim in sides:
        count = lax.axis_size(axis)
        forward = [(i, i + 1) for i in range(count - 1)]
        backward = [(target, source) for source, target in forward]
        low = lax.ppermute(
            lax.slice_in_dim(block, block.shape[dim] - width, None, axis=dim), axis, forward
        )
        high = lax.ppermute(lax.slice_in_dim(block, 0, width, axis=dim), axis, backward)
        block = jnp.concatenate([low, block, high], axis=dim)
    return block


def passed_along(value, axis, by):
    peers = lax.axis_size(axis)
    pairs = [(i, i + by) for i in range(peers) if 0 <= i + by < peers]
    return lax.ppermute(value, axis, pairs)


def sent_to_all(value, axis):
    peers = lax.axis_size(axis)
    return lax.all_to_all(
        jnp.broadcast_to(value[None], (peers, *value.shape)), axis, 0, 0, tiled=True
    )


def taken_together(value, axis):
    everything = sent_to_all(value, axis)
    return jnp.sum(everything, axis=0)


def in_one(arrays, axis):
    ends = [0]
    for a in arrays:
        ends.append(ends[-1] + a.size)
    running = taken_together(jnp.concatenate([a.ravel() for a in arrays]), axis)
    return tuple((running[b:e].reshape(a.shape) for a, b, e in zip(arrays, ends, ends[1:])))


def apply_operator(field, tiles, columns):
    count = tiles.shape[0]
    nonzero = tiles.shape[1]
    width = tiles.shape[2]
    chans = field.shape[0]
    padded = with_halo(field, ((("region", "sub"), 1),), width)
    blocks = padded.reshape(chans, count + 2, width)
    placed = (
        columns.reshape(-1)[:, None] == jnp.arange(count + 2, dtype=jnp.int32)[None, :]
    ).astype(jnp.bfloat16)
    picked = jnp.einsum("cmt,jm->cjt", blocks, placed, preferred_element_type=jnp.float32).astype(
        jnp.bfloat16
    )
    picked = picked.reshape(chans, count, nonzero, width)
    product = jnp.einsum("cknt,kntu->cku", picked, tiles, preferred_element_type=jnp.float32)
    return product.reshape(chans, count * width)


def apply_transpose(grad, tiles, columns):
    count = tiles.shape[0]
    nonzero = tiles.shape[1]
    width = tiles.shape[2]
    chans = grad.shape[0]
    blocks = grad.reshape(chans, count, width)
    contrib = jnp.einsum("cku,kntu->cknt", blocks, tiles, preferred_element_type=jnp.float32)
    placed = (
        columns.reshape(-1)[:, None] == jnp.arange(count + 2, dtype=jnp.int32)[None, :]
    ).astype(jnp.float32)
    extended = jnp.einsum(
        "cjt,jm->cmt",
        contrib.reshape(chans, count * nonzero, width),
        placed,
        precision=lax.Precision.HIGHEST,
    )
    from_next = passed_along(extended[:, 0], ("region", "sub"), -1)
    from_prev = passed_along(extended[:, count + 1], ("region", "sub"), 1)
    inner = extended[:, 1 : count + 1]
    inner = inner.at[:, count - 1].add(from_next).at[:, 0].add(from_prev)
    return inner.reshape(chans, count * width)


def mixdot(weight, field):
    return jnp.dot(weight, field, preferred_element_type=jnp.float32)


def cheb_forward(field, weights, tiles, columns):
    first = apply_operator(field, tiles, columns).astype(jnp.bfloat16)
    second = (2.0 * apply_operator(first, tiles, columns) - field.astype(jnp.float32)).astype(
        jnp.bfloat16
    )
    output = mixdot(weights[0], field) + mixdot(weights[1], first) + mixdot(weights[2], second)
    return (output, (field, first, second))


def cheb_backward(grad, weights, tiles, columns):
    second = mixdot(weights[2].T, grad).astype(jnp.bfloat16)
    first = (mixdot(weights[1].T, grad) + 2.0 * apply_transpose(second, tiles, columns)).astype(
        jnp.bfloat16
    )
    return (
        mixdot(weights[0].T, grad)
        - second.astype(jnp.float32)
        + apply_transpose(first, tiles, columns)
    )


def silu_slope(value):
    sig = jax.nn.sigmoid(value)
    return sig * (1.0 + value * (1.0 - sig))


def outer_sum(left, right):
    return jnp.einsum("cn,dn->cd", left, right, preferred_element_type=jnp.float32)


def pack_slots(message, own_hot, rank_hot):
    chans = message.shape[0]
    masked = message[:, None, :] * own_hot[None, :, :]
    packed = jnp.einsum("coi,ir->cor", masked, rank_hot, preferred_element_type=jnp.float32)
    return packed.astype(jnp.bfloat16).reshape(chans, -1)


def unpack_slots(back, own_hot, rank_hot):
    spread = jnp.einsum("cor,ir->coi", back, rank_hot, preferred_element_type=jnp.float32)
    return jnp.sum(spread * own_hot.astype(jnp.float32)[None, :, :], axis=1).astype(jnp.bfloat16)


def joint_to_owners(message, id_buffer, own_hot, rank_hot, regions, subs, slots):
    chans = message.shape[0]
    peers = regions * subs
    buffer = pack_slots(message, own_hot, rank_hot)
    got, got_ids = (
        lax.all_to_all(
            buffer.reshape(chans, peers, slots),
            ("region", "sub"),
            split_axis=1,
            concat_axis=1,
            tiled=True,
        ),
        lax.all_to_all(
            id_buffer.reshape(1, peers, slots),
            ("region", "sub"),
            split_axis=1,
            concat_axis=1,
            tiled=True,
        ),
    )
    return (got.reshape(chans, peers * slots), got_ids.reshape(peers * slots))


def joint_from_owners(values, coarse_hot, own_hot, rank_hot, regions, subs, slots):
    chans = values.shape[0]
    peers = regions * subs
    buffer = jnp.einsum("cj,sj->cs", values, coarse_hot, preferred_element_type=jnp.float32).astype(
        jnp.bfloat16
    )
    back = lax.all_to_all(
        buffer.reshape(chans, peers, slots),
        ("region", "sub"),
        split_axis=1,
        concat_axis=1,
        tiled=True,
    )
    return unpack_slots(back, own_hot, rank_hot)


def coarse_onehot(received_ids, coarse_rows):
    return (received_ids[:, None] == jnp.arange(coarse_rows, dtype=jnp.int32)[None, :]).astype(
        jnp.bfloat16
    )


def coarse_total(received, coarse_hot):
    return jnp.dot(received, coarse_hot, preferred_element_type=jnp.float32)


def on_device(
    features,
    lap_tiles,
    tile_cols,
    coarse_owner,
    coarse_slot,
    pool_weight,
    weight_in,
    weight_mid,
    weight_out,
    biases,
    out_grad,
):
    field = features[0]
    tiles = lap_tiles[0]
    columns = tile_cols[0]
    owners = coarse_owner[0, :, 0]
    parents = coarse_slot[0]
    weight_row = pool_weight[0][None, :]
    upstream = out_grad[0]
    rows = field.shape[1]
    chans = field.shape[0]
    regions = lax.axis_size("region")
    subs = lax.axis_size("sub")
    peers = regions * subs
    slots = 4 * rows // peers
    coarse_rows = rows // 4
    positions = jnp.arange(rows, dtype=jnp.int32)
    same_owner = (owners[:, None] == owners[None, :]) & (positions[None, :] < positions[:, None])
    rank = jnp.sum(same_owner.astype(jnp.int32), axis=1)
    own_bool = owners[None, :] == jnp.arange(peers, dtype=jnp.int32)[:, None]
    rank_bool = rank[:, None] == jnp.arange(slots, dtype=jnp.int32)[None, :]
    own_hot = own_bool.astype(jnp.bfloat16)
    rank_hot = rank_bool.astype(jnp.bfloat16)
    id_terms = own_bool.astype(jnp.float32) * (parents.astype(jnp.float32) + 1.0)[None, :]
    id_sums = jnp.dot(
        id_terms, rank_bool.astype(jnp.float32), precision=lax.Precision.HIGHEST
    ).reshape(peers * slots)
    id_buffer = jnp.where(id_sums > 0.5, id_sums - 1.0, jnp.float32(coarse_rows)).astype(jnp.int32)
    pre_sum, terms_in = cheb_forward(field, weight_in, tiles, columns)
    pre_in = pre_sum + biases[0][:, None]
    hidden = jax.nn.silu(pre_in).astype(jnp.bfloat16)
    message = (weight_row * hidden.astype(jnp.float32)).astype(jnp.bfloat16)
    merged_grad = cheb_backward(upstream, weight_out, tiles, columns).astype(jnp.bfloat16)
    grad_message = (weight_row * merged_grad.astype(jnp.float32)).astype(jnp.bfloat16)
    both_received, received_ids = joint_to_owners(
        jnp.concatenate([message, grad_message], axis=0),
        id_buffer,
        own_hot,
        rank_hot,
        regions,
        subs,
        slots,
    )
    coarse_hot = coarse_onehot(received_ids, coarse_rows)
    both_totals = coarse_total(both_received, coarse_hot)
    coarse = both_totals[:chans].astype(jnp.bfloat16)
    coarse_grad = both_totals[chans:]
    pre_mid = mixdot(weight_mid, coarse) + biases[1][:, None]
    coarse_out = jax.nn.silu(pre_mid).astype(jnp.bfloat16)
    mid_grad = (coarse_grad * silu_slope(pre_mid)).astype(jnp.bfloat16)
    coarse_back = mixdot(weight_mid.T, mid_grad).astype(jnp.bfloat16)
    both_lifted = joint_from_owners(
        jnp.concatenate([coarse_out, coarse_back], axis=0),
        coarse_hot,
        own_hot,
        rank_hot,
        regions,
        subs,
        slots,
    )
    lifted = both_lifted[:chans]
    lifted_grad = both_lifted[chans:]
    merged = (hidden.astype(jnp.float32) + weight_row * lifted.astype(jnp.float32)).astype(
        jnp.bfloat16
    )
    out_sum, terms_out = cheb_forward(merged, weight_out, tiles, columns)
    result = out_sum.astype(jnp.bfloat16)
    hidden_grad = merged_grad.astype(jnp.float32) + weight_row * lifted_grad.astype(jnp.float32)
    pre_grad = (hidden_grad * silu_slope(pre_in)).astype(jnp.bfloat16)
    input_grad = cheb_backward(pre_grad, weight_in, tiles, columns).astype(jnp.bfloat16)
    grads = [outer_sum(pre_grad, term) for term in terms_in]
    grads.append(outer_sum(mid_grad, coarse))
    grads = grads + [outer_sum(upstream, term) for term in terms_out]
    local_weights = jnp.stack(grads)
    local_biases = jnp.stack(
        [
            jnp.sum(pre_grad.astype(jnp.float32), axis=1),
            jnp.sum(mid_grad.astype(jnp.float32), axis=1),
        ]
    )
    part_weights, part_biases = in_one((local_weights, local_biases), ("region", "sub"))
    sum_weights, sum_biases = in_one((part_weights, part_biases), "geo")
    factor = 1.0 / math.sqrt(lax.axis_size("geo") * rows * peers)
    return (result[None], input_grad[None], sum_weights * factor, sum_biases * factor)


def solution(mesh):
    in_specs = (
        P("geo", None, ("region", "sub")),
        P("geo", ("region", "sub"), None, None, None),
        P("geo", ("region", "sub"), None),
        P("geo", ("region", "sub"), None),
        P("geo", ("region", "sub")),
        P("geo", ("region", "sub")),
        P(),
        P(),
        P(),
        P(),
        P("geo", None, ("region", "sub")),
    )
    out_specs = (P("geo", None, ("region", "sub")), P("geo", None, ("region", "sub")), P(), P())
    return jax.shard_map(
        on_device, mesh=mesh, in_specs=in_specs, out_specs=out_specs, check_vma=False
    )
```

profile of v0, /device:TPU:128, one launch (start us, length us, event | category | flops | bytes accessed | tf_op | source)
XLA Modules:
  0.0 272.6 jit_solution(4358689548934831350)
XLA Ops:
  0.6 0.9 fusion.204
  1.5 3.4 %collective-permute-start = (bf16[32,128]{1,0:T(8,128)(2,1)S(1)}, bf16[32,128]{1,0:T(8,128)(2,1)S(1)}, u32[]{:S(2)}, u32[]{:S(2)}) collective-permute-start(bf16[32,128]{1,0:T(8,128)(2,1)S(1)} %get-tuple-element.124), channel_id=1, source_target_pairs={{0,1},{1,2},{2,3},{3,4},{4,5},{5,6},{6,7},{7,8},{8,9},{9,10},{10,1... | collective-permute-start | bytes 24584 | tf_op jit(solution)/shard_map/ppermute | solution.py:14
  4.9 5.5 %collective-permute-start.1 = (bf16[32,128]{1,0:T(8,128)(2,1)S(1)}, bf16[32,128]{1,0:T(8,128)(2,1)S(1)}, u32[]{:S(2)}, u32[]{:S(2)}) collective-permute-start(bf16[32,128]{1,0:T(8,128)(2,1)S(1)} %get-tuple-element.125), channel_id=1, source_target_pairs={{1,0},{2,1},{3,2},{4,3},{5,4},{6,5},{7,6},{8,7},{9,8},{10,9},{11,1... | collective-permute-start | bytes 24584 | tf_op jit(solution)/shard_map/ppermute | solution.py:17
  10.4 5.2 %convert_reduce_fusion = s32[2048]{0:T(1024)S(1)} fusion(s32[2048]{0:T(1024)} %bitcast.447), kind=kLoop, calls=%fused_computation.4 | loop fusion | flops 20969472 | bytes 16384 | tf_op jit(solution)/shard_map/reduce_sum | solution.py:213
  16.3 1.9 select_convert_fusion
  18.3 8.1 %all-to-all-start.1 = ((s32[1,64,128]{2,0,1:T(1,128)}), s32[1,64,128]{2,0,1:T(1,128)}, u32[]{:S(2)}, u32[]{:S(2)}) async-start(s32[1,64,128]{2,0,1:T(1,128)} %bitcast.44), calls=%async_computation.1 | async-start | bytes 65536 | tf_op jit(solution)/shard_map/all_to_all | solution.py:147
  27.2 1.1 convolution_convert_fusion.1
  29.2 1.1 convolution_bitcast_fusion.6
  30.9 3.4 %collective-permute-start.5 = (f32[32,128]{1,0:T(8,128)}, f32[32,128]{1,0:T(8,128)}, u32[]{:S(2)}, u32[]{:S(2)}) collective-permute-start(f32[32,128]{1,0:T(8,128)} %bitcast.30), channel_id=1, source_target_pairs={{0,1},{1,2},{2,3},{3,4},{4,5},{5,6},{6,7},{7,8},{8,9},{9,10},{10,1... | collective-permute-start | bytes 49160 | tf_op jit(solution)/shard_map/ppermute | solution.py:25
  34.3 5.5 %collective-permute-start.4 = (f32[32,128]{1,0:T(8,128)}, f32[32,128]{1,0:T(8,128)}, u32[]{:S(2)}, u32[]{:S(2)}) collective-permute-start(f32[32,128]{1,0:T(8,128)} %bitcast.28), channel_id=1, source_target_pairs={{1,0},{2,1},{3,2},{4,3},{5,4},{6,5},{7,6},{8,7},{9,8},{10,9},{11,1... | collective-permute-start | bytes 49160 | tf_op jit(solution)/shard_map/ppermute | solution.py:25
  39.8 1.0 fusion.109
  40.8 1.6 fusion.168
  43.5 1.9 collective-permute-start.2
  45.4 7.0 %collective-permute-start.3 = (bf16[32,128]{1,0:T(8,128)(2,1)S(1)}, bf16[32,128]{1,0:T(8,128)(2,1)S(1)}, u32[]{:S(2)}, u32[]{:S(2)}) collective-permute-start(bf16[32,128]{1,0:T(8,128)(2,1)S(1)} %get-tuple-element.123), channel_id=1, source_target_pairs={{1,0},{2,1},{3,2},{4,3},{5,4},{6,5},{7,6},{8,7},{9,8},{10,9},{11,1... | collective-permute-start | bytes 24584 | tf_op jit(solution)/shard_map/ppermute | solution.py:17
  53.8 1.0 convolution_convert_fusion.4
  57.0 0.9 fusion.79
  58.8 1.1 convolution_bitcast_fusion.5
  59.9 1.9 collective-permute-start.7
  61.8 7.1 %collective-permute-start.6 = (f32[32,128]{1,0:T(8,128)S(1)}, f32[32,128]{1,0:T(8,128)S(1)}, u32[]{:S(2)}, u32[]{:S(2)}) collective-permute-start(f32[32,128]{1,0:T(8,128)S(1)} %bitcast.446), channel_id=1, source_target_pairs={{1,0},{2,1},{3,2},{4,3},{5,4},{6,5},{7,6},{8,7},{9,8},{10,9},{11,1... | collective-permute-start | bytes 49160 | tf_op jit(solution)/shard_map/ppermute | solution.py:25
  69.3 0.8 collective-permute-done.6
  70.2 0.9 fusion.18
  71.2 1.0 fusion.110
  72.2 4.7 %fusion.41 = bf16[64,64,128]{2,1,0:T(8,128)(2,1)S(1)} fusion(bf16[64,2048]{1,0:T(8,128)(2,1)S(1)} %copy-done.10, bf16[64,2048]{1,0:T(8,128)(2,1)S(1)} %pad_maximum_fusion, s32[2048]{0:T(1024)S(1)} %copy-done.29), kind=kOutput, calls=%fused_computation.55 | convolution fusion | flops 2156658688 | bytes 1581056 | tf_op jit(solution)/shard_map/coi,ir->cor/dot_general | solution.py:126
  77.6 35.5 %all_to_all.27 = bf16[64,64,128]{2,0,1:T(8,128)(2,1)S(1)} all-to-all(bf16[64,64,128]{2,0,1:T(8,128)(2,1)S(1)} %copy.221), channel_id=1, replica_groups=mesh['geo'=4,'region'=16,'sub'=4] {'region','sub'}, dimensions={1} | all-to-all | bytes 2097152 | tf_op jit(solution)/shard_map/all_to_all | solution.py:140
  113.1 3.8 %fusion.1 = f32[64,512]{1,0:T(8,128)S(1)} fusion(s32[8192]{0:T(1024)} %bitcast.45, bf16[64,64,128]{2,0,1:T(8,128)(2,1)S(1)} %all_to_all.27), kind=kOutput, calls=%fused_computation.3 | convolution fusion | flops 541065216 | bytes 1212416 | tf_op jit(solution)/shard_map/dot_general | solution.py:181
  117.3 4.8 %fusion.44 = bf16[8,64,8,128]{3,2,1,0:T(8,128)(2,1)S(1)} fusion(s32[8192]{0:T(1024)} %bitcast.45, bf16[32,512]{1,0:T(8,128)(2,1)S(1)} %fusion.81, bf16[32,512]{1,0:T(8,128)(2,1)S(1)} %get-tuple-element.126), kind=kOutput, calls=%fused_computation.56 | convolution fusion | flops 541720576 | bytes 1146880 | tf_op jit(solution)/shard_map/cj,sj->cs/dot_general | solution.py:161
  122.4 34.0 %all_to_all.28 = bf16[64,64,128]{2,0,1:T(8,128)(2,1)S(1)} all-to-all(bf16[64,64,128]{2,0,1:T(8,128)(2,1)S(1)} %bitcast.419), channel_id=1, replica_groups=mesh['geo'=4,'region'=16,'sub'=4] {'region','sub'}, dimensions={1} | all-to-all | bytes 2097152 | tf_op jit(solution)/shard_map/all_to_all | solution.py:164
  156.5 5.7 %multiply_reduce_fusion = bf16[64,2048]{1,0:T(8,128)(2,1)S(1)} fusion(f32[64,2048]{1,0:T(8,128)S(1)} %copy-done.7, bf16[64,64,128]{2,0,1:T(8,128)(2,1)S(1)} %all_to_all.28, s32[2048]{0:T(1024)S(1)} %copy-done.30), kind=kOutput, calls=%fused_computation | convolution fusion | flops 2164391936 | bytes 1843200 | tf_op jit(solution)/shard_map/cor,ir->coi/dot_general | solution.py:131
  162.5 2.5 collective-permute-start.8
  165.1 6.4 %collective-permute-start.9 = (bf16[32,128]{1,0:T(8,128)(2,1)S(1)}, bf16[32,128]{1,0:T(8,128)(2,1)S(1)}, u32[]{:S(2)}, u32[]{:S(2)}) collective-permute-start(bf16[32,128]{1,0:T(8,128)(2,1)S(1)} %get-tuple-element.121), channel_id=1, source_target_pairs={{1,0},{2,1},{3,2},{4,3},{5,4},{6,5},{7,6},{8,7},{9,8},{10,9},{11,1... | collective-permute-start | bytes 24584 | tf_op jit(solution)/shard_map/ppermute | solution.py:17
  174.0 1.9 collective-permute-start.10
  175.9 7.0 %collective-permute-start.11 = (bf16[32,128]{1,0:T(8,128)(2,1)S(1)}, bf16[32,128]{1,0:T(8,128)(2,1)S(1)}, u32[]{:S(2)}, u32[]{:S(2)}) collective-permute-start(bf16[32,128]{1,0:T(8,128)(2,1)S(1)} %get-tuple-element.119), channel_id=1, source_target_pairs={{1,0},{2,1},{3,2},{4,3},{5,4},{6,5},{7,6},{8,7},{9,8},{10,9},{11,1... | collective-permute-start | bytes 24584 | tf_op jit(solution)/shard_map/ppermute | solution.py:17
  183.0 1.2 collective-permute-done.11
  185.5 2.2 broadcast_in_dim.15
  187.7 10.5 %all-to-all-start.3 = ((f32[64,1,7232]{2,1,0:T(1,128)}), f32[64,1,7232]{2,1,0:T(1,128)}, u32[]{:S(2)}, u32[]{:S(2)}) async-start(f32[64,1,7232]{2,1,0:T(1,128)} %broadcast_in_dim.15), calls=%async_computation.3 | async-start | bytes 3735552 | tf_op jit(solution)/shard_map/all_to_all | solution.py:30
  199.3 1.1 fusion.92
  200.5 3.4 %collective-permute-start.13 = (f32[32,128]{1,0:T(8,128)S(1)}, f32[32,128]{1,0:T(8,128)S(1)}, u32[]{:S(2)}, u32[]{:S(2)}) collective-permute-start(f32[32,128]{1,0:T(8,128)S(1)} %get-tuple-element.115), channel_id=1, source_target_pairs={{0,1},{1,2},{2,3},{3,4},{4,5},{5,6},{6,7},{7,8},{8,9},{9,10},{10,1... | collective-permute-start | bytes 49160 | tf_op jit(solution)/shard_map/ppermute | solution.py:25
  203.9 5.5 %collective-permute-start.12 = (f32[32,128]{1,0:T(8,128)S(1)}, f32[32,128]{1,0:T(8,128)S(1)}, u32[]{:S(2)}, u32[]{:S(2)}) collective-permute-start(f32[32,128]{1,0:T(8,128)S(1)} %get-tuple-element.116), channel_id=1, source_target_pairs={{1,0},{2,1},{3,2},{4,3},{5,4},{6,5},{7,6},{8,7},{9,8},{10,9},{11,1... | collective-permute-start | bytes 49160 | tf_op jit(solution)/shard_map/ppermute | solution.py:25
  209.7 28.6 %collective-permute-done.12 = f32[32,128]{1,0:T(8,128)S(1)} collective-permute-done((f32[32,128]{1,0:T(8,128)S(1)}, f32[32,128]{1,0:T(8,128)S(1)}, u32[]{:S(2)}, u32[]{:S(2)}) %collective-permute-start.12) | collective-permute-done | bytes 16416 | tf_op jit(solution)/shard_map/ppermute | solution.py:25
  238.4 2.8 %collective-permute-done.13 = f32[32,128]{1,0:T(8,128)S(1)} collective-permute-done((f32[32,128]{1,0:T(8,128)S(1)}, f32[32,128]{1,0:T(8,128)S(1)}, u32[]{:S(2)}, u32[]{:S(2)}) %collective-permute-start.13) | collective-permute-done | bytes 16416 | tf_op jit(solution)/shard_map/ppermute | solution.py:25
  242.3 1.1 convolution_bitcast_fusion.4
  243.4 4.6 %collective-permute-start.14 = (f32[32,128]{1,0:T(8,128)S(1)}, f32[32,128]{1,0:T(8,128)S(1)}, u32[]{:S(2)}, u32[]{:S(2)}) collective-permute-start(f32[32,128]{1,0:T(8,128)S(1)} %bitcast.445), channel_id=1, source_target_pairs={{1,0},{2,1},{3,2},{4,3},{5,4},{6,5},{7,6},{8,7},{9,8},{10,9},{11,1... | collective-permute-start | bytes 49160 | tf_op jit(solution)/shard_map/ppermute | solution.py:25
  249.0 1.9 collective-permute-start.15
  250.9 6.4 %collective-permute-done.15 = f32[32,128]{1,0:T(8,128)S(1)} collective-permute-done((f32[32,128]{1,0:T(8,128)S(1)}, f32[32,128]{1,0:T(8,128)S(1)}, u32[]{:S(2)}, u32[]{:S(2)}) %collective-permute-start.15) | collective-permute-done | bytes 16416 | tf_op jit(solution)/shard_map/ppermute | solution.py:25
  257.3 2.6 reduce_sum.58
  260.7 4.5 %all-to-all-start.4 = ((f32[4,1,7232]{2,1,0:T(1,128)}), f32[4,1,7232]{2,1,0:T(1,128)S(1)}, u32[]{:S(2)}, u32[]{:S(2)}) async-start(f32[4,1,7232]{2,1,0:T(1,128)} %broadcast_in_dim.16), calls=%async_computation.4 | async-start | bytes 233472 | tf_op jit(solution)/shard_map/all_to_all | solution.py:30
  265.1 0.9 fusion.23
  266.0 5.0 %all-to-all-done.4 = f32[4,1,7232]{2,1,0:T(1,128)S(1)} async-done(((f32[4,1,7232]{2,1,0:T(1,128)}), f32[4,1,7232]{2,1,0:T(1,128)S(1)}, u32[]{:S(2)}, u32[]{:S(2)}) %all-to-all-start.4) | async-done | bytes 115744 | tf_op jit(solution)/shard_map/all_to_all | solution.py:30
  (158 shorter events, 20.2 us)
Async XLA Ops:
  0.6 27.7 %copy-start = (bf16[1,16,4,128,128]{4,3,2,1,0:T(8,128)(2,1)S(1)}, bf16[1,16,4,128,128]{4,3,2,1,0:T(8,128)(2,1)}, u32[]{:S(2)}) copy-start(bf16[1,16,4,128,128]{4,3,2,1,0:T(8,128)(2,1)} %param.28) | copy-start | bytes 6291460
  1.5 40.9 %collective-permute-start = (bf16[32,128]{1,0:T(8,128)(2,1)S(1)}, bf16[32,128]{1,0:T(8,128)(2,1)S(1)}, u32[]{:S(2)}, u32[]{:S(2)}) collective-permute-start(bf16[32,128]{1,0:T(8,128)(2,1)S(1)} %get-tuple-element.124), channel_id=1, source_target_pairs={{0,1},{1,2},{2,3},{3,4},{4,5},{5,6},{6,7},{7,8},{8,9},{9,10},{10,1... | collective-permute-start | bytes 24584 | tf_op jit(solution)/shard_map/ppermute | solution.py:14
  4.9 37.5 %collective-permute-start.1 = (bf16[32,128]{1,0:T(8,128)(2,1)S(1)}, bf16[32,128]{1,0:T(8,128)(2,1)S(1)}, u32[]{:S(2)}, u32[]{:S(2)}) collective-permute-start(bf16[32,128]{1,0:T(8,128)(2,1)S(1)} %get-tuple-element.125), channel_id=1, source_target_pairs={{1,0},{2,1},{3,2},{4,3},{5,4},{6,5},{7,6},{8,7},{9,8},{10,9},{11,1... | collective-permute-start | bytes 24584 | tf_op jit(solution)/shard_map/ppermute | solution.py:17
  15.6 2.7 copy-start.28
  18.3 59.3 %all-to-all-start.1 = ((s32[1,64,128]{2,0,1:T(1,128)}), s32[1,64,128]{2,0,1:T(1,128)}, u32[]{:S(2)}, u32[]{:S(2)}) async-start(s32[1,64,128]{2,0,1:T(1,128)} %bitcast.44), calls=%async_computation.1 | async-start | bytes 65536 | tf_op jit(solution)/shard_map/all_to_all | solution.py:147
  27.2 25.8 %copy-start.20 = (s32[64]{0:T(128)}, s32[64]{0:T(128)S(1)}, u32[]{:S(2)}) copy-start(s32[64]{0:T(128)S(1)} %eq.43) | copy-start | bytes 772
  28.4 11.4 %copy-start.22 = (s32[1,2048,1]{1,2,0:T(1,128)S(1)}, s32[1,2048,1]{1,2,0:T(1,128)}, u32[]{:S(2)}) copy-start(s32[1,2048,1]{1,2,0:T(1,128)} %param.30) | copy-start | bytes 24580
  28.4 12.4 %copy-start.1 = (bf16[1,32,2048]{2,1,0:T(8,128)(2,1)S(1)}, bf16[1,32,2048]{2,1,0:T(8,128)(2,1)}, u32[]{:S(2)}) copy-start(bf16[1,32,2048]{2,1,0:T(8,128)(2,1)} %param.27) | copy-start | bytes 393220
  30.9 25.3 %collective-permute-start.5 = (f32[32,128]{1,0:T(8,128)}, f32[32,128]{1,0:T(8,128)}, u32[]{:S(2)}, u32[]{:S(2)}) collective-permute-start(f32[32,128]{1,0:T(8,128)} %bitcast.30), channel_id=1, source_target_pairs={{0,1},{1,2},{2,3},{3,4},{4,5},{5,6},{6,7},{7,8},{8,9},{9,10},{10,1... | collective-permute-start | bytes 49160 | tf_op jit(solution)/shard_map/ppermute | solution.py:25
  34.3 21.1 %collective-permute-start.4 = (f32[32,128]{1,0:T(8,128)}, f32[32,128]{1,0:T(8,128)}, u32[]{:S(2)}, u32[]{:S(2)}) collective-permute-start(f32[32,128]{1,0:T(8,128)} %bitcast.28), channel_id=1, source_target_pairs={{1,0},{2,1},{3,2},{4,3},{5,4},{6,5},{7,6},{8,7},{9,8},{10,9},{11,1... | collective-permute-start | bytes 49160 | tf_op jit(solution)/shard_map/ppermute | solution.py:25
  42.4 10.0 %copy-start.25 = (f32[2,32]{1,0:T(2,128)S(1)}, f32[2,32]{1,0:T(2,128)}, u32[]{:S(2)}) copy-start(f32[2,32]{1,0:T(2,128)} %param.36) | copy-start | bytes 772
  43.4 9.6 %copy-start.8 = (bf16[16,4,8,128]{3,2,1,0:T(8,128)(2,1)}, bf16[16,4,8,128]{3,2,1,0:T(8,128)(2,1)S(1)}, u32[]{:S(2)}) copy-start(bf16[16,4,8,128]{3,2,1,0:T(8,128)(2,1)S(1)} %fusion.72) | copy-start | bytes 393220
  43.5 9.7 %collective-permute-start.2 = (bf16[32,128]{1,0:T(8,128)(2,1)S(1)}, bf16[32,128]{1,0:T(8,128)(2,1)S(1)}, u32[]{:S(2)}, u32[]{:S(2)}) collective-permute-start(bf16[32,128]{1,0:T(8,128)(2,1)S(1)} %get-tuple-element.122), channel_id=1, source_target_pairs={{0,1},{1,2},{2,3},{3,4},{4,5},{5,6},{6,7},{7,8},{8,9},{9,10},{10,1... | collective-permute-start | bytes 24584 | tf_op jit(solution)/shard_map/ppermute | solution.py:14
  45.4 8.3 %collective-permute-start.3 = (bf16[32,128]{1,0:T(8,128)(2,1)S(1)}, bf16[32,128]{1,0:T(8,128)(2,1)S(1)}, u32[]{:S(2)}, u32[]{:S(2)}) collective-permute-start(bf16[32,128]{1,0:T(8,128)(2,1)S(1)} %get-tuple-element.123), channel_id=1, source_target_pairs={{1,0},{2,1},{3,2},{4,3},{5,4},{6,5},{7,6},{8,7},{9,8},{10,9},{11,1... | collective-permute-start | bytes 24584 | tf_op jit(solution)/shard_map/ppermute | solution.py:17
  53.2 2.3 copy-start.19
  53.7 3.2 %copy-start.2 = (bf16[1,32,2048]{2,1,0:T(8,128)(2,1)S(1)}, bf16[1,32,2048]{2,1,0:T(8,128)(2,1)}, u32[]{:S(2)}) copy-start(bf16[1,32,2048]{2,1,0:T(8,128)(2,1)} %param.37) | copy-start | bytes 393220
  55.4 13.5 %copy-start.3 = (f32[16,32,128]{2,1,0:T(8,128)}, f32[16,32,128]{2,1,0:T(8,128)S(1)}, u32[]{:S(2)}) copy-start(f32[16,32,128]{2,1,0:T(8,128)S(1)} %fusion.63) | copy-start | bytes 786436
  55.4 3.3 %copy-start.21 = (s32[64]{0:T(128)S(1)}, s32[64]{0:T(128)}, u32[]{:S(2)}) copy-start(s32[64]{0:T(128)} %copy-done.20) | copy-start | bytes 772
  57.9 11.1 %copy-start.17 = (bf16[3,32,32]{2,1,0:T(8,128)(2,1)S(1)}, bf16[3,32,32]{2,1,0:T(8,128)(2,1)}, u32[]{:S(2)}) copy-start(bf16[3,32,32]{2,1,0:T(8,128)(2,1)} %param.33) | copy-start | bytes 18436
  58.7 12.4 %copy-start.9 = (bf16[16,4,8,128]{3,2,1,0:T(8,128)(2,1)S(1)}, bf16[16,4,8,128]{3,2,1,0:T(8,128)(2,1)}, u32[]{:S(2)}) copy-start(bf16[16,4,8,128]{3,2,1,0:T(8,128)(2,1)} %copy-done.8) | copy-start | bytes 393220
  58.7 12.4 %copy-start.11 = (f32[32,2048]{1,0:T(8,128)S(1)}, f32[32,2048]{1,0:T(8,128)}, u32[]{:S(2)}) copy-start(f32[32,2048]{1,0:T(8,128)} %fusion.168) | copy-start | bytes 786436
  58.8 12.4 %copy-start.23 = (f32[1,2048]{1,0:T(1,128)S(1)}, f32[1,2048]{1,0:T(1,128)}, u32[]{:S(2)}) copy-start(f32[1,2048]{1,0:T(1,128)} %param.32) | copy-start | bytes 24580
  58.8 12.4 %copy-start.27 = (f32[32]{0:T(128)S(1)}, f32[32]{0:T(128)}, u32[]{:S(2)}) copy-start(f32[32]{0:T(128)} %get-tuple-element.131) | copy-start | bytes 388
  59.9 10.3 %collective-permute-start.7 = (f32[32,128]{1,0:T(8,128)S(1)}, f32[32,128]{1,0:T(8,128)S(1)}, u32[]{:S(2)}, u32[]{:S(2)}) collective-permute-start(f32[32,128]{1,0:T(8,128)S(1)} %bitcast.444), channel_id=1, source_target_pairs={{0,1},{1,2},{2,3},{3,4},{4,5},{5,6},{6,7},{7,8},{8,9},{9,10},{10,1... | collective-permute-start | bytes 49160 | tf_op jit(solution)/shard_map/ppermute | solution.py:25
  61.8 8.4 %collective-permute-start.6 = (f32[32,128]{1,0:T(8,128)S(1)}, f32[32,128]{1,0:T(8,128)S(1)}, u32[]{:S(2)}, u32[]{:S(2)}) collective-permute-start(f32[32,128]{1,0:T(8,128)S(1)} %bitcast.446), channel_id=1, source_target_pairs={{1,0},{2,1},{3,2},{4,3},{5,4},{6,5},{7,6},{8,7},{9,8},{10,9},{11,1... | collective-permute-start | bytes 49160 | tf_op jit(solution)/shard_map/ppermute | solution.py:25
  69.2 3.0 %copy-start.10 = (bf16[64,2048]{1,0:T(8,128)(2,1)S(1)}, bf16[64,2048]{1,0:T(8,128)(2,1)}, u32[]{:S(2)}) copy-start(bf16[64,2048]{1,0:T(8,128)(2,1)} %get-tuple-element.128) | copy-start | bytes 786436
  69.2 3.0 %copy-start.29 = (s32[2048]{0:T(1024)S(1)}, s32[2048]{0:T(1024)}, u32[]{:S(2)}) copy-start(s32[2048]{0:T(1024)} %copy-done.28) | copy-start | bytes 24580
  113.1 3.8 %copy-start.24 = (bf16[32,32]{1,0:T(8,128)(2,1)S(1)}, bf16[32,32]{1,0:T(8,128)(2,1)}, u32[]{:S(2)}) copy-start(bf16[32,32]{1,0:T(8,128)(2,1)} %param.34) | copy-start | bytes 6148
  113.1 3.8 %copy-start.26 = (f32[32]{0:T(128)S(1)}, f32[32]{0:T(128)}, u32[]{:S(2)}) copy-start(f32[32]{0:T(128)} %get-tuple-element.130) | copy-start | bytes 388
  122.1 34.3 %copy-start.7 = (f32[64,2048]{1,0:T(8,128)S(1)}, f32[64,2048]{1,0:T(8,128)}, u32[]{:S(2)}) copy-start(f32[64,2048]{1,0:T(8,128)} %get-tuple-element.129) | copy-start | bytes 1572868
  122.1 34.3 %copy-start.30 = (s32[2048]{0:T(1024)S(1)}, s32[2048]{0:T(1024)}, u32[]{:S(2)}) copy-start(s32[2048]{0:T(1024)} %copy-done.28) | copy-start | bytes 24580
  156.5 5.8 %copy-start.6 = (f32[32,2048]{1,0:T(8,128)S(1)}, f32[32,2048]{1,0:T(8,128)}, u32[]{:S(2)}) copy-start(f32[32,2048]{1,0:T(8,128)} %copy-done.5) | copy-start | bytes 786436
  156.5 5.8 %copy-start.12 = (f32[32,2048]{1,0:T(8,128)S(1)}, f32[32,2048]{1,0:T(8,128)}, u32[]{:S(2)}) copy-start(f32[32,2048]{1,0:T(8,128)} %get-tuple-element.132) | copy-start | bytes 786436
  156.5 5.8 %copy-start.15 = (bf16[32,2048]{1,0:T(8,128)(2,1)S(1)}, bf16[32,2048]{1,0:T(8,128)(2,1)}, u32[]{:S(2)}) copy-start(bf16[32,2048]{1,0:T(8,128)(2,1)} %get-tuple-element.105) | copy-start | bytes 393220
  156.5 15.3 %copy-start.4 = (f32[16,32,128]{2,1,0:T(8,128)S(1)}, f32[16,32,128]{2,1,0:T(8,128)}, u32[]{:S(2)}) copy-start(f32[16,32,128]{2,1,0:T(8,128)} %copy-done.3) | copy-start | bytes 786436
  162.5 9.8 %collective-permute-start.8 = (bf16[32,128]{1,0:T(8,128)(2,1)S(1)}, bf16[32,128]{1,0:T(8,128)(2,1)S(1)}, u32[]{:S(2)}, u32[]{:S(2)}) collective-permute-start(bf16[32,128]{1,0:T(8,128)(2,1)S(1)} %get-tuple-element.120), channel_id=1, source_target_pairs={{0,1},{1,2},{2,3},{3,4},{4,5},{5,6},{6,7},{7,8},{8,9},{9,10},{10,1... | collective-permute-start | bytes 24584 | tf_op jit(solution)/shard_map/ppermute | solution.py:14
  165.1 7.7 %collective-permute-start.9 = (bf16[32,128]{1,0:T(8,128)(2,1)S(1)}, bf16[32,128]{1,0:T(8,128)(2,1)S(1)}, u32[]{:S(2)}, u32[]{:S(2)}) collective-permute-start(bf16[32,128]{1,0:T(8,128)(2,1)S(1)} %get-tuple-element.121), channel_id=1, source_target_pairs={{1,0},{2,1},{3,2},{4,3},{5,4},{6,5},{7,6},{8,7},{9,8},{10,9},{11,1... | collective-permute-start | bytes 24584 | tf_op jit(solution)/shard_map/ppermute | solution.py:17
  173.0 9.9 %copy-start.14 = (f32[7,32,32]{2,1,0:T(8,128)S(1)}, f32[7,32,32]{2,1,0:T(8,128)}, u32[]{:S(2)}) copy-start(f32[7,32,32]{2,1,0:T(8,128)} %copy-done.13) | copy-start | bytes 86020
  174.0 9.1 %collective-permute-start.10 = (bf16[32,128]{1,0:T(8,128)(2,1)S(1)}, bf16[32,128]{1,0:T(8,128)(2,1)S(1)}, u32[]{:S(2)}, u32[]{:S(2)}) collective-permute-start(bf16[32,128]{1,0:T(8,128)(2,1)S(1)} %get-tuple-element.118), channel_id=1, source_target_pairs={{0,1},{1,2},{2,3},{3,4},{4,5},{5,6},{6,7},{7,8},{8,9},{9,10},{10,1... | collective-permute-start | bytes 24584 | tf_op jit(solution)/shard_map/ppermute | solution.py:14
  175.9 8.3 %collective-permute-start.11 = (bf16[32,128]{1,0:T(8,128)(2,1)S(1)}, bf16[32,128]{1,0:T(8,128)(2,1)S(1)}, u32[]{:S(2)}, u32[]{:S(2)}) collective-permute-start(bf16[32,128]{1,0:T(8,128)(2,1)S(1)} %get-tuple-element.119), channel_id=1, source_target_pairs={{1,0},{2,1},{3,2},{4,3},{5,4},{6,5},{7,6},{8,7},{9,8},{10,9},{11,1... | collective-permute-start | bytes 24584 | tf_op jit(solution)/shard_map/ppermute | solution.py:17
  187.7 10.5 %copy-start.18 = (bf16[3,32,32]{2,1,0:T(8,128)(2,1)S(1)}, bf16[3,32,32]{2,1,0:T(8,128)(2,1)}, u32[]{:S(2)}) copy-start(bf16[3,32,32]{2,1,0:T(8,128)(2,1)} %param.33) | copy-start | bytes 18436
  187.7 69.6 %all-to-all-start.3 = ((f32[64,1,7232]{2,1,0:T(1,128)}), f32[64,1,7232]{2,1,0:T(1,128)}, u32[]{:S(2)}, u32[]{:S(2)}) async-start(f32[64,1,7232]{2,1,0:T(1,128)} %broadcast_in_dim.15), calls=%async_computation.3 | async-start | bytes 3735552 | tf_op jit(solution)/shard_map/all_to_all | solution.py:30
  199.3 10.1 %copy-start.16 = (bf16[3,32,32]{2,1,0:T(8,128)(2,1)S(1)}, bf16[3,32,32]{2,1,0:T(8,128)(2,1)}, u32[]{:S(2)}) copy-start(bf16[3,32,32]{2,1,0:T(8,128)(2,1)} %param.35) | copy-start | bytes 18436
  200.5 40.7 %collective-permute-start.13 = (f32[32,128]{1,0:T(8,128)S(1)}, f32[32,128]{1,0:T(8,128)S(1)}, u32[]{:S(2)}, u32[]{:S(2)}) collective-permute-start(f32[32,128]{1,0:T(8,128)S(1)} %get-tuple-element.115), channel_id=1, source_target_pairs={{0,1},{1,2},{2,3},{3,4},{4,5},{5,6},{6,7},{7,8},{8,9},{9,10},{10,1... | collective-permute-start | bytes 49160 | tf_op jit(solution)/shard_map/ppermute | solution.py:25
  203.9 34.5 %collective-permute-start.12 = (f32[32,128]{1,0:T(8,128)S(1)}, f32[32,128]{1,0:T(8,128)S(1)}, u32[]{:S(2)}, u32[]{:S(2)}) collective-permute-start(f32[32,128]{1,0:T(8,128)S(1)} %get-tuple-element.116), channel_id=1, source_target_pairs={{1,0},{2,1},{3,2},{4,3},{5,4},{6,5},{7,6},{8,7},{9,8},{10,9},{11,1... | collective-permute-start | bytes 49160 | tf_op jit(solution)/shard_map/ppermute | solution.py:25
  243.4 7.5 %collective-permute-start.14 = (f32[32,128]{1,0:T(8,128)S(1)}, f32[32,128]{1,0:T(8,128)S(1)}, u32[]{:S(2)}, u32[]{:S(2)}) collective-permute-start(f32[32,128]{1,0:T(8,128)S(1)} %bitcast.445), channel_id=1, source_target_pairs={{1,0},{2,1},{3,2},{4,3},{5,4},{6,5},{7,6},{8,7},{9,8},{10,9},{11,1... | collective-permute-start | bytes 49160 | tf_op jit(solution)/shard_map/ppermute | solution.py:25
  249.0 8.4 %collective-permute-start.15 = (f32[32,128]{1,0:T(8,128)S(1)}, f32[32,128]{1,0:T(8,128)S(1)}, u32[]{:S(2)}, u32[]{:S(2)}) collective-permute-start(f32[32,128]{1,0:T(8,128)S(1)} %bitcast.443), channel_id=1, source_target_pairs={{0,1},{1,2},{2,3},{3,4},{4,5},{5,6},{6,7},{7,8},{8,9},{9,10},{10,1... | collective-permute-start | bytes 49160 | tf_op jit(solution)/shard_map/ppermute | solution.py:25
  260.7 10.4 %all-to-all-start.4 = ((f32[4,1,7232]{2,1,0:T(1,128)}), f32[4,1,7232]{2,1,0:T(1,128)S(1)}, u32[]{:S(2)}, u32[]{:S(2)}) async-start(f32[4,1,7232]{2,1,0:T(1,128)} %broadcast_in_dim.16), calls=%async_computation.4 | async-start | bytes 233472 | tf_op jit(solution)/shard_map/all_to_all | solution.py:30
  (2 other events, 1.7 us)
where the time goes:
time: 274 us; the launch traced here: 273 us
  starting transfers between devices  91.9 us (34%)
  blocking collectives  69.5 us (25%)
  waiting for transfers between devices  45.9 us (17%)
  matrix products  42.3 us (15%)
  other arithmetic  11.5 us (4%)
  local copies, waits for them, and re-layouts  9.7 us (4%)
    ppermute x8, waiting for transfers between devices, passed_along(): return lax.ppermute(value, axis, pairs)  38.7 us
    all_to_all x1, blocking collectives, joint_to_owners(): lax.all_to_all(buffer.reshape(chans, peers, slots), ('region', 'sub'), sp...  35.5 us
    all_to_all x1, blocking collectives, joint_from_owners(): lax.all_to_all(buffer.reshape(chans, peers, slots), ('region', 'sub'), sp...  34 us
    ppermute x8, starting transfers between devices, passed_along(): return lax.ppermute(value, axis, pairs)  33.4 us
    ppermute x4, starting transfers between devices, with_halo(): lax.ppermute(lax.slice_in_dim(block, 0, width, axis=dim), axis, backward)  25.8 us
    all_to_all x2, starting transfers between devices, sent_to_all(): lax.all_to_all(jnp.broadcast_to(value[None], (peers, *value.shape)), axis...  15 us
    ppermute x4, starting transfers between devices, with_halo(): lax.ppermute(lax.slice_in_dim(block, block.shape[dim] - width, None, axis...  9.75 us
    dot_general x14, matrix products, mixdot(): return jnp.dot(weight, field, preferred_element_type=jnp.float32)  8.63 us
  transfers between devices with their start and end apart: 19, of which 8 were waited for; matrix products, arithmetic and copies ran while one was open for 14% of the time, Pallas kernels for 0%

commit v1 on v0

v1 whole, which is shorter than its diff:
```python
import math

import jax
import jax.numpy as jnp
from jax import lax
from jax.sharding import PartitionSpec as P

LINE = ("region", "sub")
BF = jnp.bfloat16
F32 = jnp.float32


def shifted(value, by):
    peers = lax.axis_size(LINE)
    pairs = [(i, i + by) for i in range(peers) if 0 <= i + by < peers]
    return lax.ppermute(value, LINE, pairs)


def placed_hot(columns, count):
    return columns.reshape(-1)[:, None] == jnp.arange(count + 2, dtype=jnp.int32)[None, :]


def forward_product(blocks, hot, tiles):
    chans = blocks.shape[0]
    count, nonzero, width = tiles.shape[:3]
    picked = jnp.einsum("cmt,jm->cjt", blocks, hot, preferred_element_type=F32).astype(BF)
    picked = picked.reshape(chans, count, nonzero, width)
    return jnp.einsum("cknt,kntu->cku", picked, tiles, preferred_element_type=F32)


def transpose_product(blocks, hot, tiles):
    chans = blocks.shape[0]
    count, nonzero, width = tiles.shape[:3]
    contrib = jnp.einsum("cku,kntu->cknt", blocks, tiles, preferred_element_type=F32)
    contrib = contrib.reshape(chans, count * nonzero, width)
    return jnp.einsum("cjt,jm->cmt", contrib, hot.astype(F32), precision=lax.Precision.HIGHEST)


def halo_round(field, extended):
    chans = field.shape[0]
    ext = extended.astype(BF)
    up = shifted(jnp.concatenate([field[:, -1], ext[:, -1]], axis=0), 1)
    down = shifted(jnp.concatenate([field[:, 0], ext[:, 0]], axis=0), -1)
    blocks = jnp.concatenate([up[:chans, None], field, down[:chans, None]], axis=1)
    inner = extended[:, 1:-1]
    inner = inner.at[:, 0].add(up[chans:].astype(F32)).at[:, -1].add(down[chans:].astype(F32))
    return blocks, inner


def both_terms(field, grad, tiles, columns):
    chans, rows = field.shape
    count, nonzero, width = tiles.shape[:3]
    hot = placed_hot(columns, count)
    hot_b = hot.astype(BF)
    f0 = field.reshape(chans, count, width)
    g0 = grad.reshape(chans, count, width)
    blocks, inner = halo_round(f0, transpose_product(g0, hot, tiles))
    f1 = forward_product(blocks, hot_b, tiles).astype(BF)
    g1 = inner.astype(BF)
    blocks, inner = halo_round(f1, transpose_product(g1, hot, tiles))
    f2 = (2.0 * forward_product(blocks, hot_b, tiles) - f0.astype(F32)).astype(BF)
    g2 = (2.0 * inner - g0.astype(F32)).astype(BF)
    stack = lambda *a: jnp.concatenate(a, axis=0).reshape(3 * chans, rows)
    return stack(f0, f1, f2), stack(g0, g1, g2)


def mixdot(weight, field):
    return jnp.dot(weight, field, preferred_element_type=F32)


def silu_slope(value):
    sig = jax.nn.sigmoid(value)
    return sig * (1.0 + value * (1.0 - sig))


def outer_sum(left, right):
    return jnp.einsum("cn,dn->cd", left, right, preferred_element_type=F32)


def spread(values, axes):
    peers = lax.axis_size(axes)
    return lax.all_to_all(
        jnp.broadcast_to(values[None], (peers, *values.shape)), axes, 0, 0, tiled=True
    )


def summed_everywhere(flat):
    regions = lax.axis_size("region")
    size = flat.shape[0]
    lanes = 128
    chunk = -(-size // (regions * lanes))
    padded = jnp.pad(flat, (0, regions * chunk * lanes - size)).reshape(regions, chunk, lanes)
    mine = jnp.sum(lax.all_to_all(padded, "region", 0, 0, tiled=True), axis=0)
    mine = jnp.sum(spread(mine, ("geo", "sub")), axis=0)
    return spread(mine, "region").reshape(-1)[:size]


def pack_slots(message, own_hot, rank_hot):
    chans = message.shape[0]
    masked = message[:, None, :] * own_hot[None, :, :]
    packed = jnp.einsum("coi,ir->cor", masked, rank_hot, preferred_element_type=F32)
    return packed.astype(BF)


def exchanged(buffer):
    return lax.all_to_all(buffer, LINE, split_axis=1, concat_axis=1, tiled=True)


def on_device(
    features,
    lap_tiles,
    tile_cols,
    coarse_owner,
    coarse_slot,
    pool_weight,
    weight_in,
    weight_mid,
    weight_out,
    biases,
    out_grad,
):
    field = features[0]
    tiles = lap_tiles[0]
    columns = tile_cols[0]
    owners = coarse_owner[0, :, 0]
    parents = coarse_slot[0]
    weight_row = pool_weight[0][None, :]
    upstream = out_grad[0]
    chans, rows = field.shape
    peers = lax.axis_size(LINE)
    slots = 4 * rows // peers
    coarse_rows = rows // 4
    own_hot = (owners[None, :] == jnp.arange(peers, dtype=jnp.int32)[:, None]).astype(BF)
    positions = jnp.arange(rows, dtype=jnp.int32)
    same_owner = (owners[:, None] == owners[None, :]) & (positions[None, :] < positions[:, None])
    rank = jnp.sum(same_owner.astype(jnp.int32), axis=1)
    rank_hot = (rank[:, None] == jnp.arange(slots, dtype=jnp.int32)[None, :]).astype(BF)
    base = 32
    ids = parents + 1
    id_rows = jnp.stack([ids // base, ids % base], axis=0).astype(BF)
    mix_in = jnp.concatenate([weight_in[k] for k in range(3)], axis=1)
    mix_out = jnp.concatenate([weight_out[k] for k in range(3)], axis=1)
    mix_in_t = jnp.concatenate([weight_in[k].T for k in range(3)], axis=1)
    mix_out_t = jnp.concatenate([weight_out[k].T for k in range(3)], axis=1)
    terms_in, terms_grad = both_terms(field, upstream, tiles, columns)
    pre_in = mixdot(mix_in, terms_in) + biases[0][:, None]
    hidden = jax.nn.silu(pre_in).astype(BF)
    message = (weight_row * hidden.astype(F32)).astype(BF)
    merged_grad = mixdot(mix_out_t, terms_grad).astype(BF)
    grad_message = (weight_row * merged_grad.astype(F32)).astype(BF)
    sent = jnp.concatenate([message, grad_message, id_rows], axis=0)
    got = exchanged(pack_slots(sent, own_hot, rank_hot))
    flat = got.reshape(2 * chans + 2, peers * slots)
    got_ids = (
        flat[2 * chans].astype(jnp.int32) * base + flat[2 * chans + 1].astype(jnp.int32) - 1
    )
    coarse_hot = (
        got_ids[:, None] == jnp.arange(coarse_rows, dtype=jnp.int32)[None, :]
    ).astype(BF)
    totals = mixdot(flat[: 2 * chans], coarse_hot)
    coarse = totals[:chans].astype(BF)
    coarse_grad = totals[chans:]
    pre_mid = mixdot(weight_mid, coarse) + biases[1][:, None]
    coarse_out = jax.nn.silu(pre_mid).astype(BF)
    mid_grad = (coarse_grad * silu_slope(pre_mid)).astype(BF)
    coarse_back = mixdot(weight_mid.T, mid_grad).astype(BF)
    values = jnp.concatenate([coarse_out, coarse_back], axis=0)
    buffer = jnp.einsum("cj,sj->cs", values, coarse_hot, preferred_element_type=F32).astype(BF)
    back = exchanged(buffer.reshape(2 * chans, peers, slots))
    lifted_all = jnp.einsum("cor,ir->coi", back, rank_hot, preferred_element_type=F32)
    lifted_all = jnp.sum(lifted_all * own_hot.astype(F32)[None, :, :], axis=1)
    lifted = lifted_all[:chans]
    lifted_grad = lifted_all[chans:]
    merged = (hidden.astype(F32) + weight_row * lifted).astype(BF)
    hidden_grad = merged_grad.astype(F32) + weight_row * lifted_grad
    pre_grad = (hidden_grad * silu_slope(pre_in)).astype(BF)
    grads_in = outer_sum(terms_in, pre_grad).reshape(3, chans, chans).transpose(0, 2, 1)
    grads_mid = outer_sum(mid_grad, coarse)
    grads_out = outer_sum(terms_grad, merged).reshape(3, chans, chans)
    local = jnp.concatenate(
        [
            grads_in.ravel(),
            grads_mid.ravel(),
            grads_out.ravel(),
            jnp.sum(pre_grad.astype(F32), axis=1),
            jnp.sum(mid_grad.astype(F32), axis=1),
        ]
    )
    factor = 1.0 / math.sqrt(lax.axis_size("geo") * rows * peers)
    total = summed_everywhere(local) * factor
    sum_weights = total[: 7 * chans * chans].reshape(7, chans, chans)
    sum_biases = total[7 * chans * chans :].reshape(2, chans)
    terms_out, terms_back = both_terms(merged, pre_grad, tiles, columns)
    result = mixdot(mix_out, terms_out).astype(BF)
    input_grad = mixdot(mix_in_t, terms_back).astype(BF)
    return (result[None], input_grad[None], sum_weights, sum_biases)


def solution(mesh):
    line = ("region", "sub")
    in_specs = (
        P("geo", None, line),
        P("geo", line, None, None, None),
        P("geo", line, None),
        P("geo", line, None),
        P("geo", line),
        P("geo", line),
        P(),
        P(),
        P(),
        P(),
        P("geo", None, line),
    )
    out_specs = (P("geo", None, line), P("geo", None, line), P(), P())
    return jax.shard_map(
        on_device, mesh=mesh, in_specs=in_specs, out_specs=out_specs, check_vma=False
    )
```

time: 274 us -> 201 us (0.73)
  the two profiles are of different devices: /device:TPU:128 before, /device:TPU:1 now
where the time goes in v1:
time: 201 us; the launch traced here: 200 us
  starting transfers between devices  57.6 us (29%)
  blocking collectives  42.2 us (21%)
  waiting for transfers between devices  40.6 us (20%)
  matrix products  34.3 us (17%)
  local copies, waits for them, and re-layouts  14.1 us (7%)
  other arithmetic  9.6 us (5%)
    all_to_all x1, blocking collectives, exchanged(): return lax.all_to_all(buffer, LINE, split_axis=1, concat_axis=1, tiled=True)  42.2 us
    ppermute x8, starting transfers between devices, shifted(): return lax.ppermute(value, LINE, pairs)  28.2 us
    all_to_all x1, waiting for transfers between devices, exchanged(): return lax.all_to_all(buffer, LINE, split_axis=1, concat_axis=1, tiled=True)  24.6 us
    all_to_all x2, starting transfers between devices, spread(): lax.all_to_all(jnp.broadcast_to(values[None], (peers, *values.shape)), ax...  16.6 us
    all_to_all x2, waiting for transfers between devices, spread(): lax.all_to_all(jnp.broadcast_to(values[None], (peers, *values.shape)), ax...  11 us
    all_to_all x1, starting transfers between devices, exchanged(): return lax.all_to_all(buffer, LINE, split_axis=1, concat_axis=1, tiled=True)  6.7 us
    dot_general x1, matrix products, on_device(): jnp.einsum('cor,ir->coi', back, rank_hot, preferred_element_type=F32)  6.55 us
    dot_general x7, matrix products, mixdot(): return jnp.dot(weight, field, preferred_element_type=F32)  6.48 us
  transfers between devices with their start and end apart: 12, of which 5 were waited for; matrix products, arithmetic and copies ran while one was open for 11% of the time, Pallas kernels for 0%

profile of v1, /device:TPU:1, one launch (start us, length us, event | category | flops | bytes accessed | tf_op | source)
XLA Modules:
  0.0 200.4 jit_solution(13830467166888845068)
XLA Ops:
  0.6 1.1 copy.425
  1.7 0.8 copy.342
  2.6 0.8 fusion.27
  3.5 1.1 convolution_bitcast_fusion.1
  4.7 3.9 %collective-permute-start = (bf16[64,128]{1,0:T(8,128)(2,1)S(1)}, bf16[64,128]{1,0:T(8,128)(2,1)S(1)}, u32[]{:S(2)}, u32[]{:S(2)}) collective-permute-start(bf16[64,128]{1,0:T(8,128)(2,1)S(1)} %pad_maximum_fusion.7), channel_id=1, source_target_pairs={{0,1},{1,2},{2,3},{3,4},{4,5},{5,6},{6,7},{7,8},{8,9},{9,10},{10,1... | collective-permute-start | bytes 49160 | tf_op jit(solution)/shard_map/ppermute | solution.py:16
  8.7 3.7 %collective-permute-start.1 = (bf16[64,128]{1,0:T(8,128)(2,1)S(1)}, bf16[64,128]{1,0:T(8,128)(2,1)S(1)}, u32[]{:S(2)}, u32[]{:S(2)}) collective-permute-start(bf16[64,128]{1,0:T(8,128)(2,1)S(1)} %pad_maximum_fusion.8), channel_id=1, source_target_pairs={{1,0},{2,1},{3,2},{4,3},{5,4},{6,5},{7,6},{8,7},{9,8},{10,9},{11,1... | collective-permute-start | bytes 49160 | tf_op jit(solution)/shard_map/ppermute | solution.py:16
  12.4 0.9 fusion.101
  13.3 5.1 %convert_reduce_fusion = s32[2048]{0:T(1024)} fusion(s32[2048]{0:T(1024)S(1)} %bitcast.426), kind=kLoop, calls=%fused_computation.6 | loop fusion | flops 20969472 | bytes 16384 | tf_op jit(solution)/shard_map/reduce_sum | solution.py:136
  20.8 0.7 copy.362
  21.5 0.7 copy.361
  22.2 0.7 copy.360
  23.5 0.8 fusion.23
  24.4 1.1 fusion.89
  26.5 3.9 %collective-permute-start.3 = (bf16[64,128]{1,0:T(8,128)(2,1)S(1)}, bf16[64,128]{1,0:T(8,128)(2,1)S(1)}, u32[]{:S(2)}, u32[]{:S(2)}) collective-permute-start(bf16[64,128]{1,0:T(8,128)(2,1)S(1)} %pad_maximum_fusion.10), channel_id=1, source_target_pairs={{1,0},{2,1},{3,2},{4,3},{5,4},{6,5},{7,6},{8,7},{9,8},{10,9},{11,1... | collective-permute-start | bytes 49160 | tf_op jit(solution)/shard_map/ppermute | solution.py:16
  30.5 2.1 %collective-permute-start.2 = (bf16[64,128]{1,0:T(8,128)(2,1)S(1)}, bf16[64,128]{1,0:T(8,128)(2,1)S(1)}, u32[]{:S(2)}, u32[]{:S(2)}) collective-permute-start(bf16[64,128]{1,0:T(8,128)(2,1)S(1)} %pad_maximum_fusion.9), channel_id=1, source_target_pairs={{0,1},{1,2},{2,3},{3,4},{4,5},{5,6},{6,7},{7,8},{8,9},{9,10},{10,1... | collective-permute-start | bytes 49160 | tf_op jit(solution)/shard_map/ppermute | solution.py:16
  32.6 4.1 %collective-permute-done.2 = bf16[64,128]{1,0:T(8,128)(2,1)S(1)} collective-permute-done((bf16[64,128]{1,0:T(8,128)(2,1)S(1)}, bf16[64,128]{1,0:T(8,128)(2,1)S(1)}, u32[]{:S(2)}, u32[]{:S(2)}) %collective-permute-start.2) | collective-permute-done | bytes 16416 | tf_op jit(solution)/shard_map/ppermute | solution.py:16
  38.3 1.0 fusion.112
  39.4 4.8 %fusion.29 = bf16[66,64,128]{2,1,0:T(8,128)(2,1)S(1)} fusion(bf16[64,2048]{1,0:T(8,128)(2,1)S(1)} %get-tuple-element.150, bf16[66,2048]{1,0:T(8,128)(2,1)S(1)} %pad_maximum_fusion.2, s32[2048]{0:T(1024)S(1)} %copy-done.47), kind=kOutput, calls=%fused_computation.37 | convolution fusion | flops 2224046080 | bytes 1622016 | tf_op jit(solution)/shard_map/coi,ir->cor/dot_general | solution.py:101
  44.2 0.7 copy.366
  44.9 42.2 %all_to_all.25 = bf16[66,64,128]{2,0,1:T(8,128)(2,1)S(1)} all-to-all(bf16[66,64,128]{2,0,1:T(8,128)(2,1)S(1)} %copy.366), channel_id=1, replica_groups=mesh['geo'=4,'region'=16,'sub'=4] {'region','sub'}, dimensions={1} | all-to-all | bytes 2162688 | tf_op jit(solution)/shard_map/all_to_all | solution.py:106
  87.2 3.0 %fusion.3 = f32[64,512]{1,0:T(8,128)S(1)} fusion(s32[8192]{0:T(1024)S(1)} %bitcast.423, bf16[66,64,128]{2,0,1:T(8,128)(2,1)S(1)} %all_to_all.25), kind=kOutput, calls=%fused_computation.5 | convolution fusion | flops 541065216 | bytes 1212416 | tf_op jit(solution)/shard_map/dot_general | solution.py:68
  90.6 4.1 %fusion.32 = bf16[8,64,8,128]{3,2,1,0:T(8,128)(2,1)S(1)} fusion(s32[8192]{0:T(1024)S(1)} %bitcast.424, bf16[32,512]{1,0:T(8,128)(2,1)S(1)} %fusion.82, bf16[32,512]{1,0:T(8,128)(2,1)S(1)} %get-tuple-element.131), kind=kOutput, calls=%fused_computation.38 | convolution fusion | flops 541720576 | bytes 1146880 | tf_op jit(solution)/shard_map/cj,sj->cs/dot_general | solution.py:168
  94.8 1.3 copy.481
  96.1 6.7 %all-to-all-start.1 = ((bf16[64,64,128]{2,0,1:T(8,128)(2,1)}), bf16[64,64,128]{2,0,1:T(8,128)(2,1)}, u32[]{:S(2)}, u32[]{:S(2)}) async-start(bf16[64,64,128]{2,0,1:T(8,128)(2,1)} %bitcast.383), calls=%async_computation.1 | async-start | bytes 2097152 | tf_op jit(solution)/shard_map/all_to_all | solution.py:106
  103.5 0.7 copy.388
  104.1 0.7 copy.387
  104.8 1.0 fusion.153
  105.9 24.6 %all-to-all-done.1 = bf16[64,64,128]{2,0,1:T(8,128)(2,1)} async-done(((bf16[64,64,128]{2,0,1:T(8,128)(2,1)}), bf16[64,64,128]{2,0,1:T(8,128)(2,1)}, u32[]{:S(2)}, u32[]{:S(2)}) %all-to-all-start.1) | async-done | bytes 1048608 | tf_op jit(solution)/shard_map/all_to_all | solution.py:106
  130.5 6.5 %multiply_reduce_fusion = f32[64,2048]{1,0:T(8,128)S(1)} fusion(f32[64,2048]{1,0:T(8,128)S(1)} %copy-done.1, bf16[64,64,128]{2,0,1:T(8,128)(2,1)} %all-to-all-done.1, s32[2048]{0:T(1024)S(1)} %copy-done.48), kind=kOutput, calls=%fused_computation | convolution fusion | flops 2164391936 | bytes 2105344 | tf_op jit(solution)/shard_map/cor,ir->coi/dot_general | solution.py:170
  137.4 0.8 fusion.19
  138.2 1.1 convolution_bitcast_fusion
  139.4 2.7 %collective-permute-start.4 = (bf16[64,128]{1,0:T(8,128)(2,1)S(1)}, bf16[64,128]{1,0:T(8,128)(2,1)S(1)}, u32[]{:S(2)}, u32[]{:S(2)}) collective-permute-start(bf16[64,128]{1,0:T(8,128)(2,1)S(1)} %pad_maximum_fusion.11), channel_id=1, source_target_pairs={{0,1},{1,2},{2,3},{3,4},{4,5},{5,6},{6,7},{7,8},{8,9},{9,10},{10,1... | collective-permute-start | bytes 49160 | tf_op jit(solution)/shard_map/ppermute | solution.py:16
  142.1 5.1 %collective-permute-start.5 = (bf16[64,128]{1,0:T(8,128)(2,1)S(1)}, bf16[64,128]{1,0:T(8,128)(2,1)S(1)}, u32[]{:S(2)}, u32[]{:S(2)}) collective-permute-start(bf16[64,128]{1,0:T(8,128)(2,1)S(1)} %pad_maximum_fusion.12), channel_id=1, source_target_pairs={{1,0},{2,1},{3,2},{4,3},{5,4},{6,5},{7,6},{8,7},{9,8},{10,9},{11,1... | collective-permute-start | bytes 49160 | tf_op jit(solution)/shard_map/ppermute | solution.py:16
  148.8 6.1 %all-to-all-start.2 = ((f32[16,4,128]{2,1,0:T(4,128)}), f32[16,4,128]{2,1,0:T(4,128)}, u32[]{:S(2)}, u32[]{:S(2)}) async-start(f32[16,4,128]{2,1,0:T(4,128)} %bitcast.101), calls=%async_computation.2 | async-start | bytes 65536 | tf_op jit(solution)/shard_map/all_to_all | solution.py:93
  155.0 0.8 fusion.15
  155.8 1.1 fusion.85
  158.0 1.9 collective-permute-start.6
  159.9 4.9 %collective-permute-start.7 = (bf16[64,128]{1,0:T(8,128)(2,1)S(1)}, bf16[64,128]{1,0:T(8,128)(2,1)S(1)}, u32[]{:S(2)}, u32[]{:S(2)}) collective-permute-start(bf16[64,128]{1,0:T(8,128)(2,1)S(1)} %pad_maximum_fusion.14), channel_id=1, source_target_pairs={{1,0},{2,1},{3,2},{4,3},{5,4},{6,5},{7,6},{8,7},{9,8},{10,9},{11,1... | collective-permute-start | bytes 49160 | tf_op jit(solution)/shard_map/ppermute | solution.py:16
  164.8 0.8 collective-permute-done.7
  165.6 0.7 copy_bitcast_fusion.3
  166.4 0.8 reduce_sum.58
  167.8 9.5 %all-to-all-start.3 = ((f32[16,4,128]{2,1,0:T(4,128)}), f32[16,4,128]{2,1,0:T(4,128)S(1)}, u32[]{:S(2)}, u32[]{:S(2)}) async-start(f32[16,4,128]{2,1,0:T(4,128)} %broadcast_in_dim.64), calls=%async_computation.3 | async-start | bytes 65536 | tf_op jit(solution)/shard_map/all_to_all | solution.py:82
  177.7 6.1 %all-to-all-done.3 = f32[16,4,128]{2,1,0:T(4,128)S(1)} async-done(((f32[16,4,128]{2,1,0:T(4,128)}), f32[16,4,128]{2,1,0:T(4,128)S(1)}, u32[]{:S(2)}, u32[]{:S(2)}) %all-to-all-start.3) | async-done | bytes 32800 | tf_op jit(solution)/shard_map/all_to_all | solution.py:82
  184.4 7.1 %all-to-all-start.4 = ((f32[16,4,128]{2,1,0:T(4,128)}), f32[16,4,128]{2,1,0:T(4,128)S(1)}, u32[]{:S(2)}, u32[]{:S(2)}) async-start(f32[16,4,128]{2,1,0:T(4,128)} %broadcast_in_dim.65), calls=%async_computation.4 | async-start | bytes 65536 | tf_op jit(solution)/shard_map/all_to_all | solution.py:82
  192.1 0.9 fusion.11
  193.1 0.9 fusion.12
  194.0 4.9 %all-to-all-done.4 = f32[16,4,128]{2,1,0:T(4,128)S(1)} async-done(((f32[16,4,128]{2,1,0:T(4,128)}), f32[16,4,128]{2,1,0:T(4,128)S(1)}, u32[]{:S(2)}, u32[]{:S(2)}) %all-to-all-start.4) | async-done | bytes 32800 | tf_op jit(solution)/shard_map/all_to_all | solution.py:82
  198.9 0.7 reshape.430
  (201 shorter events, 13.1 us)
Async XLA Ops:
  0.6 2.0 copy-start
  2.6 154.4 %copy-start.17 = (s32[64]{0:T(128)}, s32[64]{0:T(128)S(1)}, u32[]{:S(2)}) copy-start(s32[64]{0:T(128)S(1)} %eq.43) | copy-start | bytes 772
  2.6 2.0 %copy-start.2 = (bf16[1,32,2048]{2,1,0:T(8,128)(2,1)S(1)}, bf16[1,32,2048]{2,1,0:T(8,128)(2,1)}, u32[]{:S(2)}) copy-start(bf16[1,32,2048]{2,1,0:T(8,128)(2,1)} %param.27) | copy-start | bytes 393220
  3.4 9.0 %copy-start.28 = (s32[1,2048,1]{1,2,0:T(1,128)S(1)}, s32[1,2048,1]{1,2,0:T(1,128)}, u32[]{:S(2)}) copy-start(s32[1,2048,1]{1,2,0:T(1,128)} %param.30) | copy-start | bytes 24580
  3.4 14.9 %copy-start.24 = (bf16[3,32,32]{2,1,0:T(8,128)(2,1)S(1)}, bf16[3,32,32]{2,1,0:T(8,128)(2,1)}, u32[]{:S(2)}) copy-start(bf16[3,32,32]{2,1,0:T(8,128)(2,1)} %param.35) | copy-start | bytes 18436
  3.4 15.5 %copy-start.25 = (bf16[3,32,32]{2,1,0:T(8,128)(2,1)S(1)}, bf16[3,32,32]{2,1,0:T(8,128)(2,1)}, u32[]{:S(2)}) copy-start(bf16[3,32,32]{2,1,0:T(8,128)(2,1)} %param.33) | copy-start | bytes 18436
  3.4 16.2 %copy-start.31 = (s32[1,2048]{1,0:T(1,128)S(1)}, s32[1,2048]{1,0:T(1,128)}, u32[]{:S(2)}) copy-start(s32[1,2048]{1,0:T(1,128)} %param.31) | copy-start | bytes 24580
  3.5 16.8 %copy-start.45 = (f32[2,32]{1,0:T(2,128)S(1)}, f32[2,32]{1,0:T(2,128)}, u32[]{:S(2)}) copy-start(f32[2,32]{1,0:T(2,128)} %param.36) | copy-start | bytes 772
  4.7 18.1 %collective-permute-start = (bf16[64,128]{1,0:T(8,128)(2,1)S(1)}, bf16[64,128]{1,0:T(8,128)(2,1)S(1)}, u32[]{:S(2)}, u32[]{:S(2)}) collective-permute-start(bf16[64,128]{1,0:T(8,128)(2,1)S(1)} %pad_maximum_fusion.7), channel_id=1, source_target_pairs={{0,1},{1,2},{2,3},{3,4},{4,5},{5,6},{6,7},{7,8},{8,9},{9,10},{10,1... | collective-permute-start | bytes 49160 | tf_op jit(solution)/shard_map/ppermute | solution.py:16
  8.7 14.2 %collective-permute-start.1 = (bf16[64,128]{1,0:T(8,128)(2,1)S(1)}, bf16[64,128]{1,0:T(8,128)(2,1)S(1)}, u32[]{:S(2)}, u32[]{:S(2)}) collective-permute-start(bf16[64,128]{1,0:T(8,128)(2,1)S(1)} %pad_maximum_fusion.8), channel_id=1, source_target_pairs={{1,0},{2,1},{3,2},{4,3},{5,4},{6,5},{7,6},{8,7},{9,8},{10,9},{11,1... | collective-permute-start | bytes 49160 | tf_op jit(solution)/shard_map/ppermute | solution.py:16
  24.4 13.6 %copy-start.10 = (bf16[32,2048]{1,0:T(8,128)(2,1)}, bf16[32,2048]{1,0:T(8,128)(2,1)S(1)}, u32[]{:S(2)}) copy-start(bf16[32,2048]{1,0:T(8,128)(2,1)S(1)} %copy_bitcast_fusion.8) | copy-start | bytes 393220
  26.5 11.8 %copy-start.3 = (bf16[32,2048]{1,0:T(8,128)(2,1)}, bf16[32,2048]{1,0:T(8,128)(2,1)S(1)}, u32[]{:S(2)}) copy-start(bf16[32,2048]{1,0:T(8,128)(2,1)S(1)} %copy_bitcast_fusion.10) | copy-start | bytes 393220
  26.5 6.1 %collective-permute-start.3 = (bf16[64,128]{1,0:T(8,128)(2,1)S(1)}, bf16[64,128]{1,0:T(8,128)(2,1)S(1)}, u32[]{:S(2)}, u32[]{:S(2)}) collective-permute-start(bf16[64,128]{1,0:T(8,128)(2,1)S(1)} %pad_maximum_fusion.10), channel_id=1, source_target_pairs={{1,0},{2,1},{3,2},{4,3},{5,4},{6,5},{7,6},{8,7},{9,8},{10,9},{11,1... | collective-permute-start | bytes 49160 | tf_op jit(solution)/shard_map/ppermute | solution.py:16
  30.5 6.3 %collective-permute-start.2 = (bf16[64,128]{1,0:T(8,128)(2,1)S(1)}, bf16[64,128]{1,0:T(8,128)(2,1)S(1)}, u32[]{:S(2)}, u32[]{:S(2)}) collective-permute-start(bf16[64,128]{1,0:T(8,128)(2,1)S(1)} %pad_maximum_fusion.9), channel_id=1, source_target_pairs={{0,1},{1,2},{2,3},{3,4},{4,5},{5,6},{6,7},{7,8},{8,9},{9,10},{10,1... | collective-permute-start | bytes 49160 | tf_op jit(solution)/shard_map/ppermute | solution.py:16
  37.8 1.5 copy-start.19
  37.9 1.5 copy-start.5
  38.0 6.2 %copy-start.14 = (bf16[32,2048]{1,0:T(8,128)(2,1)}, bf16[32,2048]{1,0:T(8,128)(2,1)S(1)}, u32[]{:S(2)}) copy-start(bf16[32,2048]{1,0:T(8,128)(2,1)S(1)} %copy_bitcast_fusion.7) | copy-start | bytes 393220
  87.1 3.0 %copy-start.32 = (bf16[32,32]{1,0:T(8,128)(2,1)S(1)}, bf16[32,32]{1,0:T(8,128)(2,1)}, u32[]{:S(2)}) copy-start(bf16[32,32]{1,0:T(8,128)(2,1)} %param.34) | copy-start | bytes 6148
  90.1 14.0 %copy-start.20 = (f32[64,512]{1,0:T(8,128)}, f32[64,512]{1,0:T(8,128)S(1)}, u32[]{:S(2)}) copy-start(f32[64,512]{1,0:T(8,128)S(1)} %fusion.3) | copy-start | bytes 393220
  94.7 8.1 %copy-start.23 = (bf16[32,32]{0,1:T(8,128)(2,1)S(1)}, bf16[32,32]{0,1:T(8,128)(2,1)}, u32[]{:S(2)}) copy-start(bf16[32,32]{0,1:T(8,128)(2,1)} %get-tuple-element.134) | copy-start | bytes 6148
  94.7 8.8 %copy-start.22 = (bf16[32,32]{0,1:T(8,128)(2,1)S(1)}, bf16[32,32]{0,1:T(8,128)(2,1)}, u32[]{:S(2)}) copy-start(bf16[32,32]{0,1:T(8,128)(2,1)} %get-tuple-element.133) | copy-start | bytes 6148
  94.7 9.4 %copy-start.21 = (bf16[32,32]{0,1:T(8,128)(2,1)S(1)}, bf16[32,32]{0,1:T(8,128)(2,1)}, u32[]{:S(2)}) copy-start(bf16[32,32]{0,1:T(8,128)(2,1)} %get-tuple-element.132) | copy-start | bytes 6148
  94.7 10.1 %copy-start.4 = (bf16[32,2048]{1,0:T(8,128)(2,1)S(1)}, bf16[32,2048]{1,0:T(8,128)(2,1)}, u32[]{:S(2)}) copy-start(bf16[32,2048]{1,0:T(8,128)(2,1)} %copy-done.3) | copy-start | bytes 393220
  94.7 10.1 %copy-start.6 = (bf16[16,4,8,128]{3,2,0,1:T(8,128)(2,1)S(1)}, bf16[16,4,8,128]{3,2,0,1:T(8,128)(2,1)}, u32[]{:S(2)}) copy-start(bf16[16,4,8,128]{3,2,0,1:T(8,128)(2,1)} %copy-done.5) | copy-start | bytes 393220
  94.7 35.8 %copy-start.1 = (f32[64,2048]{1,0:T(8,128)S(1)}, f32[64,2048]{1,0:T(8,128)}, u32[]{:S(2)}) copy-start(f32[64,2048]{1,0:T(8,128)} %get-tuple-element.151) | copy-start | bytes 1572868
  94.8 35.7 %copy-start.48 = (s32[2048]{0:T(1024)S(1)}, s32[2048]{0:T(1024)}, u32[]{:S(2)}) copy-start(s32[2048]{0:T(1024)} %convert_reduce_fusion) | copy-start | bytes 24580
  96.1 34.4 %all-to-all-start.1 = ((bf16[64,64,128]{2,0,1:T(8,128)(2,1)}), bf16[64,64,128]{2,0,1:T(8,128)(2,1)}, u32[]{:S(2)}, u32[]{:S(2)}) async-start(bf16[64,64,128]{2,0,1:T(8,128)(2,1)} %bitcast.383), calls=%async_computation.1 | async-start | bytes 2097152 | tf_op jit(solution)/shard_map/all_to_all | solution.py:106
  130.5 6.6 %copy-start.8 = (f32[32,2048]{1,0:T(8,128)S(1)}, f32[32,2048]{1,0:T(8,128)}, u32[]{:S(2)}) copy-start(f32[32,2048]{1,0:T(8,128)} %copy-done.7) | copy-start | bytes 786436
  130.5 6.6 %copy-start.9 = (f32[32,2048]{1,0:T(8,128)S(1)}, f32[32,2048]{1,0:T(8,128)}, u32[]{:S(2)}) copy-start(f32[32,2048]{1,0:T(8,128)} %get-tuple-element.154) | copy-start | bytes 786436
  130.5 6.6 %copy-start.30 = (f32[1,2048]{1,0:T(1,128)S(1)}, f32[1,2048]{1,0:T(1,128)}, u32[]{:S(2)}) copy-start(f32[1,2048]{1,0:T(1,128)} %param.32) | copy-start | bytes 24580
  138.2 9.3 %copy-start.11 = (bf16[32,2048]{1,0:T(8,128)(2,1)S(1)}, bf16[32,2048]{1,0:T(8,128)(2,1)}, u32[]{:S(2)}) copy-start(bf16[32,2048]{1,0:T(8,128)(2,1)} %copy-done.10) | copy-start | bytes 393220
  138.2 9.3 %copy-start.13 = (bf16[1,32,2048]{2,1,0:T(8,128)(2,1)S(1)}, bf16[1,32,2048]{2,1,0:T(8,128)(2,1)}, u32[]{:S(2)}) copy-start(bf16[1,32,2048]{2,1,0:T(8,128)(2,1)} %param.37) | copy-start | bytes 393220
  138.2 9.3 %copy-start.15 = (bf16[32,2048]{1,0:T(8,128)(2,1)S(1)}, bf16[32,2048]{1,0:T(8,128)(2,1)}, u32[]{:S(2)}) copy-start(bf16[32,2048]{1,0:T(8,128)(2,1)} %copy-done.14) | copy-start | bytes 393220
  139.4 15.5 %collective-permute-start.4 = (bf16[64,128]{1,0:T(8,128)(2,1)S(1)}, bf16[64,128]{1,0:T(8,128)(2,1)S(1)}, u32[]{:S(2)}, u32[]{:S(2)}) collective-permute-start(bf16[64,128]{1,0:T(8,128)(2,1)S(1)} %pad_maximum_fusion.11), channel_id=1, source_target_pairs={{0,1},{1,2},{2,3},{3,4},{4,5},{5,6},{6,7},{7,8},{8,9},{9,10},{10,1... | collective-permute-start | bytes 49160 | tf_op jit(solution)/shard_map/ppermute | solution.py:16
  142.1 12.8 %collective-permute-start.5 = (bf16[64,128]{1,0:T(8,128)(2,1)S(1)}, bf16[64,128]{1,0:T(8,128)(2,1)S(1)}, u32[]{:S(2)}, u32[]{:S(2)}) collective-permute-start(bf16[64,128]{1,0:T(8,128)(2,1)S(1)} %pad_maximum_fusion.12), channel_id=1, source_target_pairs={{1,0},{2,1},{3,2},{4,3},{5,4},{6,5},{7,6},{8,7},{9,8},{10,9},{11,1... | collective-permute-start | bytes 49160 | tf_op jit(solution)/shard_map/ppermute | solution.py:16
  148.8 17.6 %all-to-all-start.2 = ((f32[16,4,128]{2,1,0:T(4,128)}), f32[16,4,128]{2,1,0:T(4,128)}, u32[]{:S(2)}, u32[]{:S(2)}) async-start(f32[16,4,128]{2,1,0:T(4,128)} %bitcast.101), calls=%async_computation.2 | async-start | bytes 65536 | tf_op jit(solution)/shard_map/all_to_all | solution.py:93
  157.4 19.9 %copy-start.18 = (s32[64]{0:T(128)S(1)}, s32[64]{0:T(128)}, u32[]{:S(2)}) copy-start(s32[64]{0:T(128)} %copy-done.17) | copy-start | bytes 772
  158.0 6.8 %collective-permute-start.6 = (bf16[64,128]{1,0:T(8,128)(2,1)S(1)}, bf16[64,128]{1,0:T(8,128)(2,1)S(1)}, u32[]{:S(2)}, u32[]{:S(2)}) collective-permute-start(bf16[64,128]{1,0:T(8,128)(2,1)S(1)} %pad_maximum_fusion.13), channel_id=1, source_target_pairs={{0,1},{1,2},{2,3},{3,4},{4,5},{5,6},{6,7},{7,8},{8,9},{9,10},{10,1... | collective-permute-start | bytes 49160 | tf_op jit(solution)/shard_map/ppermute | solution.py:16
  159.9 5.7 %collective-permute-start.7 = (bf16[64,128]{1,0:T(8,128)(2,1)S(1)}, bf16[64,128]{1,0:T(8,128)(2,1)S(1)}, u32[]{:S(2)}, u32[]{:S(2)}) collective-permute-start(bf16[64,128]{1,0:T(8,128)(2,1)S(1)} %pad_maximum_fusion.14), channel_id=1, source_target_pairs={{1,0},{2,1},{3,2},{4,3},{5,4},{6,5},{7,6},{8,7},{9,8},{10,9},{11,1... | collective-permute-start | bytes 49160 | tf_op jit(solution)/shard_map/ppermute | solution.py:16
  166.4 25.8 %copy-start.33 = (bf16[32,32]{1,0:T(8,128)(2,1)S(1)}, bf16[32,32]{1,0:T(8,128)(2,1)}, u32[]{:S(2)}) copy-start(bf16[32,32]{1,0:T(8,128)(2,1)} %get-tuple-element.138) | copy-start | bytes 6148
  166.4 25.8 %copy-start.34 = (bf16[32,32]{1,0:T(8,128)(2,1)S(1)}, bf16[32,32]{1,0:T(8,128)(2,1)}, u32[]{:S(2)}) copy-start(bf16[32,32]{1,0:T(8,128)(2,1)} %get-tuple-element.142) | copy-start | bytes 6148
  166.4 25.8 %copy-start.35 = (bf16[32,32]{1,0:T(8,128)(2,1)S(1)}, bf16[32,32]{1,0:T(8,128)(2,1)}, u32[]{:S(2)}) copy-start(bf16[32,32]{1,0:T(8,128)(2,1)} %get-tuple-element.143) | copy-start | bytes 6148
  167.8 15.9 %all-to-all-start.3 = ((f32[16,4,128]{2,1,0:T(4,128)}), f32[16,4,128]{2,1,0:T(4,128)S(1)}, u32[]{:S(2)}, u32[]{:S(2)}) async-start(f32[16,4,128]{2,1,0:T(4,128)} %broadcast_in_dim.64), calls=%async_computation.3 | async-start | bytes 65536 | tf_op jit(solution)/shard_map/all_to_all | solution.py:82
  183.8 9.3 %copy-start.16 = (bf16[32,2048]{1,0:T(8,128)(2,1)S(1)}, bf16[32,2048]{1,0:T(8,128)(2,1)}, u32[]{:S(2)}) copy-start(bf16[32,2048]{1,0:T(8,128)(2,1)} %copy_bitcast_fusion.3) | copy-start | bytes 393220
  183.8 9.3 %copy-start.39 = (bf16[32,32]{1,0:T(8,128)(2,1)S(1)}, bf16[32,32]{1,0:T(8,128)(2,1)}, u32[]{:S(2)}) copy-start(bf16[32,32]{1,0:T(8,128)(2,1)} %copy.389) | copy-start | bytes 6148
  183.8 9.3 %copy-start.40 = (bf16[32,32]{1,0:T(8,128)(2,1)S(1)}, bf16[32,32]{1,0:T(8,128)(2,1)}, u32[]{:S(2)}) copy-start(bf16[32,32]{1,0:T(8,128)(2,1)} %copy.388) | copy-start | bytes 6148
  183.8 9.3 %copy-start.41 = (bf16[32,32]{1,0:T(8,128)(2,1)S(1)}, bf16[32,32]{1,0:T(8,128)(2,1)}, u32[]{:S(2)}) copy-start(bf16[32,32]{1,0:T(8,128)(2,1)} %copy.387) | copy-start | bytes 6148
  184.4 14.5 %all-to-all-start.4 = ((f32[16,4,128]{2,1,0:T(4,128)}), f32[16,4,128]{2,1,0:T(4,128)S(1)}, u32[]{:S(2)}, u32[]{:S(2)}) async-start(f32[16,4,128]{2,1,0:T(4,128)} %broadcast_in_dim.65), calls=%async_computation.4 | async-start | bytes 65536 | tf_op jit(solution)/shard_map/all_to_all | solution.py:82
  (13 other events, 14.4 us)

commit v2 on v1

v2 whole, which is shorter than its diff:
```python
import functools
import math

import jax
import jax.numpy as jnp
from jax import lax
from jax.experimental import pallas as pl
from jax.experimental.pallas import tpu as pltpu
from jax.sharding import PartitionSpec as P

LINE = ("region", "sub")
BF = jnp.bfloat16
F32 = jnp.float32
I32 = jnp.int32
LANES = 128
AUX = 8

VM = pl.BlockSpec(memory_space=pltpu.VMEM)
SM = pl.BlockSpec(memory_space=pltpu.SMEM)


def call(body, outs, scratch, args, smem=0, flops=0, limit=24):
    specs = [SM] * smem + [VM] * (len(args) - smem)
    moved = sum(a.size * a.dtype.itemsize for a in args)
    return pl.pallas_call(
        body,
        out_shape=tuple(jax.ShapeDtypeStruct(s, d) for s, d in outs),
        in_specs=specs,
        out_specs=tuple(VM for _ in outs),
        scratch_shapes=scratch,
        cost_estimate=pl.CostEstimate(flops=flops, bytes_accessed=moved, transcendentals=0),
        compiler_params=pltpu.CompilerParams(vmem_limit_bytes=limit << 20),
    )(*args)


def dot(a, b):
    return jnp.dot(a, b, preferred_element_type=F32)


def dot_nt(a, b):
    return lax.dot_general(a, b, (((1,), (1,)), ((), ())), preferred_element_type=F32)


def tile(ref, k):
    return ref[:, k * LANES : (k + 1) * LANES]


def shifted(value, by):
    peers = lax.axis_size(LINE)
    pairs = [(i, i + by) for i in range(peers) if 0 <= i + by < peers]
    return lax.ppermute(value, LINE, pairs)


def add_transposed(cols, tiles, grad_of, ext, count, nonzero):
    ext[...] = jnp.zeros_like(ext)
    for k in range(count):
        rhs = tiles[k * nonzero : (k + 1) * nonzero].reshape(nonzero * LANES, LANES)
        y = dot_nt(grad_of(k), rhs)
        for n in range(nonzero):
            ext[cols[k * nonzero + n]] += y[:, n * LANES : (n + 1) * LANES]


def row_product(cols, tiles, blocks, k, nonzero):
    picked = [blocks[cols[k * nonzero + n]] for n in range(nonzero)]
    rhs = tiles[k * nonzero : (k + 1) * nonzero].reshape(nonzero * LANES, LANES)
    return dot(jnp.concatenate(picked, axis=1), rhs)


def fill_blocks(blocks, field, up, down, chans, count):
    blocks[0] = up[0:chans, :]
    blocks[count + 1] = down[0:chans, :]
    for k in range(count):
        blocks[k + 1] = tile(field, k)


def write_sends(up, down, first, last, ext, chans, count):
    up[0:chans, :] = last
    up[chans : 2 * chans, :] = ext[count + 1].astype(BF)
    down[0:chans, :] = first
    down[chans : 2 * chans, :] = ext[0].astype(BF)


def inner_tile(inner, up, down, k, chans, count):
    value = tile(inner, k)
    if k == 0:
        value = value + up[chans : 2 * chans, :].astype(F32)
    if k == count - 1:
        value = value + down[chans : 2 * chans, :].astype(F32)
    return value


def start_body(cols, tiles, f, g, up, down, inner, ext, *, chans, count, nonzero):
    add_transposed(cols, tiles, lambda k: tile(g, k), ext, count, nonzero)
    write_sends(up, down, tile(f, 0), tile(f, count - 1), ext, chans, count)
    for k in range(count):
        inner[:, k * LANES : (k + 1) * LANES] = ext[k + 1]


def middle_body(
    cols, tiles, f, up, down, inner, f1, g1, up2, down2, inner2, blocks, ext,
    *, chans, count, nonzero
):
    fill_blocks(blocks, f, up, down, chans, count)
    for k in range(count):
        g1[:, k * LANES : (k + 1) * LANES] = inner_tile(inner, up, down, k, chans, count).astype(BF)
    for k in range(count):
        f1[:, k * LANES : (k + 1) * LANES] = row_product(cols, tiles, blocks, k, nonzero).astype(BF)
    add_transposed(cols, tiles, lambda k: tile(g1, k), ext, count, nonzero)
    write_sends(up2, down2, tile(f1, 0), tile(f1, count - 1), ext, chans, count)
    for k in range(count):
        inner2[:, k * LANES : (k + 1) * LANES] = ext[k + 1]


def second_terms(cols, tiles, f, g, f1, up, down, inner, blocks, f2, g2, chans, count, nonzero):
    fill_blocks(blocks, f1, up, down, chans, count)
    for k in range(count):
        at = slice(k * LANES, (k + 1) * LANES)
        y = row_product(cols, tiles, blocks, k, nonzero)
        f2[:, at] = (2.0 * y - f[:, at].astype(F32)).astype(BF)
        z = inner_tile(inner, up, down, k, chans, count)
        g2[:, at] = (2.0 * z - g[:, at].astype(F32)).astype(BF)


def place_body(owner, slot, dest, rank, most, *, peers, rows):
    d = owner[...] + slot[...]
    d = d - (d // peers) * peers
    dest[...] = d
    hot = lax.broadcasted_iota(I32, (peers, rows), 0) == d
    hot = jnp.where(hot, 1.0, 0.0).astype(F32)
    a = lax.broadcasted_iota(I32, (LANES, LANES), 0)
    b = lax.broadcasted_iota(I32, (LANES, LANES), 1)
    before = jnp.where(a < b, 1.0, 0.0).astype(BF)
    carry = jnp.zeros((peers, 1), F32)
    for k in range(rows // LANES):
        h = hot[:, k * LANES : (k + 1) * LANES]
        c = dot(h.astype(BF), before) + carry
        rank[:, k * LANES : (k + 1) * LANES] = jnp.sum(h * c, axis=0, keepdims=True).astype(I32)
        carry = carry + jnp.sum(h, axis=1, keepdims=True)
    most[...] = jnp.broadcast_to(jnp.max(carry, axis=0, keepdims=True), (AUX, LANES))


def slot_hot(dest, rank, step, cap, go, rows):
    at = rank - step * cap
    inside = (at >= 0) & (at < cap)
    col = jnp.where(inside, (dest - (dest // go) * go) * cap + at, -1)
    hot = lax.broadcasted_iota(I32, (go * cap, rows), 0) == col
    return jnp.where(hot, 1.0, 0.0).astype(BF)


def merge_halves(low, high, odd, cap):
    if cap == LANES // 2:
        left = lax.broadcasted_iota(I32, low.shape, 1) < cap
        if odd:
            return jnp.where(left, pltpu.roll(low, cap, 1), high)
        return jnp.where(left, low, pltpu.roll(high, cap, 1))
    at = slice(cap, 2 * cap) if odd else slice(0, cap)
    return jnp.concatenate([low[:, at], high[:, at]], axis=1)


def pack_into(buffer, big, sent, dest, rank, most, step, *, chans, peers, cap, go, rows):
    high = 2 * chans + AUX
    group = dest // go
    for g in range(peers // go):
        big[g * high : (g + 1) * high, :] = jnp.where(group == g, sent, 0.0).astype(BF)
    out = dot_nt(big[...], slot_hot(dest, rank, step, cap, go, rows))
    row = lax.broadcasted_iota(I32, (AUX, 2 * cap), 0)
    lane = lax.broadcasted_iota(I32, (AUX, 2 * cap), 1)
    extra = jnp.where((row == 1) & (lane >= cap), float(LANES), 0.0)
    extra = extra + jnp.where(row == 2, most, 0.0)
    for p in range(peers):
        g, o = p // go, p % go
        pair = o // 2 * 2 * cap
        part = out[g * high : (g + 1) * high, pair : pair + 2 * cap]
        if go == 1:
            part = jnp.concatenate([out[g * high : (g + 1) * high]] * 2, axis=1)
        odd = o % 2 == 1
        buffer[p, 0:chans, :] = merge_halves(
            part[0:chans], part[chans : 2 * chans], odd, cap
        ).astype(BF)
        aux = part[2 * chans : high]
        buffer[p, chans : chans + AUX, :] = (merge_halves(aux, aux, odd, cap) + extra).astype(BF)


def pack_body(step, sent, dest, rank, most, buffer, big, *, cap, **sizes):
    needed = jnp.ceil(most[0:1, 0:1] * (1.0 / cap))
    pack_into(
        buffer, big, sent[...].astype(F32), dest[...], rank[...], needed, step[0], cap=cap, **sizes
    )


def unpack_body(step, back, dest, rank, lifted, big, *, chans, peers, cap, go, rows):
    d = dest[...]
    hot = slot_hot(d, rank[...], step[0], cap, go, rows)
    group = d // go
    high = 2 * chans
    for p in range(0, peers, 2 if go > 1 else 1):
        g, o = p // go, p % go
        a = back[p].astype(F32)
        if go == 1:
            low, top = a[:, 0:cap], a[:, cap : 2 * cap]
            at = slice(0, cap)
        else:
            b = back[p + 1].astype(F32)
            at = slice(o * cap, (o + 2) * cap)
            if cap == LANES // 2:
                low, top = merge_halves(a, b, False, cap), merge_halves(a, b, True, cap)
            else:
                low = jnp.concatenate([a[:, 0:cap], b[:, 0:cap]], axis=1)
                top = jnp.concatenate([a[:, cap:], b[:, cap:]], axis=1)
        big[g * high : g * high + chans, at] = low.astype(BF)
        big[g * high + chans : (g + 1) * high, at] = top.astype(BF)
    width = min(256, rows)
    for w in range(rows // width):
        at = slice(w * width, (w + 1) * width)
        y = dot(big[...], hot[:, at])
        total = jnp.zeros((high, width), F32)
        for g in range(peers // go):
            total = jnp.where(group[:, at] == g, y[g * high : (g + 1) * high], total)
        lifted[:, at] = total.astype(BF)


def coarse_hot(got, hot, masked, *, chans, peers, cap, parts):
    wide = 2 * cap

    def one(p, carry):
        aux = got[p, chans : chans + AUX, :].astype(F32)
        at = pl.ds(pl.multiple_of(p * wide, wide), wide)
        code = aux[1:2, :].astype(I32)
        q = lax.broadcasted_iota(I32, (2 * LANES, wide), 0)
        hot[:, at] = jnp.where(q == code, 1.0, 0.0).astype(BF)
        if masked is not None:
            body = got[p, 0:chans, :].astype(F32)
            for h in range(parts):
                masked[h * chans : (h + 1) * chans, at] = jnp.where(
                    aux[0:1, :] == h + 1.0, body, 0.0
                ).astype(BF)
        return carry

    lax.fori_loop(0, peers, one, 0, unroll=4)


def coarse_totals(hot, masked, chans, parts):
    acc = dot_nt(masked[...], hot[...])
    split = [acc[h * chans : (h + 1) * chans] for h in range(parts)]
    low = jnp.concatenate([s[:, 0:LANES] for s in split], axis=1)
    top = jnp.concatenate([s[:, LANES:] for s in split], axis=1)
    return low, top


def slope(value):
    sig = jax.nn.sigmoid(value)
    return sig * (1.0 + value * (1.0 - sig))


def coarse_math(coarse_sum, coarse_grad, weight, weight_t, bias, grads):
    coarse = coarse_sum.astype(BF)
    pre = dot(weight[...], coarse) + bias[...]
    out = (pre * jax.nn.sigmoid(pre)).astype(BF)
    mid_grad = (coarse_grad * slope(pre)).astype(BF)
    chans = pre.shape[0]
    grads[0:chans, :] = dot_nt(mid_grad, coarse)
    grads[chans : 2 * chans, :] = jnp.broadcast_to(
        jnp.sum(mid_grad.astype(F32), axis=1, keepdims=True), (chans, chans)
    )
    return out, dot(weight_t[...], mid_grad).astype(BF)


def coarse_gather(back, got, hot, out, behind, *, chans, peers, cap, parts):
    wide = 2 * cap
    stacked = [
        jnp.concatenate(
            [out[:, h * LANES : (h + 1) * LANES], behind[:, h * LANES : (h + 1) * LANES]], axis=1
        )
        for h in range(parts)
    ]
    stacked = jnp.concatenate(stacked, axis=0)
    step = max(1, 512 // wide)

    def one(b, carry):
        at = pl.ds(pl.multiple_of(b * step * wide, step * wide), step * wide)
        y = dot(stacked, hot[:, at])
        for j in range(step):
            p = b * step + j
            part = got[p, chans : chans + AUX, :].astype(F32)[0:1, :]
            total = jnp.zeros((chans, wide), F32)
            for h in range(parts):
                total = jnp.where(
                    part == h + 1.0,
                    y[h * chans : (h + 1) * chans, j * wide : (j + 1) * wide],
                    total,
                )
            back[p] = total.astype(BF)
        return carry

    lax.fori_loop(0, peers // step, one, 0, unroll=2)


def coarse_body(got, weight, weight_t, bias, back, grads, hot, masked, **sizes):
    coarse_hot(got, hot, masked, **sizes)
    low, top = coarse_totals(hot, masked, sizes["chans"], sizes["parts"])
    out, behind = coarse_math(low, top, weight, weight_t, bias, grads)
    coarse_gather(back, got, hot, out, behind, **sizes)


def totals_body(got, before, after, hot, masked, **sizes):
    chans = sizes["chans"]
    coarse_hot(got, hot, masked, **sizes)
    low, top = coarse_totals(hot, masked, chans, sizes["parts"])
    after[0:chans, :] = before[0:chans, :] + low
    after[chans : 2 * chans, :] = before[chans : 2 * chans, :] + top


def math_body(totals, weight, weight_t, bias, values, grads):
    chans = totals.shape[0] // 2
    out, behind = coarse_math(
        totals[0:chans, :], totals[chans : 2 * chans, :], weight, weight_t, bias, grads
    )
    values[0:chans, :] = out
    values[chans : 2 * chans, :] = behind


def gather_body(got, values, back, hot, **sizes):
    chans = sizes["chans"]
    coarse_hot(got, hot, None, **sizes)
    coarse_gather(
        back, got, hot, values[0:chans, :], values[chans : 2 * chans, :], **sizes
    )


def first_end_body(
    cols, tiles, f, g, f1, g1, up, down, inner, pool, mix_in, mix_out_t, bias,
    dest, rank, most, slot, owner,
    f2, g2, pre_in, hidden, merged_grad, sent, buffer, blocks, big,
    *, chans, count, nonzero, peers, cap, go, rows
):
    second_terms(cols, tiles, f, g, f1, up, down, inner, blocks, f2, g2, chans, count, nonzero)
    for k in range(count):
        at = slice(k * LANES, (k + 1) * LANES)
        w = pool[:, at]
        pre = dot(mix_in[...], jnp.concatenate([f[:, at], f1[:, at], f2[:, at]], axis=0)) + bias[...]
        pre_in[:, at] = pre
        h = (pre * jax.nn.sigmoid(pre)).astype(BF)
        hidden[:, at] = h
        m = dot(mix_out_t[...], jnp.concatenate([g[:, at], g1[:, at], g2[:, at]], axis=0)).astype(BF)
        merged_grad[:, at] = m
        sent[0:chans, at] = (w * h.astype(F32)).astype(BF)
        sent[chans : 2 * chans, at] = (w * m.astype(F32)).astype(BF)
    each = rows // 4 // peers
    index = owner[...] * each + slot[...] // peers
    part = index // LANES
    row = lax.broadcasted_iota(I32, (AUX, rows), 0)
    sent[2 * chans : 2 * chans + AUX, :] = (
        jnp.where(row == 0, part + 1, jnp.where(row == 1, index - part * LANES, 0))
        .astype(F32)
        .astype(BF)
    )
    needed = jnp.ceil(most[0:1, 0:1] * (1.0 / cap))
    pack_into(
        buffer, big, sent[...].astype(F32), dest[...], rank[...], needed, 0,
        chans=chans, peers=peers, cap=cap, go=go, rows=rows,
    )


def second_start_body(
    cols, tiles, lifted, hidden, merged_grad, pre_in, pool,
    merged, pre_grad, up, down, inner, ext,
    *, chans, count, nonzero
):
    for k in range(count):
        at = slice(k * LANES, (k + 1) * LANES)
        w = pool[:, at]
        merged[:, at] = (
            hidden[:, at].astype(F32) + w * lifted[0:chans, at].astype(F32)
        ).astype(BF)
        hidden_grad = merged_grad[:, at].astype(F32) + w * lifted[chans : 2 * chans, at].astype(F32)
        pre_grad[:, at] = (hidden_grad * slope(pre_in[:, at])).astype(BF)
    add_transposed(cols, tiles, lambda k: tile(pre_grad, k), ext, count, nonzero)
    write_sends(up, down, tile(merged, 0), tile(merged, count - 1), ext, chans, count)
    for k in range(count):
        inner[:, k * LANES : (k + 1) * LANES] = ext[k + 1]


def weights_body(merged, pre_grad, f, f1, f2, g, g1, g2, mid, local, *, chans):
    p, m = pre_grad[...], merged[...]
    gin = [dot_nt(p, t[...]) for t in (f, f1, f2)]
    gout = [dot_nt(t[...], m) for t in (g, g1, g2)]
    local[0:chans, :] = jnp.concatenate(gin + [mid[0:chans, :]], axis=1)
    total = jnp.broadcast_to(jnp.sum(p.astype(F32), axis=1, keepdims=True), (chans, chans))
    lane = lax.broadcasted_iota(I32, (chans, chans), 1)
    sums = jnp.where(lane == 0, total, mid[chans : 2 * chans, :])
    local[chans : 2 * chans, :] = jnp.concatenate(gout + [sums], axis=1)


def second_end_body(
    cols, tiles, f, g, f1, g1, up, down, inner, mix_out, mix_in_t,
    result, input_grad, f2, g2, blocks,
    *, chans, count, nonzero
):
    second_terms(cols, tiles, f, g, f1, up, down, inner, blocks, f2, g2, chans, count, nonzero)
    for k in range(count):
        at = slice(k * LANES, (k + 1) * LANES)
        terms = jnp.concatenate([f[:, at], f1[:, at], f2[:, at]], axis=0)
        result[:, at] = dot(mix_out[...], terms).astype(BF)
        terms = jnp.concatenate([g[:, at], g1[:, at], g2[:, at]], axis=0)
        input_grad[:, at] = dot(mix_in_t[...], terms).astype(BF)


def spread(values, axes):
    peers = lax.axis_size(axes)
    return lax.all_to_all(
        jnp.broadcast_to(values[None], (peers, *values.shape)), axes, 0, 0, tiled=True
    )


def summed_everywhere(local):
    regions = lax.axis_size("region")
    parts = local.reshape(regions, -1, LANES)
    mine = jnp.sum(lax.all_to_all(parts, "region", 0, 0, tiled=True), axis=0)
    mine = jnp.sum(spread(mine, ("geo", "sub")), axis=0)
    return spread(mine, "region").reshape(local.shape)


def exchanged(buffer):
    return lax.all_to_all(buffer, LINE, 0, 0, tiled=True)


def on_device(
    features,
    lap_tiles,
    tile_cols,
    coarse_owner,
    coarse_slot,
    pool_weight,
    weight_in,
    weight_mid,
    weight_out,
    biases,
    out_grad,
):
    chans, rows = features.shape[1:]
    count, nonzero = lap_tiles.shape[1:3]
    peers = lax.axis_size(LINE)
    cap = 2 * rows // peers
    go = max(1, 256 // cap)
    coarse_rows = rows // 4
    parts = coarse_rows // LANES
    f, g = features[0], out_grad[0]
    tiles = lap_tiles[0].reshape(count * nonzero, LANES, LANES)
    cols = tile_cols[0].reshape(-1)
    owner = coarse_owner[0].reshape(1, rows)
    slot = coarse_slot
    pool = pool_weight
    side = lambda w: jnp.concatenate([w[k] for k in range(3)], axis=1)
    side_t = lambda w: jnp.concatenate([w[k].T for k in range(3)], axis=1)
    line = dict(chans=chans, count=count, nonzero=nonzero)
    ways = dict(chans=chans, peers=peers, cap=cap, go=go, rows=rows)
    level = dict(chans=chans, peers=peers, cap=cap, parts=parts)
    full = (chans, rows)
    halo = (2 * chans, LANES)
    ext = pltpu.VMEM((count + 2, chans, LANES), F32)
    blocks = pltpu.VMEM((count + 2, chans, LANES), BF)
    work = 2 * chans * rows * nonzero * LANES
    chunk = (peers, chans + AUX, 2 * cap)
    reply = (peers, chans, 2 * cap)
    hot_s = pltpu.VMEM((2 * LANES, peers * 2 * cap), BF)
    masked_s = pltpu.VMEM((parts * chans, peers * 2 * cap), BF)
    pack_s = pltpu.VMEM((peers // go * (2 * chans + AUX), rows), BF)
    lift_s = pltpu.VMEM((peers // go * 2 * chans, go * cap), BF)

    up, down, inner = call(
        functools.partial(start_body, **line),
        [(halo, BF), (halo, BF), (full, F32)],
        [ext],
        (cols, tiles, f, g),
        smem=1,
        flops=work,
    )
    up, down = shifted(up, 1), shifted(down, -1)
    dest, rank, most = call(
        functools.partial(place_body, peers=peers, rows=rows),
        [((1, rows), I32), ((1, rows), I32), ((AUX, LANES), F32)],
        [],
        (owner, slot),
        flops=2 * work,
    )
    f1, g1, up, down, inner = call(
        functools.partial(middle_body, **line),
        [(full, BF), (full, BF), (halo, BF), (halo, BF), (full, F32)],
        [blocks, ext],
        (cols, tiles, f, up, down, inner),
        smem=1,
        flops=2 * work,
    )
    up, down = shifted(up, 1), shifted(down, -1)
    f2, g2, pre_in, hidden, merged_grad, sent, buffer = call(
        functools.partial(first_end_body, **line, peers=peers, cap=cap, go=go, rows=rows),
        [
            (full, BF),
            (full, BF),
            (full, F32),
            (full, BF),
            (full, BF),
            ((2 * chans + AUX, rows), BF),
            (chunk, BF),
        ],
        [blocks, pack_s],
        (
            cols, tiles, f, g, f1, g1, up, down, inner, pool, side(weight_in), side_t(weight_out),
            biases[0][:, None], dest, rank, most, slot, owner,
        ),
        smem=1,
        flops=4 * work,
        limit=32,
    )
    got = exchanged(buffer)
    rounds = jnp.max(got[:, chans + 2, 0].astype(F32)).astype(I32)
    bias_mid = biases[1][:, None]
    weight_mid_t = weight_mid.T

    def unpacked(back, step):
        return call(
            functools.partial(unpack_body, **ways),
            [((2 * chans, rows), BF)],
            [lift_s],
            (step, back, dest, rank),
            smem=1,
        )[0]

    def one_round(got):
        back, grads = call(
            functools.partial(coarse_body, **level),
            [(reply, BF), ((2 * chans, chans), F32)],
            [hot_s, masked_s],
            (got, weight_mid, weight_mid_t, bias_mid),
            limit=32,
        )
        return unpacked(exchanged(back), jnp.zeros((1,), I32)), grads

    def more_rounds(got):
        def received(step):
            return exchanged(
                call(
                    functools.partial(pack_body, **ways),
                    [(chunk, BF)],
                    [pack_s],
                    (step.reshape(1), sent, dest, rank, most),
                    smem=1,
                    limit=32,
                )[0]
            )

        def add(step, totals):
            return call(
                functools.partial(totals_body, **level),
                [((2 * chans, coarse_rows), F32)],
                [hot_s, masked_s],
                (received(step), totals),
                limit=32,
            )[0]

        totals = lax.fori_loop(0, rounds, add, jnp.zeros((2 * chans, coarse_rows), F32))
        values, grads = call(
            math_body,
            [((2 * chans, coarse_rows), BF), ((2 * chans, chans), F32)],
            [],
            (totals, weight_mid, weight_mid_t, bias_mid),
        )

        def fetch(step, lifted):
            back = call(
                functools.partial(gather_body, **level),
                [(reply, BF)],
                [hot_s],
                (received(step), values),
                limit=32,
            )[0]
            return lifted + unpacked(exchanged(back), step.reshape(1))

        return lax.fori_loop(0, rounds, fetch, jnp.zeros((2 * chans, rows), BF)), grads

    lifted, mid = lax.cond(rounds > 1, more_rounds, one_round, got)

    merged, pre_grad, up, down, inner = call(
        functools.partial(second_start_body, **line),
        [(full, BF), (full, BF), (halo, BF), (halo, BF), (full, F32)],
        [ext],
        (cols, tiles, lifted, hidden, merged_grad, pre_in, pool),
        smem=1,
        flops=work,
    )
    up, down = shifted(up, 1), shifted(down, -1)
    local = call(
        functools.partial(weights_body, chans=chans),
        [((2 * chans, LANES), F32)],
        [],
        (merged, pre_grad, f, f1, f2, g, g1, g2, mid),
        flops=work,
    )[0]
    m1, p1, up, down, inner = call(
        functools.partial(middle_body, **line),
        [(full, BF), (full, BF), (halo, BF), (halo, BF), (full, F32)],
        [blocks, ext],
        (cols, tiles, merged, up, down, inner),
        smem=1,
        flops=2 * work,
    )
    up, down = shifted(up, 1), shifted(down, -1)
    result, input_grad = call(
        functools.partial(second_end_body, **line),
        [(full, BF), (full, BF)],
        [pltpu.VMEM(full, BF), pltpu.VMEM(full, BF), blocks],
        (
            cols, tiles, merged, pre_grad, m1, p1, up, down, inner,
            side(weight_out), side_t(weight_in),
        ),
        smem=1,
        flops=2 * work,
    )
    factor = 1.0 / math.sqrt(lax.axis_size("geo") * rows * peers)
    total = summed_everywhere(local) * factor
    first = total[:chans].reshape(chans, 4, chans).transpose(1, 0, 2)
    second = total[chans:].reshape(chans, 4, chans).transpose(1, 0, 2)
    sum_weights = jnp.concatenate([first, second[:3]], axis=0)
    sum_biases = second[3, :, :2].T
    return (result[None], input_grad[None], sum_weights, sum_biases)


def solution(mesh):
    line = ("region", "sub")
    in_specs = (
        P("geo", None, line),
        P("geo", line, None, None, None),
        P("geo", line, None),
        P("geo", line, None),
        P("geo", line),
        P("geo", line),
        P(),
        P(),
        P(),
        P(),
        P("geo", None, line),
    )
    out_specs = (P("geo", None, line), P("geo", None, line), P(), P())
    return jax.shard_map(
        on_device, mesh=mesh, in_specs=in_specs, out_specs=out_specs, check_vma=False
    )
```

time: 201 us -> 162 us (0.81)
  matrix products: 34.3 us -> 0 us
  Pallas kernels: 0 us -> 23.5 us
  waiting for transfers between devices: 40.6 us -> 25.7 us
  other arithmetic: 9.6 us -> 0.94 us
  blocking collectives: 42.2 us -> 35.2 us
    dot_general x29 -> x0, matrix products: 34.3 us -> none  [the longest x1 6.55 us: on_device(): jnp.einsum('cor,ir->coi', back, rank_hot, preferred_element_type=F32)]
    pallas_call x0 -> x10, Pallas kernels: none -> 23.5 us  [call(): pl.pallas_call(body, out_shape=tuple((jax.ShapeDtypeStruct(s, d) for s, d...]
    unnamed x103 -> x68, local copies, waits for them, and re-layouts: 2.73 us -> 12 us
    all_to_all x1 -> x2, blocking collectives: 42.2 us -> 35.2 us  [the longest x1 23.1 us: exchanged(): return lax.all_to_all(buffer, LINE, 0, 0, tiled=True)]
    reduce_sum x3 -> x1, other arithmetic: 6.11 us -> 0.03 us  [summed_everywhere(): mine = jnp.sum(lax.all_to_all(parts, 'region', 0, 0, tiled=True), axis=0)]
    all_to_all x2, waiting for transfers between devices: 11 us -> 5.35 us  [spread(): lax.all_to_all(jnp.broadcast_to(values[None], (peers, *values.shape)), ax...]
    all_to_all x2 -> x1, waiting for transfers between devices: 24.6 us -> 19.7 us  [exchanged(): return lax.all_to_all(buffer, LINE, 0, 0, tiled=True)]
    all_to_all x2, starting transfers between devices: 16.6 us -> 11.9 us  [spread(): lax.all_to_all(jnp.broadcast_to(values[None], (peers, *values.shape)), ax...]
  transfers between devices with their start and end apart: 12 -> 11, of which waited for: 5 -> 3; matrix products, arithmetic and copies ran while one was open for 11% -> 2% of each run, Pallas kernels for 0% -> 3%
where the time goes in v2:
time: 162 us; the launch traced here: 161 us
  starting transfers between devices  57.6 us (36%)
  blocking collectives  35.2 us (22%)
  waiting for transfers between devices  25.7 us (16%)
  Pallas kernels  23.5 us (15%)
  local copies, waits for them, and re-layouts  15.9 us (10%)
  between operations  1.7 us (1%)
    ppermute x8, starting transfers between devices, shifted(): return lax.ppermute(value, LINE, pairs)  29.2 us
    pallas_call x10, Pallas kernels, call(): pl.pallas_call(body, out_shape=tuple((jax.ShapeDtypeStruct(s, d) for s, d...  23.5 us
    all_to_all x1, blocking collectives, exchanged(): return lax.all_to_all(buffer, LINE, 0, 0, tiled=True)  23.1 us
    all_to_all x1, waiting for transfers between devices, exchanged(): return lax.all_to_all(buffer, LINE, 0, 0, tiled=True)  19.7 us
    all_to_all x1, starting transfers between devices, exchanged(): return lax.all_to_all(buffer, LINE, 0, 0, tiled=True)  16.5 us
    all_to_all x1, blocking collectives, summed_everywhere(): mine = jnp.sum(lax.all_to_all(parts, 'region', 0, 0, tiled=True), axis=0)  12.1 us
    unnamed x68, local copies, waits for them, and re-layouts  12 us
    all_to_all x2, starting transfers between devices, spread(): lax.all_to_all(jnp.broadcast_to(values[None], (peers, *values.shape)), ax...  11.9 us
  transfers between devices with their start and end apart: 11, of which 3 were waited for; matrix products, arithmetic and copies ran while one was open for 2% of the time, Pallas kernels for 3%

profile of v2, /device:TPU:1, one launch (start us, length us, event | category | flops | bytes accessed | tf_op | source)
XLA Modules:
  0.0 160.5 jit_solution(2020254416864345531)
XLA Ops:
  0.6 0.8 copy.70
  1.5 1.6 copy-done
  3.1 0.9 copy-done.2
  4.0 0.9 copy-done.4
  4.9 1.4 shard_map.138
  6.4 4.1 %collective-permute-start = (bf16[64,128]{1,0:T(8,128)(2,1)S(1)}, bf16[64,128]{1,0:T(8,128)(2,1)S(1)}, u32[]{:S(2)}, u32[]{:S(2)}) collective-permute-start(bf16[64,128]{1,0:T(8,128)(2,1)S(1)} %get-tuple-element.163), channel_id=1, source_target_pairs={{0,1},{1,2},{2,3},{3,4},{4,5},{5,6},{6,7},{7,8},{8,9},{9,10},{10,1... | collective-permute-start | bytes 49160 | tf_op jit(solution)/shard_map/ppermute | solution.py:51
  10.4 3.7 %collective-permute-start.1 = (bf16[64,128]{1,0:T(8,128)(2,1)S(1)}, bf16[64,128]{1,0:T(8,128)(2,1)S(1)}, u32[]{:S(2)}, u32[]{:S(2)}) collective-permute-start(bf16[64,128]{1,0:T(8,128)(2,1)S(1)} %get-tuple-element.164), channel_id=1, source_target_pairs={{1,0},{2,1},{3,2},{4,3},{5,4},{6,5},{7,6},{8,7},{9,8},{10,9},{11,1... | collective-permute-start | bytes 49160 | tf_op jit(solution)/shard_map/ppermute | solution.py:51
  14.2 0.6 fusion.1
  14.8 0.6 slice_bitcast_fusion.5
  15.8 1.7 %shard_map.139 = (bf16[32,2048]{1,0:T(8,128)(2,1)S(1)}, bf16[32,2048]{1,0:T(8,128)(2,1)S(1)}, bf16[64,128]{1,0:T(8,128)(2,1)S(1)}, bf16[64,128]{1,0:T(8,128)(2,1)S(1)}, f32[32,2048]{1,0:T(8,128)S(1)}) custom-call(s32[64]{0:T(128)S(1)} %reshape_squeeze.9.cols, bf16[64,128,128]{2,1,0:T(8,128)(2,1)S(1)} %bitcast.55, bf16[32,2048]{1,0:T(8,128)(2,1)S(1)} %bitcast.61, ...), custom_call_target="tpu_custom_call" | custom-call | flops 134217728 | bytes 2523392 | tf_op jit(solution)/shard_map/pallas_call | solution.py:25
  17.5 2.3 %collective-permute-start.2 = (bf16[64,128]{1,0:T(8,128)(2,1)S(1)}, bf16[64,128]{1,0:T(8,128)(2,1)S(1)}, u32[]{:S(2)}, u32[]{:S(2)}) collective-permute-start(bf16[64,128]{1,0:T(8,128)(2,1)S(1)} %get-tuple-element.168), channel_id=1, source_target_pairs={{0,1},{1,2},{2,3},{3,4},{4,5},{5,6},{6,7},{7,8},{8,9},{9,10},{10,1... | collective-permute-start | bytes 49160 | tf_op jit(solution)/shard_map/ppermute | solution.py:51
  19.8 4.5 %collective-permute-start.3 = (bf16[64,128]{1,0:T(8,128)(2,1)S(1)}, bf16[64,128]{1,0:T(8,128)(2,1)S(1)}, u32[]{:S(2)}, u32[]{:S(2)}) collective-permute-start(bf16[64,128]{1,0:T(8,128)(2,1)S(1)} %get-tuple-element.169), channel_id=1, source_target_pairs={{1,0},{2,1},{3,2},{4,3},{5,4},{6,5},{7,6},{8,7},{9,8},{10,9},{11,1... | collective-permute-start | bytes 49160 | tf_op jit(solution)/shard_map/ppermute | solution.py:51
  24.5 0.9 shard_map.140
  25.4 3.7 %shard_map.141 = (bf16[32,2048]{1,0:T(8,128)(2,1)S(1)}, bf16[32,2048]{1,0:T(8,128)(2,1)S(1)}, f32[32,2048]{1,0:T(8,128)S(1)}, bf16[32,2048]{1,0:T(8,128)(2,1)S(1...) custom-call(s32[64]{0:T(128)S(1)} %reshape_squeeze.9.cols, ...), custom_call_target="tpu_custom_call" | custom-call | flops 268435456 | bytes 2974080 | tf_op jit(solution)/shard_map/pallas_call | solution.py:25
  29.1 0.7 copy-done.6
  29.8 0.7 copy-done.8
  30.5 0.7 copy-done.10
  31.1 0.7 copy-done.12
  31.8 16.5 %all-to-all-start.4 = ((bf16[64,40,128]{2,1,0:T(8,128)(2,1)}), bf16[64,40,128]{2,1,0:T(8,128)(2,1)S(1)}, u32[]{:S(2)}, u32[]{:S(2)}) async-start(bf16[64,40,128]{2,1,0:T(8,128)(2,1)} %get-tuple-element.174), calls=%async_computation.4 | async-start | bytes 1310720 | tf_op jit(solution)/shard_map/all_to_all | solution.py:424
  48.4 19.7 %all-to-all-done.4 = bf16[64,40,128]{2,1,0:T(8,128)(2,1)S(1)} async-done(((bf16[64,40,128]{2,1,0:T(8,128)(2,1)}), bf16[64,40,128]{2,1,0:T(8,128)(2,1)S(1)}, u32[]{:S(2)}, u32[]{:S(2)}) %all-to-all-start.4) | async-done | bytes 655392 | tf_op jit(solution)/shard_map/all_to_all | solution.py:424
  68.1 0.7 slice_reduce_fusion
  69.5 32.3 %conditional.1 = (bf16[64,2048]{1,0:T(8,128)(2,1)}, f32[64,32]{1,0:T(8,128)}) conditional(s32[]{:T(128)} %convert_element_type.8, (bf16[64,40,128]{2,1,0:T(8,128)(2,1)S(1)}, bf16[32,32]{1,0:T(8,128)(2,1)S(1)}, bf16[32,32]{1,0:T(8,128)(2,1)S(1)}, f32[32,1]{0,1:T(1,128)S(1)}, s32[1,2048]{1,0:T(1,128)}, /*index=5*/s32[1,2048]{1,0:T(1,128)}) %tuple.81, ...), branch_computations={%region_1.0_spmd, %region_2.0_spmd} | conditional | flops 131076 | bytes 9122668 | solution.py:581
  69.6 6.3 %branch_0_fun.2 = (bf16[64,32,128]{2,1,0:T(8,128)(2,1)S(1)}, f32[64,32]{1,0:T(8,128)}) custom-call(bf16[64,40,128]{2,1,0:T(8,128)(2,1)S(1)} %get-tuple-element.88.got, bf16[32,32]{1,0:T(8,128)(2,1)S(1)} %get-tuple-element.89.weight, bf16[32,32]{1,0:T(8,128)(2,1)S(1)} %get-tuple-element.90.weight_t, f32[32,1]{1,0:T(8,128)S(1)} %copy.82.bias), custom_call_target="tpu_custom_call" | custom-call | bytes 659584 | tf_op jit(solution)/shard_map/cond/branch_0_fun/pallas_call | solution.py:25
  75.9 23.1 %all_to_all.42.back = bf16[64,32,128]{2,1,0:T(8,128)(2,1)S(1)} all-to-all(bf16[64,32,128]{2,1,0:T(8,128)(2,1)S(1)} %get-tuple-element.92), channel_id=1, replica_groups=mesh['geo'=4,'region'=16,'sub'=4] {'region','sub'}, dimensions={0} | all-to-all | bytes 1048576 | tf_op jit(solution)/shard_map/cond/branch_0_fun/all_to_all | solution.py:424
  99.0 2.8 %branch_0_fun.3 = bf16[64,2048]{1,0:T(8,128)(2,1)} custom-call(s32[1]{0:T(128)} %constant.3.clone.step, bf16[64,32,128]{2,1,0:T(8,128)(2,1)S(1)} %all_to_all.42.back, s32[1,2048]{1,0:T(1,128)} %get-tuple-element.93.dest, s32[1,2048]{1,0:T(1,128)} %get-tuple-element.94.rank), custom_call_target="tpu_custom_call" | custom-call | bytes 540676 | tf_op jit(solution)/shard_map/cond/branch_0_fun/pallas_call | solution.py:25
  101.8 0.9 copy-done.7
  102.7 0.9 copy-done.11
  103.6 0.9 copy-done.13
  104.5 0.7 copy-done.15
  105.2 0.7 copy-done.17
  105.9 1.9 %shard_map.142 = (bf16[32,2048]{1,0:T(8,128)(2,1)S(1)}, bf16[32,2048]{1,0:T(8,128)(2,1)S(1)}, bf16[64,128]{1,0:T(8,128)(2,1)S(1)}, bf16[64,128]{1,0:T(8,128)(2,1)S(1)}, f32[32,2048]{1,0:T(8,128)S(1)}) custom-call(s32[64]{0:T(128)S(1)} %copy-done.17, bf16[64,128,128]{2,1,0:T(8,128)(2,1)S(1)} %bitcast.57, bf16[64,2048]{1,0:T(8,128)(2,1)} %get-tuple-element.176.lifted, ...), custom_call_target="tpu_custom_call" | custom-call | flops 67108864 | bytes 2892032 | tf_op jit(solution)/shard_map/pallas_call | solution.py:25
  107.8 1.2 shard_map.145
  109.0 12.1 %all_to_all.43 = f32[16,4,128]{2,1,0:T(4,128)S(1)} all-to-all(f32[16,4,128]{2,1,0:T(4,128)S(1)} %bitcast.67), channel_id=1, replica_groups=mesh['geo'=4,'region'=16,'sub'=4] {'region'}, dimensions={0} | all-to-all | bytes 65536 | tf_op jit(solution)/shard_map/all_to_all | solution.py:418
  121.1 0.6 broadcast_in_dim.20
  121.8 5.5 %all-to-all-start.6 = ((f32[16,4,128]{2,1,0:T(4,128)}), f32[16,4,128]{2,1,0:T(4,128)S(1)}, u32[]{:S(2)}, u32[]{:S(2)}) async-start(f32[16,4,128]{2,1,0:T(4,128)} %broadcast_in_dim.20), calls=%async_computation.6 | async-start | bytes 65536 | tf_op jit(solution)/shard_map/all_to_all | solution.py:410
  127.3 3.3 %collective-permute-start.4 = (bf16[64,128]{1,0:T(8,128)(2,1)S(1)}, bf16[64,128]{1,0:T(8,128)(2,1)S(1)}, u32[]{:S(2)}, u32[]{:S(2)}) collective-permute-start(bf16[64,128]{1,0:T(8,128)(2,1)S(1)} %get-tuple-element.182), channel_id=1, source_target_pairs={{0,1},{1,2},{2,3},{3,4},{4,5},{5,6},{6,7},{7,8},{8,9},{9,10},{10,1... | collective-permute-start | bytes 49160 | tf_op jit(solution)/shard_map/ppermute | solution.py:51
  130.5 4.0 %collective-permute-start.5 = (bf16[64,128]{1,0:T(8,128)(2,1)S(1)}, bf16[64,128]{1,0:T(8,128)(2,1)S(1)}, u32[]{:S(2)}, u32[]{:S(2)}) collective-permute-start(bf16[64,128]{1,0:T(8,128)(2,1)S(1)} %get-tuple-element.183), channel_id=1, source_target_pairs={{1,0},{2,1},{3,2},{4,3},{5,4},{6,5},{7,6},{8,7},{9,8},{10,9},{11,1... | collective-permute-start | bytes 49160 | tf_op jit(solution)/shard_map/ppermute | solution.py:51
  134.8 0.6 collective-permute-done.5.down
  135.4 1.7 %shard_map.143 = (bf16[32,2048]{1,0:T(8,128)(2,1)S(1)}, bf16[32,2048]{1,0:T(8,128)(2,1)S(1)}, bf16[64,128]{1,0:T(8,128)(2,1)S(1)}, bf16[64,128]{1,0:T(8,128)(2,1)S(1)}, f32[32,2048]{1,0:T(8,128)S(1)}) custom-call(s32[64]{0:T(128)S(1)} %copy-done.18, bf16[64,128,128]{2,1,0:T(8,128)(2,1)S(1)} %bitcast.58, bf16[32,2048]{1,0:T(8,128)(2,1)S(1)} %get-tuple-element.180.f.merged, ...), custom_call_target="tpu_custom_call" | custom-call | flops 134217728 | bytes 2523392 | tf_op jit(solution)/shard_map/pallas_call | solution.py:25
  137.1 2.8 %collective-permute-start.6 = (bf16[64,128]{1,0:T(8,128)(2,1)S(1)}, bf16[64,128]{1,0:T(8,128)(2,1)S(1)}, u32[]{:S(2)}, u32[]{:S(2)}) collective-permute-start(bf16[64,128]{1,0:T(8,128)(2,1)S(1)} %get-tuple-element.187), channel_id=1, source_target_pairs={{0,1},{1,2},{2,3},{3,4},{4,5},{5,6},{6,7},{7,8},{8,9},{9,10},{10,1... | collective-permute-start | bytes 49160 | tf_op jit(solution)/shard_map/ppermute | solution.py:51
  139.9 4.6 %collective-permute-start.7 = (bf16[64,128]{1,0:T(8,128)(2,1)S(1)}, bf16[64,128]{1,0:T(8,128)(2,1)S(1)}, u32[]{:S(2)}, u32[]{:S(2)}) collective-permute-start(bf16[64,128]{1,0:T(8,128)(2,1)S(1)} %get-tuple-element.188), channel_id=1, source_target_pairs={{1,0},{2,1},{3,2},{4,3},{5,4},{6,5},{7,6},{8,7},{9,8},{10,9},{11,1... | collective-permute-start | bytes 49160 | tf_op jit(solution)/shard_map/ppermute | solution.py:51
  144.5 0.6 broadcast_in_dim.21
  145.1 6.4 %all-to-all-start.7 = ((f32[16,4,128]{2,1,0:T(4,128)}), f32[16,4,128]{2,1,0:T(4,128)S(1)}, u32[]{:S(2)}, u32[]{:S(2)}) async-start(f32[16,4,128]{2,1,0:T(4,128)} %broadcast_in_dim.21), calls=%async_computation.7 | async-start | bytes 65536 | tf_op jit(solution)/shard_map/all_to_all | solution.py:410
  151.7 1.9 %shard_map.144 = (bf16[32,2048]{1,0:T(8,128)(2,1)}, bf16[32,2048]{1,0:T(8,128)(2,1)}) custom-call(s32[64]{0:T(128)S(1)} %copy-done.18, bf16[64,128,128]{2,1,0:T(8,128)(2,1)S(1)} %bitcast.59, bf16[32,2048]{1,0:T(8,128)(2,1)S(1)} %get-tuple-element.180.f.merged, bf16[32,2048]{1,0:T(8,128)(2,1)S(1)} %get-tuple-element.181.g.pre_grad, ...), custom_call_target="tpu_custom_call" | custom-call | flops 134217728 | bytes 2928896 | tf_op jit(solution)/shard_map/pallas_call | solution.py:25
  153.6 5.3 %all-to-all-done.7 = f32[16,4,128]{2,1,0:T(4,128)S(1)} async-done(((f32[16,4,128]{2,1,0:T(4,128)}), f32[16,4,128]{2,1,0:T(4,128)S(1)}, u32[]{:S(2)}, u32[]{:S(2)}) %all-to-all-start.7) | async-done | bytes 32800 | tf_op jit(solution)/shard_map/all_to_all | solution.py:410
  159.0 0.1 reshape.34
  159.2 0.6 copy.85
  159.9 0.7 copy.86
  (78 shorter events, 1.4 us)
Async XLA Ops:
  0.6 13.6 %copy-start.30 = (bf16[3,32,32]{2,1,0:T(8,128)(2,1)S(1)}, bf16[3,32,32]{2,1,0:T(8,128)(2,1)}, u32[]{:S(2)}) copy-start(bf16[3,32,32]{2,1,0:T(8,128)(2,1)} %param.23) | copy-start | bytes 18436
  1.5 23.9 %copy-start.16 = (s32[64]{0:T(128)}, s32[64]{0:T(128)S(1)}, u32[]{:S(2)}) copy-start(s32[64]{0:T(128)S(1)} %reshape_squeeze.9.cols) | copy-start | bytes 772
  1.5 1.6 copy-start
  3.1 0.9 copy-start.2
  4.0 0.9 copy-start.4
  4.9 9.9 %copy-start.31 = (bf16[3,32,32]{2,1,0:T(8,128)(2,1)S(1)}, bf16[3,32,32]{2,1,0:T(8,128)(2,1)}, u32[]{:S(2)}) copy-start(bf16[3,32,32]{2,1,0:T(8,128)(2,1)} %param.25) | copy-start | bytes 18436
  4.9 10.5 %copy-start.32 = (f32[2,32]{1,0:T(2,128)S(1)}, f32[2,32]{1,0:T(2,128)}, u32[]{:S(2)}) copy-start(f32[2,32]{1,0:T(2,128)} %param.26) | copy-start | bytes 772
  4.9 10.8 %copy-start.1 = (bf16[1,16,4,128,128]{4,3,2,1,0:T(8,128)(2,1)S(1)}, bf16[1,16,4,128,128]{4,3,2,1,0:T(8,128)(2,1)}, u32[]{:S(2)}) copy-start(bf16[1,16,4,128,128]{4,3,2,1,0:T(8,128)(2,1)} %param.18) | copy-start | bytes 6291460
  4.9 10.8 %copy-start.3 = (bf16[1,32,2048]{2,1,0:T(8,128)(2,1)S(1)}, bf16[1,32,2048]{2,1,0:T(8,128)(2,1)}, u32[]{:S(2)}) copy-start(bf16[1,32,2048]{2,1,0:T(8,128)(2,1)} %param.17) | copy-start | bytes 393220
  4.9 19.5 %copy-start.19 = (s32[1,2048,1]{1,2,0:T(1,128)S(1)}, s32[1,2048,1]{1,2,0:T(1,128)}, u32[]{:S(2)}) copy-start(s32[1,2048,1]{1,2,0:T(1,128)} %param.20) | copy-start | bytes 24580
  4.9 19.5 %copy-start.20 = (s32[1,2048]{1,0:T(1,128)S(1)}, s32[1,2048]{1,0:T(1,128)}, u32[]{:S(2)}) copy-start(s32[1,2048]{1,0:T(1,128)} %slot.3) | copy-start | bytes 24580
  6.3 19.0 %copy-start.5 = (bf16[1,32,2048]{2,1,0:T(8,128)(2,1)S(1)}, bf16[1,32,2048]{2,1,0:T(8,128)(2,1)}, u32[]{:S(2)}) copy-start(bf16[1,32,2048]{2,1,0:T(8,128)(2,1)} %param.27) | copy-start | bytes 393220
  6.4 19.0 %copy-start.14 = (f32[1,2048]{1,0:T(1,128)S(1)}, f32[1,2048]{1,0:T(1,128)}, u32[]{:S(2)}) copy-start(f32[1,2048]{1,0:T(1,128)} %pool.3) | copy-start | bytes 24580
  6.4 9.3 %collective-permute-start = (bf16[64,128]{1,0:T(8,128)(2,1)S(1)}, bf16[64,128]{1,0:T(8,128)(2,1)S(1)}, u32[]{:S(2)}, u32[]{:S(2)}) collective-permute-start(bf16[64,128]{1,0:T(8,128)(2,1)S(1)} %get-tuple-element.163), channel_id=1, source_target_pairs={{0,1},{1,2},{2,3},{3,4},{4,5},{5,6},{6,7},{7,8},{8,9},{9,10},{10,1... | collective-permute-start | bytes 49160 | tf_op jit(solution)/shard_map/ppermute | solution.py:51
  10.4 5.3 %collective-permute-start.1 = (bf16[64,128]{1,0:T(8,128)(2,1)S(1)}, bf16[64,128]{1,0:T(8,128)(2,1)S(1)}, u32[]{:S(2)}, u32[]{:S(2)}) collective-permute-start(bf16[64,128]{1,0:T(8,128)(2,1)S(1)} %get-tuple-element.164), channel_id=1, source_target_pairs={{1,0},{2,1},{3,2},{4,3},{5,4},{6,5},{7,6},{8,7},{9,8},{10,9},{11,1... | collective-permute-start | bytes 49160 | tf_op jit(solution)/shard_map/ppermute | solution.py:51
  17.5 7.9 %collective-permute-start.2 = (bf16[64,128]{1,0:T(8,128)(2,1)S(1)}, bf16[64,128]{1,0:T(8,128)(2,1)S(1)}, u32[]{:S(2)}, u32[]{:S(2)}) collective-permute-start(bf16[64,128]{1,0:T(8,128)(2,1)S(1)} %get-tuple-element.168), channel_id=1, source_target_pairs={{0,1},{1,2},{2,3},{3,4},{4,5},{5,6},{6,7},{7,8},{8,9},{9,10},{10,1... | collective-permute-start | bytes 49160 | tf_op jit(solution)/shard_map/ppermute | solution.py:51
  19.8 5.6 %collective-permute-start.3 = (bf16[64,128]{1,0:T(8,128)(2,1)S(1)}, bf16[64,128]{1,0:T(8,128)(2,1)S(1)}, u32[]{:S(2)}, u32[]{:S(2)}) collective-permute-start(bf16[64,128]{1,0:T(8,128)(2,1)S(1)} %get-tuple-element.169), channel_id=1, source_target_pairs={{1,0},{2,1},{3,2},{4,3},{5,4},{6,5},{7,6},{8,7},{9,8},{10,9},{11,1... | collective-permute-start | bytes 49160 | tf_op jit(solution)/shard_map/ppermute | solution.py:51
  25.4 22.9 %copy-start.21 = (bf16[32,32]{1,0:T(8,128)(2,1)S(1)}, bf16[32,32]{1,0:T(8,128)(2,1)}, u32[]{:S(2)}) copy-start(bf16[32,32]{1,0:T(8,128)(2,1)} %param.24) | copy-start | bytes 6148
  29.1 0.7 copy-start.6
  29.8 0.7 copy-start.8
  30.5 0.7 copy-start.10
  31.1 0.7 copy-start.12
  31.8 36.3 %all-to-all-start.4 = ((bf16[64,40,128]{2,1,0:T(8,128)(2,1)}), bf16[64,40,128]{2,1,0:T(8,128)(2,1)S(1)}, u32[]{:S(2)}, u32[]{:S(2)}) async-start(bf16[64,40,128]{2,1,0:T(8,128)(2,1)} %get-tuple-element.174), calls=%async_computation.4 | async-start | bytes 1310720 | tf_op jit(solution)/shard_map/all_to_all | solution.py:424
  101.8 0.9 copy-start.7
  102.7 0.9 copy-start.11
  103.6 0.9 copy-start.13
  104.5 0.7 copy-start.15
  105.2 0.7 copy-start.17
  105.9 1.9 %copy-start.9 = (bf16[32,2048]{1,0:T(8,128)(2,1)S(1)}, bf16[32,2048]{1,0:T(8,128)(2,1)}, u32[]{:S(2)}) copy-start(bf16[32,2048]{1,0:T(8,128)(2,1)} %copy-done.8) | copy-start | bytes 393220
  105.9 28.6 %copy-start.26 = (bf16[1,32,32]{2,1,0:T(8,128)(2,1)S(1)}, bf16[1,32,32]{2,1,0:T(8,128)(2,1)}, u32[]{:S(2)}) copy-start(bf16[1,32,32]{2,1,0:T(8,128)(2,1)} %get-tuple-element.313) | copy-start | bytes 6148
  105.9 28.7 %copy-start.25 = (bf16[1,32,32]{2,1,0:T(8,128)(2,1)S(1)}, bf16[1,32,32]{2,1,0:T(8,128)(2,1)}, u32[]{:S(2)}) copy-start(bf16[1,32,32]{2,1,0:T(8,128)(2,1)} %get-tuple-element.317) | copy-start | bytes 6148
  105.9 28.8 %copy-start.24 = (bf16[1,32,32]{2,1,0:T(8,128)(2,1)S(1)}, bf16[1,32,32]{2,1,0:T(8,128)(2,1)}, u32[]{:S(2)}) copy-start(bf16[1,32,32]{2,1,0:T(8,128)(2,1)} %get-tuple-element.318) | copy-start | bytes 6148
  105.9 29.5 %copy-start.18 = (s32[64]{0:T(128)S(1)}, s32[64]{0:T(128)}, u32[]{:S(2)}) copy-start(s32[64]{0:T(128)} %copy-done.16) | copy-start | bytes 772
  107.8 43.8 %copy-start.27 = (bf16[32,32]{1,0:T(8,128)(2,1)S(1)}, bf16[32,32]{1,0:T(8,128)(2,1)}, u32[]{:S(2)}) copy-start(bf16[32,32]{1,0:T(8,128)(2,1)} %get-tuple-element.319) | copy-start | bytes 6148
  107.8 43.8 %copy-start.28 = (bf16[32,32]{1,0:T(8,128)(2,1)S(1)}, bf16[32,32]{1,0:T(8,128)(2,1)}, u32[]{:S(2)}) copy-start(bf16[32,32]{1,0:T(8,128)(2,1)} %get-tuple-element.323) | copy-start | bytes 6148
  107.8 43.8 %copy-start.29 = (bf16[32,32]{1,0:T(8,128)(2,1)S(1)}, bf16[32,32]{1,0:T(8,128)(2,1)}, u32[]{:S(2)}) copy-start(bf16[32,32]{1,0:T(8,128)(2,1)} %get-tuple-element.324) | copy-start | bytes 6148
  121.8 22.7 %all-to-all-start.6 = ((f32[16,4,128]{2,1,0:T(4,128)}), f32[16,4,128]{2,1,0:T(4,128)S(1)}, u32[]{:S(2)}, u32[]{:S(2)}) async-start(f32[16,4,128]{2,1,0:T(4,128)} %broadcast_in_dim.20), calls=%async_computation.6 | async-start | bytes 65536 | tf_op jit(solution)/shard_map/all_to_all | solution.py:410
  127.3 7.5 %collective-permute-start.4 = (bf16[64,128]{1,0:T(8,128)(2,1)S(1)}, bf16[64,128]{1,0:T(8,128)(2,1)S(1)}, u32[]{:S(2)}, u32[]{:S(2)}) collective-permute-start(bf16[64,128]{1,0:T(8,128)(2,1)S(1)} %get-tuple-element.182), channel_id=1, source_target_pairs={{0,1},{1,2},{2,3},{3,4},{4,5},{5,6},{6,7},{7,8},{8,9},{9,10},{10,1... | collective-permute-start | bytes 49160 | tf_op jit(solution)/shard_map/ppermute | solution.py:51
  130.5 4.8 %collective-permute-start.5 = (bf16[64,128]{1,0:T(8,128)(2,1)S(1)}, bf16[64,128]{1,0:T(8,128)(2,1)S(1)}, u32[]{:S(2)}, u32[]{:S(2)}) collective-permute-start(bf16[64,128]{1,0:T(8,128)(2,1)S(1)} %get-tuple-element.183), channel_id=1, source_target_pairs={{1,0},{2,1},{3,2},{4,3},{5,4},{6,5},{7,6},{8,7},{9,8},{10,9},{11,1... | collective-permute-start | bytes 49160 | tf_op jit(solution)/shard_map/ppermute | solution.py:51
  137.1 14.6 %collective-permute-start.6 = (bf16[64,128]{1,0:T(8,128)(2,1)S(1)}, bf16[64,128]{1,0:T(8,128)(2,1)S(1)}, u32[]{:S(2)}, u32[]{:S(2)}) collective-permute-start(bf16[64,128]{1,0:T(8,128)(2,1)S(1)} %get-tuple-element.187), channel_id=1, source_target_pairs={{0,1},{1,2},{2,3},{3,4},{4,5},{5,6},{6,7},{7,8},{8,9},{9,10},{10,1... | collective-permute-start | bytes 49160 | tf_op jit(solution)/shard_map/ppermute | solution.py:51
  139.9 11.8 %collective-permute-start.7 = (bf16[64,128]{1,0:T(8,128)(2,1)S(1)}, bf16[64,128]{1,0:T(8,128)(2,1)S(1)}, u32[]{:S(2)}, u32[]{:S(2)}) collective-permute-start(bf16[64,128]{1,0:T(8,128)(2,1)S(1)} %get-tuple-element.188), channel_id=1, source_target_pairs={{1,0},{2,1},{3,2},{4,3},{5,4},{6,5},{7,6},{8,7},{9,8},{10,9},{11,1... | collective-permute-start | bytes 49160 | tf_op jit(solution)/shard_map/ppermute | solution.py:51
  145.1 13.8 %all-to-all-start.7 = ((f32[16,4,128]{2,1,0:T(4,128)}), f32[16,4,128]{2,1,0:T(4,128)S(1)}, u32[]{:S(2)}, u32[]{:S(2)}) async-start(f32[16,4,128]{2,1,0:T(4,128)} %broadcast_in_dim.21), calls=%async_computation.7 | async-start | bytes 65536 | tf_op jit(solution)/shard_map/all_to_all | solution.py:410

commit v3 on v2

v3 whole, which is shorter than its diff:
```python
import functools
import math

import jax
import jax.numpy as jnp
from jax import lax
from jax.experimental import pallas as pl
from jax.experimental.pallas import tpu as pltpu
from jax.sharding import PartitionSpec as P


LINE = ("region", "sub")
BF = jnp.bfloat16
F32 = jnp.float32
I32 = jnp.int32
LANES = 128
AUX = 8
PAD = 16
START_LIMIT = 59

VM = pl.BlockSpec(memory_space=pltpu.VMEM)
SM = pl.BlockSpec(memory_space=pltpu.SMEM)
HB = pl.BlockSpec(memory_space=pltpu.HBM)


def call(body, outs, scratch, args, smem=0, flops=0, limit=24, far=(), far_out=()):
    specs = [SM] * smem + [VM] * (len(args) - smem)
    for i in far:
        specs[i] = HB
    moved = sum(a.size * a.dtype.itemsize for a in args)
    return pl.pallas_call(
        body,
        out_shape=tuple(jax.ShapeDtypeStruct(s, d) for s, d in outs),
        in_specs=specs,
        out_specs=tuple(HB if i in far_out else VM for i in range(len(outs))),
        scratch_shapes=scratch,
        cost_estimate=pl.CostEstimate(flops=flops, bytes_accessed=moved, transcendentals=0),
        compiler_params=pltpu.CompilerParams(vmem_limit_bytes=limit << 20),
    )(*args)


def dot(a, b):
    return jnp.dot(a, b, preferred_element_type=F32)


def dot_nt(a, b):
    return lax.dot_general(a, b, (((1,), (1,)), ((), ())), preferred_element_type=F32)


def lanes(k):
    if isinstance(k, int):
        return slice(k * LANES, (k + 1) * LANES)
    return pl.ds(pl.multiple_of(k * LANES, LANES), LANES)


def tile(ref, k):
    return ref[:, lanes(k)]


def each(count, one, compact):
    if not compact:
        for k in range(count):
            one(k)
        return

    def body(k, carry):
        one(k)
        return carry

    lax.fori_loop(0, count, body, 0)


def shifted(value, by):
    peers = lax.axis_size(LINE)
    pairs = [(i, i + by) for i in range(peers) if 0 <= i + by < peers]
    return lax.ppermute(value, LINE, pairs)


def fetched(tiles_h, tiles, sems, count, nonzero, compact):
    pieces = 4 if count % 4 == 0 else 1
    size = count // pieces
    copies = []
    for i in range(pieces):
        at = slice(i * size * nonzero, (i + 1) * size * nonzero)
        copies.append(pltpu.make_async_copy(tiles_h.at[at], tiles.at[at], sems.at[i]))
        copies[-1].start()

    if compact:
        for c in copies:
            c.wait()

    def ready(k):
        if not compact and k % size == 0:
            copies[k // size].wait()

    return ready


def add_transposed(cols, tiles, grad_of, ext, count, nonzero, compact):
    ext[...] = jnp.zeros_like(ext)

    def one(k):
        y = dot_nt(grad_of(k), row_tiles(tiles, k, nonzero))
        for n in range(nonzero):
            ext[cols[k, n]] += y[:, n * LANES : (n + 1) * LANES]

    each(count, one, compact)


def row_tiles(tiles, k, nonzero):
    return tiles[pl.ds(k * nonzero, nonzero)].reshape(nonzero * LANES, LANES)


def row_product(cols, tiles, blocks, k, nonzero):
    picked = [blocks[cols[k, n]] for n in range(nonzero)]
    return dot(jnp.concatenate(picked, axis=1), row_tiles(tiles, k, nonzero))


def fill_blocks(blocks, field, up, down, chans, count, compact):
    blocks[0] = up[0:chans, :]
    blocks[count + 1] = down[0:chans, :]

    def one(k):
        blocks[k + 1] = tile(field, k)

    each(count, one, compact)


def write_sends(up, down, first, last, ext, chans, count):
    up[0:chans, :] = last
    up[chans : 2 * chans, :] = ext[count + 1].astype(BF)
    down[0:chans, :] = first
    down[chans : 2 * chans, :] = ext[0].astype(BF)


def inner_tile(inner, up, down, k, chans, count):
    value = tile(inner, k)
    if not isinstance(k, int):
        first = jnp.where(k == 0, 1.0, 0.0)
        last = jnp.where(k == count - 1, 1.0, 0.0)
        value = value + first * up[chans : 2 * chans, :].astype(F32)
        return value + last * down[chans : 2 * chans, :].astype(F32)
    if k == 0:
        value = value + up[chans : 2 * chans, :].astype(F32)
    if k == count - 1:
        value = value + down[chans : 2 * chans, :].astype(F32)
    return value


def start_body(
    cols, tiles_h, f_h, g_h, up, down, inner, ext, tiles, edge, g, sems, *, chans, count, nonzero, compact
):
    last = slice((count - 1) * LANES, count * LANES)
    copies = [
        pltpu.make_async_copy(g_h, g, sems.at[4]),
        pltpu.make_async_copy(f_h.at[:, 0:LANES], edge.at[0], sems.at[5]),
        pltpu.make_async_copy(f_h.at[:, last], edge.at[1], sems.at[6]),
    ]
    copies[0].start()
    ready = fetched(tiles_h, tiles, sems, count, nonzero, compact)
    copies[1].start()
    copies[2].start()
    copies[0].wait()

    def grad_of(k):
        ready(k)
        return tile(g, k)

    add_transposed(cols, tiles, grad_of, ext, count, nonzero, compact)
    copies[1].wait()
    copies[2].wait()
    write_sends(up, down, edge[0], edge[1], ext, chans, count)

    def one(k):
        inner[:, lanes(k)] = ext[k + 1]

    each(count, one, compact)


def middle_body(
    cols, tiles_h, f, up, down, inner, f1, g1, up2, down2, inner2, blocks, ext, tiles, sems,
    *, chans, count, nonzero, compact
):
    ready = fetched(tiles_h, tiles, sems, count, nonzero, compact)
    fill_blocks(blocks, f, up, down, chans, count, compact)

    def one(k):
        g1[:, lanes(k)] = inner_tile(inner, up, down, k, chans, count).astype(BF)

    each(count, one, compact)

    def one(k):
        ready(k)
        f1[:, lanes(k)] = row_product(cols, tiles, blocks, k, nonzero).astype(BF)

    each(count, one, compact)
    add_transposed(cols, tiles, lambda k: tile(g1, k), ext, count, nonzero, compact)
    write_sends(up2, down2, tile(f1, 0), tile(f1, count - 1), ext, chans, count)

    def one(k):
        inner2[:, lanes(k)] = ext[k + 1]

    each(count, one, compact)


def second_terms(
    cols, tiles, f, g, f1, up, down, inner, blocks, f2, g2, chans, count, nonzero, ready, compact
):
    fill_blocks(blocks, f1, up, down, chans, count, compact)

    def one(k):
        ready(k)
        at = lanes(k)
        y = row_product(cols, tiles, blocks, k, nonzero)
        f2[:, at] = (2.0 * y - f[:, at].astype(F32)).astype(BF)
        z = inner_tile(inner, up, down, k, chans, count)
        g2[:, at] = (2.0 * z - g[:, at].astype(F32)).astype(BF)

    each(count, one, compact)


def place_body(owner, slot, dest, rank, most, *, peers, rows):
    d = owner[...] + slot[...]
    d = d - (d // peers) * peers
    dest[...] = d
    hot = lax.broadcasted_iota(I32, (peers, rows), 0) == d
    hot = jnp.where(hot, 1.0, 0.0).astype(F32)
    a = lax.broadcasted_iota(I32, (LANES, LANES), 0)
    b = lax.broadcasted_iota(I32, (LANES, LANES), 1)
    before = jnp.where(a < b, 1.0, 0.0).astype(BF)
    carry = jnp.zeros((peers, 1), F32)
    for k in range(rows // LANES):
        h = hot[:, k * LANES : (k + 1) * LANES]
        c = dot(h.astype(BF), before) + carry
        rank[:, k * LANES : (k + 1) * LANES] = jnp.sum(h * c, axis=0, keepdims=True).astype(I32)
        carry = carry + jnp.sum(h, axis=1, keepdims=True)
    most[...] = jnp.broadcast_to(jnp.max(carry, axis=0, keepdims=True), (AUX, LANES))


def slot_hot(dest, rank, step, cap, go, rows):
    at = rank - step * cap
    inside = (at >= 0) & (at < cap)
    col = jnp.where(inside, (dest - (dest // go) * go) * cap + at, -1)
    hot = lax.broadcasted_iota(I32, (go * cap, rows), 0) == col
    return jnp.where(hot, 1.0, 0.0).astype(BF)


def merge_halves(low, high, odd, cap):
    if cap == LANES // 2:
        left = lax.broadcasted_iota(I32, low.shape, 1) < cap
        if odd:
            return jnp.where(left, pltpu.roll(low, cap, 1), high)
        return jnp.where(left, low, pltpu.roll(high, cap, 1))
    at = slice(cap, 2 * cap) if odd else slice(0, cap)
    return jnp.concatenate([low[:, at], high[:, at]], axis=1)


def pack_into(
    buffer, big, out, sent, dest, rank, most, step, *, chans, peers, cap, go, rows
):
    high = 2 * chans + PAD
    group = dest // go

    def mask(g, carry):
        here = jnp.where(group == g, 1.0, 0.0).astype(BF)
        big[pl.ds(pl.multiple_of(g * high, high), high), :] = sent[...] * here
        return carry

    lax.fori_loop(0, peers // go, mask, 0, unroll=2)
    out[...] = dot_nt(big[...], slot_hot(dest, rank, step, cap, go, rows))
    row = lax.broadcasted_iota(I32, (AUX, 2 * cap), 0)
    lane = lax.broadcasted_iota(I32, (AUX, 2 * cap), 1)
    extra = jnp.where((row == 1) & (lane >= cap), float(LANES), 0.0)
    extra = extra + jnp.where(row == 2, most, 0.0)

    def place(g, carry):
        part = out[pl.ds(pl.multiple_of(g * high, high), high), :]
        for o in range(go):
            pair = o // 2 * 2 * cap
            near = jnp.concatenate([part] * 2, axis=1) if go == 1 else part[:, pair : pair + 2 * cap]
            odd = o % 2 == 1
            p = g * go + o
            body = merge_halves(near[0:chans], near[chans : 2 * chans], odd, cap)
            buffer[p, 0:chans, :] = body.astype(BF)
            aux = near[2 * chans : 2 * chans + AUX]
            buffer[p, chans : chans + AUX, :] = (merge_halves(aux, aux, odd, cap) + extra).astype(BF)
        return carry

    lax.fori_loop(0, peers // go, place, 0, unroll=2)


def pack_body(step, sent, dest, rank, most, buffer, big, out, *, cap, **sizes):
    needed = jnp.ceil(most[0:1, 0:1] * (1.0 / cap))
    pack_into(buffer, big, out, sent, dest[...], rank[...], needed, step[0], cap=cap, **sizes)


def unpack_body(step, back, dest, rank, lifted, big, hot, *, chans, peers, cap, go, rows):
    hot[...] = slot_hot(dest[...], rank[...], step[0], cap, go, rows)
    high = 2 * chans

    def gather(g, carry):
        rows_low = pl.ds(pl.multiple_of(g * high, high), chans)
        rows_top = pl.ds(pl.multiple_of(g * high + chans, chans), chans)
        for o in range(0, go, 2):
            a = back[g * go + o].astype(F32)
            if go == 1:
                low, top = a[:, 0:cap], a[:, cap : 2 * cap]
                at = slice(0, cap)
            else:
                b = back[g * go + o + 1].astype(F32)
                at = slice(o * cap, (o + 2) * cap)
                if cap == LANES // 2:
                    low, top = merge_halves(a, b, False, cap), merge_halves(a, b, True, cap)
                else:
                    low = jnp.concatenate([a[:, 0:cap], b[:, 0:cap]], axis=1)
                    top = jnp.concatenate([a[:, cap:], b[:, cap:]], axis=1)
            big[rows_low, at] = low.astype(BF)
            big[rows_top, at] = top.astype(BF)
        return carry

    lax.fori_loop(0, peers // go, gather, 0, unroll=2)
    width = min(256, rows)

    def select(w, carry):
        at = pl.ds(pl.multiple_of(w * width, width), width)
        y = dot(big[...], hot[:, at])
        group = dest[:, at] // go
        total = jnp.zeros((high, width), F32)
        for g in range(peers // go):
            total = jnp.where(group == g, y[g * high : (g + 1) * high], total)
        lifted[:, at] = total.astype(BF)
        return carry

    lax.fori_loop(0, rows // width, select, 0)


def coarse_hot(got, hot, masked, *, chans, peers, cap, parts):
    wide = 2 * cap

    def one(p, carry):
        aux = got[p, chans : chans + AUX, :].astype(F32)
        at = pl.ds(pl.multiple_of(p * wide, wide), wide)
        code = aux[1:2, :].astype(I32)
        q = lax.broadcasted_iota(I32, (2 * LANES, wide), 0)
        hot[:, at] = jnp.where(q == code, 1.0, 0.0).astype(BF)
        if masked is not None:
            body = got[p, 0:chans, :].astype(F32)
            for h in range(parts):
                masked[h * chans : (h + 1) * chans, at] = jnp.where(
                    aux[0:1, :] == h + 1.0, body, 0.0
                ).astype(BF)
        return carry

    lax.fori_loop(0, peers, one, 0, unroll=4)


def coarse_totals(hot, masked, chans, parts):
    acc = dot_nt(masked[...], hot[...])
    split = [acc[h * chans : (h + 1) * chans] for h in range(parts)]
    low = jnp.concatenate([s[:, 0:LANES] for s in split], axis=1)
    top = jnp.concatenate([s[:, LANES:] for s in split], axis=1)
    return low, top


def slope(value):
    sig = jax.nn.sigmoid(value)
    return sig * (1.0 + value * (1.0 - sig))


def coarse_math(coarse_sum, coarse_grad, weight, weight_t, bias, grads):
    coarse = coarse_sum.astype(BF)
    pre = dot(weight[...], coarse) + bias[...]
    out = (pre * jax.nn.sigmoid(pre)).astype(BF)
    mid_grad = (coarse_grad * slope(pre)).astype(BF)
    chans = pre.shape[0]
    grads[0:chans, :] = dot_nt(mid_grad, coarse)
    ones = jnp.ones((chans, mid_grad.shape[1]), BF)
    grads[chans : 2 * chans, :] = dot_nt(ones, mid_grad)
    return out, dot(weight_t[...], mid_grad).astype(BF)


def coarse_gather(back, got, hot, out, behind, *, chans, peers, cap, parts):
    wide = 2 * cap
    stacked = [
        jnp.concatenate(
            [out[:, h * LANES : (h + 1) * LANES], behind[:, h * LANES : (h + 1) * LANES]], axis=1
        )
        for h in range(parts)
    ]
    stacked = jnp.concatenate(stacked, axis=0)
    step = max(1, 512 // wide)

    def one(b, carry):
        at = pl.ds(pl.multiple_of(b * step * wide, step * wide), step * wide)
        y = dot(stacked, hot[:, at])
        for j in range(step):
            p = b * step + j
            part = got[p, chans : chans + AUX, :].astype(F32)[0:1, :]
            total = jnp.zeros((chans, wide), F32)
            for h in range(parts):
                total = jnp.where(
                    part == h + 1.0,
                    y[h * chans : (h + 1) * chans, j * wide : (j + 1) * wide],
                    total,
                )
            back[p] = total.astype(BF)
        return carry

    lax.fori_loop(0, peers // step, one, 0, unroll=2)


def coarse_body(got, weight, weight_t, bias, back, grads, hot, masked, **sizes):
    coarse_hot(got, hot, masked, **sizes)
    low, top = coarse_totals(hot, masked, sizes["chans"], sizes["parts"])
    out, behind = coarse_math(low, top, weight, weight_t, bias, grads)
    coarse_gather(back, got, hot, out, behind, **sizes)


def totals_body(got, before, after, hot, masked, **sizes):
    chans = sizes["chans"]
    coarse_hot(got, hot, masked, **sizes)
    low, top = coarse_totals(hot, masked, chans, sizes["parts"])
    after[0:chans, :] = before[0:chans, :] + low
    after[chans : 2 * chans, :] = before[chans : 2 * chans, :] + top


def math_body(totals, weight, weight_t, bias, values, grads):
    chans = totals.shape[0] // 2
    out, behind = coarse_math(
        totals[0:chans, :], totals[chans : 2 * chans, :], weight, weight_t, bias, grads
    )
    values[0:chans, :] = out
    values[chans : 2 * chans, :] = behind


def gather_body(got, values, back, hot, **sizes):
    chans = sizes["chans"]
    coarse_hot(got, hot, None, **sizes)
    coarse_gather(
        back, got, hot, values[0:chans, :], values[chans : 2 * chans, :], **sizes
    )


def first_end_body(
    cols, tiles_h, f, g, f1, g1, up, down, inner, pool, mix_in, mix_out_t, bias,
    dest, rank, most, slot, owner,
    f2, g2, pre_in, hidden, merged_grad, sent, buffer, blocks, big, out, tiles, sems,
    *, chans, count, nonzero, compact, peers, cap, go, rows
):
    ready = fetched(tiles_h, tiles, sems, count, nonzero, compact)
    second_terms(
        cols, tiles, f, g, f1, up, down, inner, blocks, f2, g2, chans, count, nonzero, ready,
        compact,
    )

    def one(k):
        at = lanes(k)
        w = pool[:, at]
        pre = dot(mix_in[...], jnp.concatenate([f[:, at], f1[:, at], f2[:, at]], axis=0)) + bias[...]
        pre_in[:, at] = pre
        h = (pre * jax.nn.sigmoid(pre)).astype(BF)
        hidden[:, at] = h
        m = dot(mix_out_t[...], jnp.concatenate([g[:, at], g1[:, at], g2[:, at]], axis=0)).astype(BF)
        merged_grad[:, at] = m
        sent[0:chans, at] = (w * h.astype(F32)).astype(BF)
        sent[chans : 2 * chans, at] = (w * m.astype(F32)).astype(BF)

    each(count, one, compact)
    share = rows // 4 // peers
    index = owner[...] * share + slot[...] // peers
    part = index // LANES
    row = lax.broadcasted_iota(I32, (PAD, rows), 0)
    sent[2 * chans : 2 * chans + PAD, :] = (
        jnp.where(row == 0, part + 1, jnp.where(row == 1, index - part * LANES, 0))
        .astype(F32)
        .astype(BF)
    )
    needed = jnp.ceil(most[0:1, 0:1] * (1.0 / cap))
    pack_into(
        buffer, big, out, sent, dest[...], rank[...], needed, 0,
        chans=chans, peers=peers, cap=cap, go=go, rows=rows,
    )


def second_start_body(
    cols, tiles_h, lifted, hidden, merged_grad, pre_in, pool,
    merged, pre_grad, up, down, inner, ext, tiles, sems,
    *, chans, count, nonzero, compact
):
    ready = fetched(tiles_h, tiles, sems, count, nonzero, compact)

    def one(k):
        at = lanes(k)
        w = pool[:, at]
        merged[:, at] = (
            hidden[:, at].astype(F32) + w * lifted[0:chans, at].astype(F32)
        ).astype(BF)
        hidden_grad = merged_grad[:, at].astype(F32) + w * lifted[chans : 2 * chans, at].astype(F32)
        pre_grad[:, at] = (hidden_grad * slope(pre_in[:, at])).astype(BF)

    each(count, one, compact)

    def grad_of(k):
        ready(k)
        return tile(pre_grad, k)

    add_transposed(cols, tiles, grad_of, ext, count, nonzero, compact)
    write_sends(up, down, tile(merged, 0), tile(merged, count - 1), ext, chans, count)

    def one(k):
        inner[:, lanes(k)] = ext[k + 1]

    each(count, one, compact)


def weights_body(merged, pre_grad, f, f1, f2, g, g1, g2, mid, most, local, *, chans, cap):
    p, m = pre_grad[...], merged[...]
    gin = [dot_nt(p, t[...]) for t in (f, f1, f2)]
    gout = [dot_nt(t[...], m) for t in (g, g1, g2)]
    local[0:chans, :] = jnp.concatenate(gin + [mid[0:chans, :]], axis=1)
    total = dot_nt(jnp.ones(p.shape, BF), p)
    row = lax.broadcasted_iota(I32, (chans, chans), 0)
    sums = jnp.where(row == 0, total, mid[chans : 2 * chans, :])
    over = jnp.where(most[0:1, 0:1] > cap, 1.0, 0.0)
    sums = jnp.where(row == 2, over, sums)
    local[chans : 2 * chans, :] = jnp.concatenate(gout + [sums], axis=1)


def second_end_body(
    cols, tiles_h, f, g, f1, g1, up, down, inner, mix_out, mix_in_t,
    result, input_grad, f2, g2, blocks, tiles, sems,
    *, chans, count, nonzero, compact
):
    ready = fetched(tiles_h, tiles, sems, count, nonzero, compact)
    second_terms(
        cols, tiles, f, g, f1, up, down, inner, blocks, f2, g2, chans, count, nonzero, ready,
        compact,
    )

    def one(k):
        at = lanes(k)
        terms = jnp.concatenate([f[:, at], f1[:, at], f2[:, at]], axis=0)
        result[:, at] = dot(mix_out[...], terms).astype(BF)
        terms = jnp.concatenate([g[:, at], g1[:, at], g2[:, at]], axis=0)
        input_grad[:, at] = dot(mix_in_t[...], terms).astype(BF)

    each(count, one, compact)


def last_body(total, weights, biases, *, chans, factor):
    for k in range(7):
        low = k // 4 * chans
        at = slice(k % 4 * chans, (k % 4 + 1) * chans)
        weights[k] = total[low : low + chans, at] * factor
    biases[...] = total[chans : chans + 2, 3 * chans : 4 * chans] * factor


def spread(values, axes):
    peers = lax.axis_size(axes)
    return lax.all_to_all(
        jnp.broadcast_to(values[None], (peers, *values.shape)), axes, 0, 0, tiled=True
    )


def summed_everywhere(local):
    regions = lax.axis_size("region")
    parts = local.reshape(regions, -1, LANES)
    mine = lax.all_to_all(parts, "region", 0, 0, tiled=True)
    mine = jnp.sum(mine, axis=0)
    mine = spread(mine, ("geo", "sub"))
    mine = jnp.sum(mine, axis=0)
    return spread(mine, "region").reshape(local.shape)


def exchanged(buffer):
    return lax.all_to_all(buffer, LINE, 0, 0, tiled=True)


def on_device(*arrays):
    result, input_grad, weights, biases, over = level(*arrays, several=False)

    def again(carry):
        return (*level(*arrays, several=True)[:4], jnp.zeros_like(over))

    done = lax.while_loop(
        lambda carry: carry[4] > 0.5, again, (result, input_grad, weights, biases, over)
    )
    return done[0][None], done[1][None], done[2], done[3]


def level(
    features,
    lap_tiles,
    tile_cols,
    coarse_owner,
    coarse_slot,
    pool_weight,
    weight_in,
    weight_mid,
    weight_out,
    biases,
    out_grad,
    *,
    several,
):
    chans, rows = features.shape[1:]
    count, nonzero = lap_tiles.shape[1:3]
    peers = lax.axis_size(LINE)
    cap = 2 * rows // peers
    go = max(1, 256 // cap)
    coarse_rows = rows // 4
    parts = coarse_rows // LANES
    f, g = features[0], out_grad[0]
    tiles = lap_tiles[0].reshape(count * nonzero, LANES, LANES)
    cols = tile_cols[0]
    owner = coarse_owner[0].reshape(1, rows)
    slot = coarse_slot
    pool = pool_weight
    side = lambda w: jnp.concatenate([w[k] for k in range(3)], axis=1)
    side_t = lambda w: jnp.concatenate([w[k].T for k in range(3)], axis=1)
    line = dict(chans=chans, count=count, nonzero=nonzero, compact=several)
    ways = dict(chans=chans, peers=peers, cap=cap, go=go, rows=rows)
    sizes = dict(chans=chans, peers=peers, cap=cap, parts=parts)
    full = (chans, rows)
    halo = (2 * chans, LANES)
    ext = pltpu.VMEM((count + 2, chans, LANES), F32)
    blocks = pltpu.VMEM((count + 2, chans, LANES), BF)
    work = 2 * chans * rows * nonzero * LANES
    chunk = (peers, chans + AUX, 2 * cap)
    reply = (peers, chans, 2 * cap)
    hot_s = pltpu.VMEM((2 * LANES, peers * 2 * cap), BF)
    masked_s = pltpu.VMEM((parts * chans, peers * 2 * cap), BF)
    tall = peers // go * (2 * chans + PAD)
    pack_s = [pltpu.VMEM((tall, rows), BF), pltpu.VMEM((tall, go * cap), F32)]
    lift_s = [
        pltpu.VMEM((peers // go * 2 * chans, go * cap), BF),
        pltpu.VMEM((go * cap, rows), BF),
    ]
    store = [pltpu.VMEM(tiles.shape, BF), pltpu.SemaphoreType.DMA((4,))]
    bias_mid = biases[1][:, None]
    weight_mid_t = weight_mid.T

    def passed(up, down):
        up = shifted(up, 1)
        down = shifted(down, -1)
        return up, down

    def middle(field, up, down, inner):
        return call(
            functools.partial(middle_body, **line),
            [(full, BF), (full, BF), (halo, BF), (halo, BF), (full, F32)],
            [blocks, ext, *store],
            (cols, tiles, field, up, down, inner),
            smem=1,
            far=(1,),
            flops=2 * work,
        )

    up, down, inner = call(
        functools.partial(start_body, **line),
        [(halo, BF), (halo, BF), (full, F32)],
        [
            ext,
            pltpu.VMEM(tiles.shape, BF),
            pltpu.VMEM((2, chans, LANES), BF),
            pltpu.VMEM(full, BF),
            pltpu.SemaphoreType.DMA((7,)),
        ],
        (cols, tiles, f, g),
        smem=1,
        flops=work,
        far=(1, 2, 3),
        limit=START_LIMIT,
    )
    up, down = passed(up, down)
    dest, rank, most = call(
        functools.partial(place_body, peers=peers, rows=rows),
        [((1, rows), I32), ((1, rows), I32), ((AUX, LANES), F32)],
        [],
        (owner, slot),
        flops=2 * work,
    )
    f1, g1, up, down, inner = middle(f, up, down, inner)
    up, down = passed(up, down)
    f2, g2, pre_in, hidden, merged_grad, sent, buffer = call(
        functools.partial(first_end_body, **line, peers=peers, cap=cap, go=go, rows=rows),
        [
            (full, BF),
            (full, BF),
            (full, F32),
            (full, BF),
            (full, BF),
            ((2 * chans + PAD, rows), BF),
            (chunk, BF),
        ],
        [blocks, *pack_s, *store],
        (
            cols, tiles, f, g, f1, g1, up, down, inner, pool, side(weight_in), side_t(weight_out),
            biases[0][:, None], dest, rank, most, slot, owner,
        ),
        smem=1,
        flops=4 * work,
        limit=32,
        far=(1,),
    )
    got = exchanged(buffer)

    def unpacked(back, step):
        return call(
            functools.partial(unpack_body, **ways),
            [((2 * chans, rows), BF)],
            lift_s,
            (step, back, dest, rank),
            smem=1,
        )[0]

    def received(step):
        return exchanged(
            call(
                functools.partial(pack_body, **ways),
                [(chunk, BF)],
                pack_s,
                (step.reshape(1), sent, dest, rank, most),
                smem=1,
                limit=32,
            )[0]
        )

    def add(step, totals):
        return call(
            functools.partial(totals_body, **sizes),
            [((2 * chans, coarse_rows), F32)],
            [hot_s, masked_s],
            (received(step), totals),
            limit=32,
        )[0]

    if several:
        rounds = jnp.max(got[:, chans + 2, 0].astype(F32)).astype(I32)
        totals = lax.fori_loop(0, rounds, add, jnp.zeros((2 * chans, coarse_rows), F32))
        values, mid = call(
            math_body,
            [((2 * chans, coarse_rows), BF), ((2 * chans, chans), F32)],
            [],
            (totals, weight_mid, weight_mid_t, bias_mid),
        )

        def fetch(step, lifted):
            back = call(
                functools.partial(gather_body, **sizes),
                [(reply, BF)],
                [hot_s],
                (received(step), values),
                limit=32,
            )[0]
            return lifted + unpacked(exchanged(back), step.reshape(1))

        lifted = lax.fori_loop(0, rounds, fetch, jnp.zeros((2 * chans, rows), BF))
    else:
        back, mid = call(
            functools.partial(coarse_body, **sizes),
            [(reply, BF), ((2 * chans, chans), F32)],
            [hot_s, masked_s],
            (got, weight_mid, weight_mid_t, bias_mid),
            limit=32,
        )
        lifted = unpacked(exchanged(back), jnp.zeros((1,), I32))

    merged, pre_grad, up, down, inner = call(
        functools.partial(second_start_body, **line),
        [(full, BF), (full, BF), (halo, BF), (halo, BF), (full, F32)],
        [ext, *store],
        (cols, tiles, lifted, hidden, merged_grad, pre_in, pool),
        smem=1,
        far=(1,),
        flops=work,
    )
    up, down = passed(up, down)
    local = call(
        functools.partial(weights_body, chans=chans, cap=cap),
        [((2 * chans, LANES), F32)],
        [],
        (merged, pre_grad, f, f1, f2, g, g1, g2, mid, most),
        flops=work,
    )[0]
    m1, p1, up, down, inner = middle(merged, up, down, inner)
    up, down = passed(up, down)
    result, input_grad = call(
        functools.partial(second_end_body, **line),
        [(full, BF), (full, BF)],
        [pltpu.VMEM(full, BF), pltpu.VMEM(full, BF), blocks, *store],
        (
            cols, tiles, merged, pre_grad, m1, p1, up, down, inner,
            side(weight_out), side_t(weight_in),
        ),
        smem=1,
        flops=2 * work,
        far=(1,),
    )
    factor = 1.0 / math.sqrt(lax.axis_size("geo") * rows * peers)
    summed = summed_everywhere(local)
    sum_weights, sum_biases = call(
        functools.partial(last_body, chans=chans, factor=factor),
        [((7, chans, chans), F32), ((2, chans), F32)],
        [],
        (summed,),
    )
    return result, input_grad, sum_weights, sum_biases, summed[chans + 2, 3 * chans]


def solution(mesh):
    line = ("region", "sub")
    in_specs = (
        P("geo", None, line),
        P("geo", line, None, None, None),
        P("geo", line, None),
        P("geo", line, None),
        P("geo", line),
        P("geo", line),
        P(),
        P(),
        P(),
        P(),
        P("geo", None, line),
    )
    out_specs = (P("geo", None, line), P("geo", None, line), P(), P())
    return jax.shard_map(
        on_device, mesh=mesh, in_specs=in_specs, out_specs=out_specs, check_vma=False
    )
```

time: 162 us -> 161 us (level)
  Pallas kernels: 23.5 us -> 34.5 us
  local copies, waits for them, and re-layouts: 15.9 us -> 5.18 us
    pallas_call x10 -> x11, Pallas kernels: 23.5 us -> 34.5 us  [call(): pl.pallas_call(body, out_shape=tuple((jax.ShapeDtypeStruct(s, d) for s, d...]
    unnamed x68 -> x26, local copies, waits for them, and re-layouts: 12 us -> 1.18 us
  transfers between devices with their start and end apart: 11 -> 11, of which waited for: 3 -> 5; matrix products, arithmetic and copies ran while one was open for 2% -> 1% of each run, Pallas kernels for 3% -> 4%
where the time goes in v3:
time: 161 us; the launch traced here: 160 us
  starting transfers between devices  58.4 us (36%)
  blocking collectives  35.2 us (22%)
  Pallas kernels  34.5 us (21%)
  waiting for transfers between devices  25 us (16%)
  local copies, waits for them, and re-layouts  5.18 us (3%)
    pallas_call x11, Pallas kernels, call(): pl.pallas_call(body, out_shape=tuple((jax.ShapeDtypeStruct(s, d) for s, d...  34.5 us
    ppermute x8, starting transfers between devices, shifted(): return lax.ppermute(value, LINE, pairs)  29.7 us
    all_to_all x1, blocking collectives, exchanged(): return lax.all_to_all(buffer, LINE, 0, 0, tiled=True)  23.1 us
    all_to_all x1, waiting for transfers between devices, exchanged(): return lax.all_to_all(buffer, LINE, 0, 0, tiled=True)  19.6 us
    all_to_all x1, starting transfers between devices, exchanged(): return lax.all_to_all(buffer, LINE, 0, 0, tiled=True)  16.8 us
    all_to_all x1, blocking collectives, summed_everywhere(): mine = lax.all_to_all(parts, 'region', 0, 0, tiled=True)  12.1 us
    all_to_all x2, starting transfers between devices, spread(): lax.all_to_all(jnp.broadcast_to(values[None], (peers, *values.shape)), ax...  11.9 us
    all_to_all x2, waiting for transfers between devices, spread(): lax.all_to_all(jnp.broadcast_to(values[None], (peers, *values.shape)), ax...  3.77 us
  transfers between devices with their start and end apart: 11, of which 5 were waited for; matrix products, arithmetic and copies ran while one was open for 1% of the time, Pallas kernels for 4%

profile of v3, /device:TPU:1, one launch (start us, length us, event | category | flops | bytes accessed | tf_op | source)
XLA Modules:
  0.0 160.5 jit_solution(17171717719742474901)
XLA Ops:
  0.7 1.4 copy.145.cols
  2.1 4.0 %shard_map.138 = (bf16[64,128]{1,0:T(8,128)(2,1)}, bf16[64,128]{1,0:T(8,128)(2,1)}, f32[32,2048]{1,0:T(8,128)}) custom-call(s32[16,4]{1,0:T(8,128)} %copy.145.cols, bf16[64,128,128]{2,1,0:T(8,128)(2,1)} %bitcast.31.tiles_h, bf16[32,2048]{1,0:T(8,128)(2,1)} %bitcast.98, bf16[32,2048]{1,0:T(8,128)(2,1)} %bitcast.106), custom_call_target="tpu_custom_call" | custom-call | flops 67108864 | bytes 2359552 | tf_op jit(solution)/shard_map/pallas_call | solution.py:31
  6.1 0.0 copy-start.7
  6.1 4.1 %collective-permute-start.8 = (bf16[64,128]{1,0:T(8,128)(2,1)}, bf16[64,128]{1,0:T(8,128)(2,1)S(1)}, u32[]{:S(2)}, u32[]{:S(2)}) collective-permute-start(bf16[64,128]{1,0:T(8,128)(2,1)} %get-tuple-element.232), channel_id=1, source_target_pairs={{0,1},{1,2},{2,3},{3,4},{4,5},{5,6},{6,7},{7,8},{8,9},{9,10},{10,1... | collective-permute-start | bytes 49160 | tf_op jit(solution)/shard_map/ppermute | solution.py:76
  10.2 3.7 %collective-permute-start.9 = (bf16[64,128]{1,0:T(8,128)(2,1)}, bf16[64,128]{1,0:T(8,128)(2,1)S(1)}, u32[]{:S(2)}, u32[]{:S(2)}) collective-permute-start(bf16[64,128]{1,0:T(8,128)(2,1)} %get-tuple-element.233), channel_id=1, source_target_pairs={{1,0},{2,1},{3,2},{4,3},{5,4},{6,5},{7,6},{8,7},{9,8},{10,9},{11,1... | collective-permute-start | bytes 49160 | tf_op jit(solution)/shard_map/ppermute | solution.py:76
  13.9 0.1 copy.130
  14.1 0.1 copy.133
  14.2 0.1 copy.134
  14.3 0.1 copy.135
  14.4 0.1 copy.136
  14.4 0.1 copy.137
  14.5 0.1 copy.138
  14.6 0.4 collective-permute-done.9.down
  15.0 0.9 copy-done.3
  16.0 3.3 %shard_map.139 = (bf16[32,2048]{1,0:T(8,128)(2,1)S(1)}, bf16[32,2048]{1,0:T(8,128)(2,1)S(1)}, bf16[64,128]{1,0:T(8,128)(2,1)S(1)}, bf16[64,128]{1,0:T(8,128)(2,1)S(1)}, f32[32,2048]{1,0:T(8,128)S(1)}) custom-call(s32[16,4]{1,0:T(8,128)S(1)} %copy-done.2, bf16[64,128,128]{2,1,0:T(8,128)(2,1)} %bitcast.31.tiles_h, bf16[32,2048]{1,0:T(8,128)(2,1)S(1)} %bitcast.99, ...), custom_call_target="tpu_custom_call" | custom-call | flops 134217728 | bytes 2523392 | tf_op jit(solution)/shard_map/pallas_call | solution.py:31
  19.3 3.0 %collective-permute-start.10 = (bf16[64,128]{1,0:T(8,128)(2,1)S(1)}, bf16[64,128]{1,0:T(8,128)(2,1)S(1)}, u32[]{:S(2)}, u32[]{:S(2)}) collective-permute-start(bf16[64,128]{1,0:T(8,128)(2,1)S(1)} %get-tuple-element.237), channel_id=1, source_target_pairs={{0,1},{1,2},{2,3},{3,4},{4,5},{5,6},{6,7},{7,8},{8,9},{9,10},{10,1... | collective-permute-start | bytes 49160 | tf_op jit(solution)/shard_map/ppermute | solution.py:76
  22.3 4.3 %collective-permute-start.11 = (bf16[64,128]{1,0:T(8,128)(2,1)S(1)}, bf16[64,128]{1,0:T(8,128)(2,1)S(1)}, u32[]{:S(2)}, u32[]{:S(2)}) collective-permute-start(bf16[64,128]{1,0:T(8,128)(2,1)S(1)} %get-tuple-element.238), channel_id=1, source_target_pairs={{1,0},{2,1},{3,2},{4,3},{5,4},{6,5},{7,6},{8,7},{9,8},{10,9},{11,1... | collective-permute-start | bytes 49160 | tf_op jit(solution)/shard_map/ppermute | solution.py:76
  26.6 0.1 pad_maximum_fusion.4
  26.7 0.1 copy.140.bias
  26.8 0.3 shard_map.140
  27.1 0.4 collective-permute-done.11.down
  27.5 6.6 %shard_map.141 = (bf16[32,2048]{1,0:T(8,128)(2,1)S(1)}, bf16[32,2048]{1,0:T(8,128)(2,1)S(1)}, f32[32,2048]{1,0:T(8,128)S(1)}, bf16[32,2048]{1,0:T(8,128)(2,1)S(1...) custom-call(s32[16,4]{1,0:T(8,128)S(1)} %copy-done.2, ...), custom_call_target="tpu_custom_call" | custom-call | flops 268435456 | bytes 2974080 | tf_op jit(solution)/shard_map/pallas_call | solution.py:31
  34.1 16.8 %all-to-all-start.7 = ((bf16[64,40,128]{2,1,0:T(8,128)(2,1)}), bf16[64,40,128]{2,1,0:T(8,128)(2,1)S(1)}, u32[]{:S(2)}, u32[]{:S(2)}) async-start(bf16[64,40,128]{2,1,0:T(8,128)(2,1)} %get-tuple-element.243), calls=%async_computation.7 | async-start | bytes 1310720 | tf_op jit(solution)/shard_map/all_to_all | solution.py:576
  50.9 0.1 copy.142.bias
  51.0 0.1 copy.141
  51.1 19.6 %all-to-all-done.7.got = bf16[64,40,128]{2,1,0:T(8,128)(2,1)S(1)} async-done(((bf16[64,40,128]{2,1,0:T(8,128)(2,1)}), bf16[64,40,128]{2,1,0:T(8,128)(2,1)S(1)}, u32[]{:S(2)}, u32[]{:S(2)}) %all-to-all-start.7) | async-done | bytes 655392 | tf_op jit(solution)/shard_map/all_to_all | solution.py:576
  70.7 5.9 %shard_map.142 = (bf16[64,32,128]{2,1,0:T(8,128)(2,1)S(1)}, f32[64,32]{1,0:T(8,128)S(1)}) custom-call(bf16[64,40,128]{2,1,0:T(8,128)(2,1)S(1)} %all-to-all-done.7.got, bf16[32,32]{1,0:T(8,128)(2,1)S(1)} %copy-done.4, bf16[32,32]{1,0:T(8,128)(2,1)S(1)} %bitcast.112, f32[32,1]{1,0:T(8,128)S(1)} %copy.142.bias), custom_call_target="tpu_custom_call" | custom-call | bytes 659584 | tf_op jit(solution)/shard_map/pallas_call | solution.py:31
  76.6 23.1 %all_to_all.60.back = bf16[64,32,128]{2,1,0:T(8,128)(2,1)S(1)} all-to-all(bf16[64,32,128]{2,1,0:T(8,128)(2,1)S(1)} %get-tuple-element.244), channel_id=1, replica_groups=mesh['geo'=4,'region'=16,'sub'=4] {'region','sub'}, dimensions={0} | all-to-all | bytes 1048576 | tf_op jit(solution)/shard_map/all_to_all | solution.py:576
  99.7 3.4 %shard_map.143.lifted = bf16[64,2048]{1,0:T(8,128)(2,1)S(1)} custom-call(s32[1]{0:T(128)} %constant.16.clone.1.step, bf16[64,32,128]{2,1,0:T(8,128)(2,1)S(1)} %all_to_all.60.back, s32[1,2048]{1,0:T(1,128)S(1)} %get-tuple-element.240.dest, s32[1,2048]{1,0:T(1,128)S(1)} %get-tuple-element.241.rank), custom_call_target="tpu_custom_call" | custom-call | bytes 540676 | tf_op jit(solution)/shard_map/pallas_call | solution.py:31
  103.2 2.9 %shard_map.144 = (bf16[32,2048]{1,0:T(8,128)(2,1)S(1)}, bf16[32,2048]{1,0:T(8,128)(2,1)S(1)}, bf16[64,128]{1,0:T(8,128)(2,1)S(1)}, bf16[64,128]{1,0:T(8,128)(2,1)S(1)}, f32[32,2048]{1,0:T(8,128)S(1)}) custom-call(s32[16,4]{1,0:T(8,128)S(1)} %copy-done.2, bf16[64,128,128]{2,1,0:T(8,128)(2,1)} %bitcast.31.tiles_h, bf16[64,2048]{1,0:T(8,128)(2,1)S(1)} %shard_map.143.lifted, ...), custom_call_target="tpu_custom_call" | custom-call | flops 67108864 | bytes 2892032 | tf_op jit(solution)/shard_map/pallas_call | solution.py:31
  106.1 0.4 shard_map.147
  106.5 12.1 %all_to_all.61 = f32[16,4,128]{2,1,0:T(4,128)S(1)} all-to-all(f32[16,4,128]{2,1,0:T(4,128)S(1)} %bitcast.95), channel_id=1, replica_groups=mesh['geo'=4,'region'=16,'sub'=4] {'region'}, dimensions={0} | all-to-all | bytes 65536 | tf_op jit(solution)/shard_map/all_to_all | solution.py:568
  118.7 0.6 broadcast_in_dim.12
  119.3 5.5 %all-to-all-start.10 = ((f32[16,4,128]{2,1,0:T(4,128)}), f32[16,4,128]{2,1,0:T(4,128)S(1)}, u32[]{:S(2)}, u32[]{:S(2)}) async-start(f32[16,4,128]{2,1,0:T(4,128)} %broadcast_in_dim.12), calls=%async_computation.10 | async-start | bytes 65536 | tf_op jit(solution)/shard_map/all_to_all | solution.py:560
  124.8 3.3 %collective-permute-start.12 = (bf16[64,128]{1,0:T(8,128)(2,1)S(1)}, bf16[64,128]{1,0:T(8,128)(2,1)S(1)}, u32[]{:S(2)}, u32[]{:S(2)}) collective-permute-start(bf16[64,128]{1,0:T(8,128)(2,1)S(1)} %get-tuple-element.250), channel_id=1, source_target_pairs={{0,1},{1,2},{2,3},{3,4},{4,5},{5,6},{6,7},{7,8},{8,9},{9,10},{10,1... | collective-permute-start | bytes 49160 | tf_op jit(solution)/shard_map/ppermute | solution.py:76
  128.0 4.0 %collective-permute-start.13 = (bf16[64,128]{1,0:T(8,128)(2,1)S(1)}, bf16[64,128]{1,0:T(8,128)(2,1)S(1)}, u32[]{:S(2)}, u32[]{:S(2)}) collective-permute-start(bf16[64,128]{1,0:T(8,128)(2,1)S(1)} %get-tuple-element.251), channel_id=1, source_target_pairs={{1,0},{2,1},{3,2},{4,3},{5,4},{6,5},{7,6},{8,7},{9,8},{10,9},{11,1... | collective-permute-start | bytes 49160 | tf_op jit(solution)/shard_map/ppermute | solution.py:76
  132.0 0.8 collective-permute-done.13.down
  132.9 3.3 %shard_map.145 = (bf16[32,2048]{1,0:T(8,128)(2,1)S(1)}, bf16[32,2048]{1,0:T(8,128)(2,1)S(1)}, bf16[64,128]{1,0:T(8,128)(2,1)S(1)}, bf16[64,128]{1,0:T(8,128)(2,1)S(1)}, f32[32,2048]{1,0:T(8,128)S(1)}) custom-call(s32[16,4]{1,0:T(8,128)S(1)} %copy-done.2, bf16[64,128,128]{2,1,0:T(8,128)(2,1)} %bitcast.31.tiles_h, ...), custom_call_target="tpu_custom_call" | custom-call | flops 134217728 | bytes 2523392 | tf_op jit(solution)/shard_map/pallas_call | solution.py:31
  136.2 2.7 %collective-permute-start.14 = (bf16[64,128]{1,0:T(8,128)(2,1)S(1)}, bf16[64,128]{1,0:T(8,128)(2,1)S(1)}, u32[]{:S(2)}, u32[]{:S(2)}) collective-permute-start(bf16[64,128]{1,0:T(8,128)(2,1)S(1)} %get-tuple-element.255), channel_id=1, source_target_pairs={{0,1},{1,2},{2,3},{3,4},{4,5},{5,6},{6,7},{7,8},{8,9},{9,10},{10,1... | collective-permute-start | bytes 49160 | tf_op jit(solution)/shard_map/ppermute | solution.py:76
  139.0 4.6 %collective-permute-start.15 = (bf16[64,128]{1,0:T(8,128)(2,1)S(1)}, bf16[64,128]{1,0:T(8,128)(2,1)S(1)}, u32[]{:S(2)}, u32[]{:S(2)}) collective-permute-start(bf16[64,128]{1,0:T(8,128)(2,1)S(1)} %get-tuple-element.256), channel_id=1, source_target_pairs={{1,0},{2,1},{3,2},{4,3},{5,4},{6,5},{7,6},{8,7},{9,8},{10,9},{11,1... | collective-permute-start | bytes 49160 | tf_op jit(solution)/shard_map/ppermute | solution.py:76
  143.6 0.6 broadcast_in_dim.13
  144.2 6.4 %all-to-all-start.11 = ((f32[16,4,128]{2,1,0:T(4,128)}), f32[16,4,128]{2,1,0:T(4,128)S(1)}, u32[]{:S(2)}, u32[]{:S(2)}) async-start(f32[16,4,128]{2,1,0:T(4,128)} %broadcast_in_dim.13), calls=%async_computation.11 | async-start | bytes 65536 | tf_op jit(solution)/shard_map/all_to_all | solution.py:560
  150.7 0.1 pad_maximum_fusion.6
  150.8 3.5 %shard_map.146 = (bf16[32,2048]{1,0:T(8,128)(2,1)}, bf16[32,2048]{1,0:T(8,128)(2,1)}) custom-call(s32[16,4]{1,0:T(8,128)S(1)} %copy-done.2, bf16[64,128,128]{2,1,0:T(8,128)(2,1)} %bitcast.31.tiles_h, bf16[32,2048]{1,0:T(8,128)(2,1)S(1)} %get-tuple-element.248.f.merged, bf16[32,2048]{1,0:T(8,128)(2,1)S(1)} %get-tuple-element.249.g.pre_grad, ...), custom_call_target="tpu_custom_call" | custom-call | flops 134217728 | bytes 2928896 | tf_op jit(solution)/shard_map/pallas_call | solution.py:31
  154.3 3.8 %all-to-all-done.11 = f32[16,4,128]{2,1,0:T(4,128)S(1)} async-done(((f32[16,4,128]{2,1,0:T(4,128)}), f32[16,4,128]{2,1,0:T(4,128)S(1)}, u32[]{:S(2)}, u32[]{:S(2)}) %all-to-all-start.11) | async-done | bytes 32800 | tf_op jit(solution)/shard_map/all_to_all | solution.py:560
  158.1 0.7 shard_map.148
  158.8 0.6 slice.79
  159.4 0.9 while.33
  (33 shorter events, 0.1 us)
Async XLA Ops:
  0.6 14.4 %copy-start.5 = (bf16[1,32,2048]{2,1,0:T(8,128)(2,1)S(1)}, bf16[1,32,2048]{2,1,0:T(8,128)(2,1)}, u32[]{:S(2)}) copy-start(bf16[1,32,2048]{2,1,0:T(8,128)(2,1)} %param.17) | copy-start | bytes 393220
  0.6 13.3 %copy-start.13 = (bf16[3,32,32]{2,1,0:T(8,128)(2,1)S(1)}, bf16[3,32,32]{2,1,0:T(8,128)(2,1)}, u32[]{:S(2)}) copy-start(bf16[3,32,32]{2,1,0:T(8,128)(2,1)} %param.23) | copy-start | bytes 18436
  0.7 13.4 %copy-start.8 = (bf16[3,32,32]{2,1,0:T(8,128)(2,1)S(1)}, bf16[3,32,32]{2,1,0:T(8,128)(2,1)}, u32[]{:S(2)}) copy-start(bf16[3,32,32]{2,1,0:T(8,128)(2,1)} %param.25) | copy-start | bytes 18436
  0.7 13.4 %copy-start.12 = (f32[2,32]{1,0:T(2,128)S(1)}, f32[2,32]{1,0:T(2,128)}, u32[]{:S(2)}) copy-start(f32[2,32]{1,0:T(2,128)} %param.26) | copy-start | bytes 772
  2.1 12.9 %copy-start.2 = (s32[16,4]{1,0:T(8,128)S(1)}, s32[16,4]{1,0:T(8,128)}, u32[]{:S(2)}) copy-start(s32[16,4]{1,0:T(8,128)} %copy.145.cols) | copy-start | bytes 772
  2.1 24.8 %copy-start.9 = (s32[1,2048,1]{1,2,0:T(1,128)S(1)}, s32[1,2048,1]{1,2,0:T(1,128)}, u32[]{:S(2)}) copy-start(s32[1,2048,1]{1,2,0:T(1,128)} %param.20) | copy-start | bytes 24580
  2.1 24.8 %copy-start.10 = (s32[1,2048]{1,0:T(1,128)S(1)}, s32[1,2048]{1,0:T(1,128)}, u32[]{:S(2)}) copy-start(s32[1,2048]{1,0:T(1,128)} %slot.3) | copy-start | bytes 24580
  6.1 21.4 %copy-start.6 = (bf16[1,32,2048]{2,1,0:T(8,128)(2,1)S(1)}, bf16[1,32,2048]{2,1,0:T(8,128)(2,1)}, u32[]{:S(2)}) copy-start(bf16[1,32,2048]{2,1,0:T(8,128)(2,1)} %param.27) | copy-start | bytes 393220
  6.1 21.4 %copy-start.7 = (f32[1,2048]{1,0:T(1,128)S(1)}, f32[1,2048]{1,0:T(1,128)}, u32[]{:S(2)}) copy-start(f32[1,2048]{1,0:T(1,128)} %pool.3) | copy-start | bytes 24580
  6.1 8.5 %collective-permute-start.8 = (bf16[64,128]{1,0:T(8,128)(2,1)}, bf16[64,128]{1,0:T(8,128)(2,1)S(1)}, u32[]{:S(2)}, u32[]{:S(2)}) collective-permute-start(bf16[64,128]{1,0:T(8,128)(2,1)} %get-tuple-element.232), channel_id=1, source_target_pairs={{0,1},{1,2},{2,3},{3,4},{4,5},{5,6},{6,7},{7,8},{8,9},{9,10},{10,1... | collective-permute-start | bytes 49160 | tf_op jit(solution)/shard_map/ppermute | solution.py:76
  10.2 4.8 %collective-permute-start.9 = (bf16[64,128]{1,0:T(8,128)(2,1)}, bf16[64,128]{1,0:T(8,128)(2,1)S(1)}, u32[]{:S(2)}, u32[]{:S(2)}) collective-permute-start(bf16[64,128]{1,0:T(8,128)(2,1)} %get-tuple-element.233), channel_id=1, source_target_pairs={{1,0},{2,1},{3,2},{4,3},{5,4},{6,5},{7,6},{8,7},{9,8},{10,9},{11,1... | collective-permute-start | bytes 49160 | tf_op jit(solution)/shard_map/ppermute | solution.py:76
  15.0 1.0 copy-start.3
  19.3 7.8 %collective-permute-start.10 = (bf16[64,128]{1,0:T(8,128)(2,1)S(1)}, bf16[64,128]{1,0:T(8,128)(2,1)S(1)}, u32[]{:S(2)}, u32[]{:S(2)}) collective-permute-start(bf16[64,128]{1,0:T(8,128)(2,1)S(1)} %get-tuple-element.237), channel_id=1, source_target_pairs={{0,1},{1,2},{2,3},{3,4},{4,5},{5,6},{6,7},{7,8},{8,9},{9,10},{10,1... | collective-permute-start | bytes 49160 | tf_op jit(solution)/shard_map/ppermute | solution.py:76
  22.3 5.2 %collective-permute-start.11 = (bf16[64,128]{1,0:T(8,128)(2,1)S(1)}, bf16[64,128]{1,0:T(8,128)(2,1)S(1)}, u32[]{:S(2)}, u32[]{:S(2)}) collective-permute-start(bf16[64,128]{1,0:T(8,128)(2,1)S(1)} %get-tuple-element.238), channel_id=1, source_target_pairs={{1,0},{2,1},{3,2},{4,3},{5,4},{6,5},{7,6},{8,7},{9,8},{10,9},{11,1... | collective-permute-start | bytes 49160 | tf_op jit(solution)/shard_map/ppermute | solution.py:76
  27.5 23.5 %copy-start.4 = (bf16[32,32]{1,0:T(8,128)(2,1)S(1)}, bf16[32,32]{1,0:T(8,128)(2,1)}, u32[]{:S(2)}) copy-start(bf16[32,32]{1,0:T(8,128)(2,1)} %weight.1) | copy-start | bytes 6148
  34.1 36.6 %all-to-all-start.7 = ((bf16[64,40,128]{2,1,0:T(8,128)(2,1)}), bf16[64,40,128]{2,1,0:T(8,128)(2,1)S(1)}, u32[]{:S(2)}, u32[]{:S(2)}) async-start(bf16[64,40,128]{2,1,0:T(8,128)(2,1)} %get-tuple-element.243), calls=%async_computation.7 | async-start | bytes 1310720 | tf_op jit(solution)/shard_map/all_to_all | solution.py:576
  119.3 24.3 %all-to-all-start.10 = ((f32[16,4,128]{2,1,0:T(4,128)}), f32[16,4,128]{2,1,0:T(4,128)S(1)}, u32[]{:S(2)}, u32[]{:S(2)}) async-start(f32[16,4,128]{2,1,0:T(4,128)} %broadcast_in_dim.12), calls=%async_computation.10 | async-start | bytes 65536 | tf_op jit(solution)/shard_map/all_to_all | solution.py:560
  124.8 7.3 %collective-permute-start.12 = (bf16[64,128]{1,0:T(8,128)(2,1)S(1)}, bf16[64,128]{1,0:T(8,128)(2,1)S(1)}, u32[]{:S(2)}, u32[]{:S(2)}) collective-permute-start(bf16[64,128]{1,0:T(8,128)(2,1)S(1)} %get-tuple-element.250), channel_id=1, source_target_pairs={{0,1},{1,2},{2,3},{3,4},{4,5},{5,6},{6,7},{7,8},{8,9},{9,10},{10,1... | collective-permute-start | bytes 49160 | tf_op jit(solution)/shard_map/ppermute | solution.py:76
  128.0 4.8 %collective-permute-start.13 = (bf16[64,128]{1,0:T(8,128)(2,1)S(1)}, bf16[64,128]{1,0:T(8,128)(2,1)S(1)}, u32[]{:S(2)}, u32[]{:S(2)}) collective-permute-start(bf16[64,128]{1,0:T(8,128)(2,1)S(1)} %get-tuple-element.251), channel_id=1, source_target_pairs={{1,0},{2,1},{3,2},{4,3},{5,4},{6,5},{7,6},{8,7},{9,8},{10,9},{11,1... | collective-permute-start | bytes 49160 | tf_op jit(solution)/shard_map/ppermute | solution.py:76
  136.2 23.2 %copy-start.11 = (s32[1,16,4]{1,2,0:T(4,128)S(1)}, s32[1,16,4]{1,2,0:T(4,128)}, u32[]{:S(2)}) copy-start(s32[1,16,4]{1,2,0:T(4,128)} %param.19) | copy-start | bytes 772
  136.2 14.5 %collective-permute-start.14 = (bf16[64,128]{1,0:T(8,128)(2,1)S(1)}, bf16[64,128]{1,0:T(8,128)(2,1)S(1)}, u32[]{:S(2)}, u32[]{:S(2)}) collective-permute-start(bf16[64,128]{1,0:T(8,128)(2,1)S(1)} %get-tuple-element.255), channel_id=1, source_target_pairs={{0,1},{1,2},{2,3},{3,4},{4,5},{5,6},{6,7},{7,8},{8,9},{9,10},{10,1... | collective-permute-start | bytes 49160 | tf_op jit(solution)/shard_map/ppermute | solution.py:76
  139.0 11.8 %collective-permute-start.15 = (bf16[64,128]{1,0:T(8,128)(2,1)S(1)}, bf16[64,128]{1,0:T(8,128)(2,1)S(1)}, u32[]{:S(2)}, u32[]{:S(2)}) collective-permute-start(bf16[64,128]{1,0:T(8,128)(2,1)S(1)} %get-tuple-element.256), channel_id=1, source_target_pairs={{1,0},{2,1},{3,2},{4,3},{5,4},{6,5},{7,6},{8,7},{9,8},{10,9},{11,1... | collective-permute-start | bytes 49160 | tf_op jit(solution)/shard_map/ppermute | solution.py:76
  144.2 13.8 %all-to-all-start.11 = ((f32[16,4,128]{2,1,0:T(4,128)}), f32[16,4,128]{2,1,0:T(4,128)S(1)}, u32[]{:S(2)}, u32[]{:S(2)}) async-start(f32[16,4,128]{2,1,0:T(4,128)} %broadcast_in_dim.13), calls=%async_computation.11 | async-start | bytes 65536 | tf_op jit(solution)/shard_map/all_to_all | solution.py:560

commit v4 on v3

--- a/solution.py
+++ b/solution.py
@@ -15,24 +15,23 @@
 I32 = jnp.int32
 LANES = 128
 AUX = 8
+START_LIMIT = 16
 PAD = 16
-START_LIMIT = 59
 
 VM = pl.BlockSpec(memory_space=pltpu.VMEM)
 SM = pl.BlockSpec(memory_space=pltpu.SMEM)
-HB = pl.BlockSpec(memory_space=pltpu.HBM)
-
-
-def call(body, outs, scratch, args, smem=0, flops=0, limit=24, far=(), far_out=()):
+
+
+def call(body, outs, scratch, args, smem=0, flops=0, limit=24, far=()):
     specs = [SM] * smem + [VM] * (len(args) - smem)
     for i in far:
-        specs[i] = HB
+        specs[i] = pl.BlockSpec(memory_space=pl.ANY)
     moved = sum(a.size * a.dtype.itemsize for a in args)
     return pl.pallas_call(
         body,
         out_shape=tuple(jax.ShapeDtypeStruct(s, d) for s, d in outs),
         in_specs=specs,
-        out_specs=tuple(HB if i in far_out else VM for i in range(len(outs))),
+        out_specs=tuple(VM for _ in outs),
         scratch_shapes=scratch,
         cost_estimate=pl.CostEstimate(flops=flops, bytes_accessed=moved, transcendentals=0),
         compiler_params=pltpu.CompilerParams(vmem_limit_bytes=limit << 20),
@@ -74,26 +73,6 @@
     peers = lax.axis_size(LINE)
     pairs = [(i, i + by) for i in range(peers) if 0 <= i + by < peers]
     return lax.ppermute(value, LINE, pairs)
-
-
-def fetched(tiles_h, tiles, sems, count, nonzero, compact):
-    pieces = 4 if count % 4 == 0 else 1
-    size = count // pieces
-    copies = []
-    for i in range(pieces):
-        at = slice(i * size * nonzero, (i + 1) * size * nonzero)
-        copies.append(pltpu.make_async_copy(tiles_h.at[at], tiles.at[at], sems.at[i]))
-        copies[-1].start()
-
-    if compact:
-        for c in copies:
-            c.wait()
-
-    def ready(k):
-        if not compact and k % size == 0:
-            copies[k // size].wait()
-
-    return ready
 
 
 def add_transposed(cols, tiles, grad_of, ext, count, nonzero, compact):
@@ -148,28 +127,26 @@
 
 
 def start_body(
-    cols, tiles_h, f_h, g_h, up, down, inner, ext, tiles, edge, g, sems, *, chans, count, nonzero, compact
-):
-    last = slice((count - 1) * LANES, count * LANES)
-    copies = [
-        pltpu.make_async_copy(g_h, g, sems.at[4]),
-        pltpu.make_async_copy(f_h.at[:, 0:LANES], edge.at[0], sems.at[5]),
-        pltpu.make_async_copy(f_h.at[:, last], edge.at[1], sems.at[6]),
-    ]
-    copies[0].start()
-    ready = fetched(tiles_h, tiles, sems, count, nonzero, compact)
-    copies[1].start()
-    copies[2].start()
-    copies[0].wait()
+    cols, tiles_h, f, g, up, down, inner, tiles, ext, sems, *, chans, count, nonzero, compact
+):
+    pieces = 4 if count % 4 == 0 else 1
+    size = count // pieces
+    copies = []
+    for i in range(pieces):
+        at = slice(i * size * nonzero, (i + 1) * size * nonzero)
+        copies.append(pltpu.make_async_copy(tiles_h.at[at], tiles.at[at], sems.at[i]))
+        copies[-1].start()
+    if compact:
+        for c in copies:
+            c.wait()
 
     def grad_of(k):
-        ready(k)
+        if not compact and k % size == 0:
+            copies[k // size].wait()
         return tile(g, k)
 
     add_transposed(cols, tiles, grad_of, ext, count, nonzero, compact)
-    copies[1].wait()
-    copies[2].wait()
-    write_sends(up, down, edge[0], edge[1], ext, chans, count)
+    write_sends(up, down, tile(f, 0), tile(f, count - 1), ext, chans, count)
 
     def one(k):
         inner[:, lanes(k)] = ext[k + 1]
@@ -178,10 +155,9 @@
 
 
 def middle_body(
-    cols, tiles_h, f, up, down, inner, f1, g1, up2, down2, inner2, blocks, ext, tiles, sems,
+    cols, tiles, f, up, down, inner, f1, g1, up2, down2, inner2, blocks, ext,
     *, chans, count, nonzero, compact
 ):
-    ready = fetched(tiles_h, tiles, sems, count, nonzero, compact)
     fill_blocks(blocks, f, up, down, chans, count, compact)
 
     def one(k):
@@ -190,7 +166,6 @@
     each(count, one, compact)
 
     def one(k):
-        ready(k)
         f1[:, lanes(k)] = row_product(cols, tiles, blocks, k, nonzero).astype(BF)
 
     each(count, one, compact)
@@ -204,12 +179,11 @@
 
 
 def second_terms(
-    cols, tiles, f, g, f1, up, down, inner, blocks, f2, g2, chans, count, nonzero, ready, compact
+    cols, tiles, f, g, f1, up, down, inner, blocks, f2, g2, chans, count, nonzero, compact
 ):
     fill_blocks(blocks, f1, up, down, chans, count, compact)
 
     def one(k):
-        ready(k)
         at = lanes(k)
         y = row_product(cols, tiles, blocks, k, nonzero)
         f2[:, at] = (2.0 * y - f[:, at].astype(F32)).astype(BF)
@@ -256,8 +230,9 @@
 
 
 def pack_into(
-    buffer, big, out, sent, dest, rank, most, step, *, chans, peers, cap, go, rows
-):
+    buffer, big, out, sent, dest, rank, most, step, *, chans, peers, cap, go, rows, compact
+):
+    unroll = 1 if compact else peers // go
     high = 2 * chans + PAD
     group = dest // go
 
@@ -266,7 +241,7 @@
         big[pl.ds(pl.multiple_of(g * high, high), high), :] = sent[...] * here
         return carry
 
-    lax.fori_loop(0, peers // go, mask, 0, unroll=2)
+    lax.fori_loop(0, peers // go, mask, 0, unroll=unroll)
     out[...] = dot_nt(big[...], slot_hot(dest, rank, step, cap, go, rows))
     row = lax.broadcasted_iota(I32, (AUX, 2 * cap), 0)
     lane = lax.broadcasted_iota(I32, (AUX, 2 * cap), 1)
@@ -286,7 +261,7 @@
             buffer[p, chans : chans + AUX, :] = (merge_halves(aux, aux, odd, cap) + extra).astype(BF)
         return carry
 
-    lax.fori_loop(0, peers // go, place, 0, unroll=2)
+    lax.fori_loop(0, peers // go, place, 0, unroll=unroll)
 
 
 def pack_body(step, sent, dest, rank, most, buffer, big, out, *, cap, **sizes):
@@ -294,7 +269,10 @@
     pack_into(buffer, big, out, sent, dest[...], rank[...], needed, step[0], cap=cap, **sizes)
 
 
-def unpack_body(step, back, dest, rank, lifted, big, hot, *, chans, peers, cap, go, rows):
+def unpack_body(
+    step, back, dest, rank, lifted, big, hot, *, chans, peers, cap, go, rows, compact
+):
+    unroll = 1 if compact else peers // go
     hot[...] = slot_hot(dest[...], rank[...], step[0], cap, go, rows)
     high = 2 * chans
 
@@ -318,7 +296,7 @@
             big[rows_top, at] = top.astype(BF)
         return carry
 
-    lax.fori_loop(0, peers // go, gather, 0, unroll=2)
+    lax.fori_loop(0, peers // go, gather, 0, unroll=unroll)
     width = min(256, rows)
 
     def select(w, carry):
@@ -331,7 +309,7 @@
         lifted[:, at] = total.astype(BF)
         return carry
 
-    lax.fori_loop(0, rows // width, select, 0)
+    lax.fori_loop(0, rows // width, select, 0, unroll=1 if compact else rows // width)
 
 
 def coarse_hot(got, hot, masked, *, chans, peers, cap, parts):
@@ -441,27 +419,27 @@
     )
 
 
+def mixed(mix, first, second, third, k):
+    at = lanes(k)
+    return dot(mix[...], jnp.concatenate([first[:, at], second[:, at], third[:, at]], axis=0))
+
+
 def first_end_body(
-    cols, tiles_h, f, g, f1, g1, up, down, inner, pool, mix_in, mix_out_t, bias,
+    cols, tiles, f, g, f1, g1, up, down, inner, pool, mix_in, mix_out_t, bias,
     dest, rank, most, slot, owner,
-    f2, g2, pre_in, hidden, merged_grad, sent, buffer, blocks, big, out, tiles, sems,
+    f2, g2, buffer, sent, blocks, big, out,
     *, chans, count, nonzero, compact, peers, cap, go, rows
 ):
-    ready = fetched(tiles_h, tiles, sems, count, nonzero, compact)
     second_terms(
-        cols, tiles, f, g, f1, up, down, inner, blocks, f2, g2, chans, count, nonzero, ready,
-        compact,
+        cols, tiles, f, g, f1, up, down, inner, blocks, f2, g2, chans, count, nonzero, compact
     )
 
     def one(k):
         at = lanes(k)
         w = pool[:, at]
-        pre = dot(mix_in[...], jnp.concatenate([f[:, at], f1[:, at], f2[:, at]], axis=0)) + bias[...]
-        pre_in[:, at] = pre
+        pre = mixed(mix_in, f, f1, f2, k) + bias[...]
         h = (pre * jax.nn.sigmoid(pre)).astype(BF)
-        hidden[:, at] = h
-        m = dot(mix_out_t[...], jnp.concatenate([g[:, at], g1[:, at], g2[:, at]], axis=0)).astype(BF)
-        merged_grad[:, at] = m
+        m = mixed(mix_out_t, g, g1, g2, k).astype(BF)
         sent[0:chans, at] = (w * h.astype(F32)).astype(BF)
         sent[chans : 2 * chans, at] = (w * m.astype(F32)).astype(BF)
 
@@ -478,33 +456,28 @@
     needed = jnp.ceil(most[0:1, 0:1] * (1.0 / cap))
     pack_into(
         buffer, big, out, sent, dest[...], rank[...], needed, 0,
-        chans=chans, peers=peers, cap=cap, go=go, rows=rows,
+        chans=chans, peers=peers, cap=cap, go=go, rows=rows, compact=compact,
     )
 
 
 def second_start_body(
-    cols, tiles_h, lifted, hidden, merged_grad, pre_in, pool,
-    merged, pre_grad, up, down, inner, ext, tiles, sems,
+    cols, tiles, lifted, f, f1, f2, g, g1, g2, pool, mix_in, mix_out_t, bias,
+    merged, pre_grad, up, down, inner, ext,
     *, chans, count, nonzero, compact
 ):
-    ready = fetched(tiles_h, tiles, sems, count, nonzero, compact)
-
-    def one(k):
+    def fine(k):
         at = lanes(k)
         w = pool[:, at]
-        merged[:, at] = (
-            hidden[:, at].astype(F32) + w * lifted[0:chans, at].astype(F32)
-        ).astype(BF)
-        hidden_grad = merged_grad[:, at].astype(F32) + w * lifted[chans : 2 * chans, at].astype(F32)
-        pre_grad[:, at] = (hidden_grad * slope(pre_in[:, at])).astype(BF)
-
-    each(count, one, compact)
-
-    def grad_of(k):
-        ready(k)
-        return tile(pre_grad, k)
-
-    add_transposed(cols, tiles, grad_of, ext, count, nonzero, compact)
+        pre = mixed(mix_in, f, f1, f2, k) + bias[...]
+        sig = jax.nn.sigmoid(pre)
+        h = (pre * sig).astype(BF)
+        m = mixed(mix_out_t, g, g1, g2, k).astype(BF)
+        merged[:, at] = (h.astype(F32) + w * lifted[0:chans, at].astype(F32)).astype(BF)
+        hidden_grad = m.astype(F32) + w * lifted[chans : 2 * chans, at].astype(F32)
+        pre_grad[:, at] = (hidden_grad * (sig * (1.0 + pre * (1.0 - sig)))).astype(BF)
+
+    each(count, fine, compact)
+    add_transposed(cols, tiles, lambda k: tile(pre_grad, k), ext, count, nonzero, compact)
     write_sends(up, down, tile(merged, 0), tile(merged, count - 1), ext, chans, count)
 
     def one(k):
@@ -527,14 +500,12 @@
 
 
 def second_end_body(
-    cols, tiles_h, f, g, f1, g1, up, down, inner, mix_out, mix_in_t,
-    result, input_grad, f2, g2, blocks, tiles, sems,
+    cols, tiles, f, g, f1, g1, up, down, inner, mix_out, mix_in_t,
+    result, input_grad, f2, g2, blocks,
     *, chans, count, nonzero, compact
 ):
-    ready = fetched(tiles_h, tiles, sems, count, nonzero, compact)
     second_terms(
-        cols, tiles, f, g, f1, up, down, inner, blocks, f2, g2, chans, count, nonzero, ready,
-        compact,
+        cols, tiles, f, g, f1, up, down, inner, blocks, f2, g2, chans, count, nonzero, compact
     )
 
     def one(k):
@@ -619,7 +590,7 @@
     side = lambda w: jnp.concatenate([w[k] for k in range(3)], axis=1)
     side_t = lambda w: jnp.concatenate([w[k].T for k in range(3)], axis=1)
     line = dict(chans=chans, count=count, nonzero=nonzero, compact=several)
-    ways = dict(chans=chans, peers=peers, cap=cap, go=go, rows=rows)
+    ways = dict(chans=chans, peers=peers, cap=cap, go=go, rows=rows, compact=several)
     sizes = dict(chans=chans, peers=peers, cap=cap, parts=parts)
     full = (chans, rows)
     halo = (2 * chans, LANES)
@@ -636,7 +607,6 @@
         pltpu.VMEM((peers // go * 2 * chans, go * cap), BF),
         pltpu.VMEM((go * cap, rows), BF),
     ]
-    store = [pltpu.VMEM(tiles.shape, BF), pltpu.SemaphoreType.DMA((4,))]
     bias_mid = biases[1][:, None]
     weight_mid_t = weight_mid.T
 
@@ -649,28 +619,21 @@
         return call(
             functools.partial(middle_body, **line),
             [(full, BF), (full, BF), (halo, BF), (halo, BF), (full, F32)],
-            [blocks, ext, *store],
+            [blocks, ext],
             (cols, tiles, field, up, down, inner),
             smem=1,
-            far=(1,),
             flops=2 * work,
         )
 
-    up, down, inner = call(
+    up, down, inner, tiles = call(
         functools.partial(start_body, **line),
-        [(halo, BF), (halo, BF), (full, F32)],
-        [
-            ext,
-            pltpu.VMEM(tiles.shape, BF),
-            pltpu.VMEM((2, chans, LANES), BF),
-            pltpu.VMEM(full, BF),
-            pltpu.SemaphoreType.DMA((7,)),
-        ],
+        [(halo, BF), (halo, BF), (full, F32), (tiles.shape, BF)],
+        [ext, pltpu.SemaphoreType.DMA((4,))],
         (cols, tiles, f, g),
         smem=1,
+        far=(1,),
+        limit=START_LIMIT,
         flops=work,
-        far=(1, 2, 3),
-        limit=START_LIMIT,
     )
     up, down = passed(up, down)
     dest, rank, most = call(
@@ -682,27 +645,22 @@
     )
     f1, g1, up, down, inner = middle(f, up, down, inner)
     up, down = passed(up, down)
-    f2, g2, pre_in, hidden, merged_grad, sent, buffer = call(
+    mixes = (side(weight_in), side_t(weight_out), biases[0][:, None])
+    packed = (2 * chans + PAD, rows)
+    ended = call(
         functools.partial(first_end_body, **line, peers=peers, cap=cap, go=go, rows=rows),
-        [
-            (full, BF),
-            (full, BF),
-            (full, F32),
-            (full, BF),
-            (full, BF),
-            ((2 * chans + PAD, rows), BF),
-            (chunk, BF),
-        ],
-        [blocks, *pack_s, *store],
+        [(full, BF), (full, BF), (chunk, BF)] + [(packed, BF)] * several,
+        [pltpu.VMEM(packed, BF)] * (not several) + [blocks, *pack_s],
         (
-            cols, tiles, f, g, f1, g1, up, down, inner, pool, side(weight_in), side_t(weight_out),
-            biases[0][:, None], dest, rank, most, slot, owner,
+            cols, tiles, f, g, f1, g1, up, down, inner, pool, *mixes,
+            dest, rank, most, slot, owner,
         ),
         smem=1,
         flops=4 * work,
         limit=32,
-        far=(1,),
-    )
+    )
+    f2, g2, buffer = ended[:3]
+    sent = ended[-1]
     got = exchanged(buffer)
 
     def unpacked(back, step):
@@ -769,10 +727,9 @@
     merged, pre_grad, up, down, inner = call(
         functools.partial(second_start_body, **line),
         [(full, BF), (full, BF), (halo, BF), (halo, BF), (full, F32)],
-        [ext, *store],
-        (cols, tiles, lifted, hidden, merged_grad, pre_in, pool),
+        [ext],
+        (cols, tiles, lifted, f, f1, f2, g, g1, g2, pool, *mixes),
         smem=1,
-        far=(1,),
         flops=work,
     )
     up, down = passed(up, down)
@@ -788,14 +745,13 @@
     result, input_grad = call(
         functools.partial(second_end_body, **line),
         [(full, BF), (full, BF)],
-        [pltpu.VMEM(full, BF), pltpu.VMEM(full, BF), blocks, *store],
+        [pltpu.VMEM(full, BF), pltpu.VMEM(full, BF), blocks],
         (
             cols, tiles, merged, pre_grad, m1, p1, up, down, inner,
             side(weight_out), side_t(weight_in),
         ),
         smem=1,
         flops=2 * work,
-        far=(1,),
     )
     factor = 1.0 / math.sqrt(lax.axis_size("geo") * rows * peers)
     summed = summed_everywhere(local)

time: 161 us -> 152 us (0.944)
  Pallas kernels: 34.5 us -> 25.2 us
    pallas_call x11, Pallas kernels: 34.5 us -> 25.2 us  [call(): pl.pallas_call(body, out_shape=tuple((jax.ShapeDtypeStruct(s, d) for s, d...]
  transfers between devices with their start and end apart: 11 -> 11, of which waited for: 5 -> 3; matrix products, arithmetic and copies ran while one was open for 1% -> 2% of each run, Pallas kernels for 4% -> 3%
where the time goes in v4:
time: 152 us; the launch traced here: 151 us
  starting transfers between devices  57.3 us (38%)
  blocking collectives  35.2 us (23%)
  Pallas kernels  25.2 us (17%)
  waiting for transfers between devices  25 us (16%)
  local copies, waits for them, and re-layouts  5.66 us (4%)
    ppermute x8, starting transfers between devices, shifted(): return lax.ppermute(value, LINE, pairs)  29 us
    pallas_call x11, Pallas kernels, call(): pl.pallas_call(body, out_shape=tuple((jax.ShapeDtypeStruct(s, d) for s, d...  25.2 us
    all_to_all x1, blocking collectives, exchanged(): return lax.all_to_all(buffer, LINE, 0, 0, tiled=True)  23.1 us
    all_to_all x1, waiting for transfers between devices, exchanged(): return lax.all_to_all(buffer, LINE, 0, 0, tiled=True)  19.6 us
    all_to_all x1, starting transfers between devices, exchanged(): return lax.all_to_all(buffer, LINE, 0, 0, tiled=True)  16.4 us
    all_to_all x1, blocking collectives, summed_everywhere(): mine = lax.all_to_all(parts, 'region', 0, 0, tiled=True)  12.1 us
    all_to_all x2, starting transfers between devices, spread(): lax.all_to_all(jnp.broadcast_to(values[None], (peers, *values.shape)), ax...  11.9 us
    all_to_all x2, waiting for transfers between devices, spread(): lax.all_to_all(jnp.broadcast_to(values[None], (peers, *values.shape)), ax...  4.47 us
  transfers between devices with their start and end apart: 11, of which 3 were waited for; matrix products, arithmetic and copies ran while one was open for 2% of the time, Pallas kernels for 3%

profile of v4, /device:TPU:1, one launch (start us, length us, event | category | flops | bytes accessed | tf_op | source)
XLA Modules:
  0.0 151.3 jit_solution(12132717195980808070)
XLA Ops:
  0.7 0.8 copy.157.cols
  1.4 3.2 %shard_map.138 = (bf16[64,128]{1,0:T(8,128)(2,1)S(1)}, bf16[64,128]{1,0:T(8,128)(2,1)S(1)}, f32[32,2048]{1,0:T(8,128)S(1)}, bf16[64,128,128]{2,1,0:T(8,128)(2,1)S(1)}) custom-call(s32[16,4]{1,0:T(8,128)S(1)} %copy.157.cols, bf16[64,128,128]{2,1,0:T(8,128)(2,1)} %bitcast.98, bf16[32,2048]{1,0:T(8,128)(2,1)} %bitcast.32.f, bf16[32,2048]{1,0:T(8,128)(2,1)} %bitcast.33.g), custom_call_target="tpu_custom_call" | custom-call | flops 67108864 | bytes 2359552 | tf_op jit(solution)/shard_map/pallas_call | solution.py:30
  4.7 3.9 %collective-permute-start.8 = (bf16[64,128]{1,0:T(8,128)(2,1)S(1)}, bf16[64,128]{1,0:T(8,128)(2,1)S(1)}, u32[]{:S(2)}, u32[]{:S(2)}) collective-permute-start(bf16[64,128]{1,0:T(8,128)(2,1)S(1)} %get-tuple-element.229), channel_id=1, source_target_pairs={{0,1},{1,2},{2,3},{3,4},{4,5},{5,6},{6,7},{7,8},{8,9},{9,10},{10,1... | collective-permute-start | bytes 49160 | tf_op jit(solution)/shard_map/ppermute | solution.py:75
  8.6 3.7 %collective-permute-start.9 = (bf16[64,128]{1,0:T(8,128)(2,1)S(1)}, bf16[64,128]{1,0:T(8,128)(2,1)S(1)}, u32[]{:S(2)}, u32[]{:S(2)}) collective-permute-start(bf16[64,128]{1,0:T(8,128)(2,1)S(1)} %get-tuple-element.230), channel_id=1, source_target_pairs={{1,0},{2,1},{3,2},{4,3},{5,4},{6,5},{7,6},{8,7},{9,8},{10,9},{11,1... | collective-permute-start | bytes 49160 | tf_op jit(solution)/shard_map/ppermute | solution.py:75
  12.4 0.1 copy.141
  12.5 0.6 slice_bitcast_fusion.18
  13.1 0.6 slice_bitcast_fusion.25
  13.8 0.1 copy.144
  13.8 0.1 copy.145
  13.9 0.1 copy.146
  14.0 0.1 copy.147
  14.1 0.1 copy.148
  14.2 0.1 copy.149
  14.3 0.0 collective-permute-done.9.down
  14.3 2.1 %shard_map.139 = (bf16[32,2048]{1,0:T(8,128)(2,1)S(1)}, bf16[32,2048]{1,0:T(8,128)(2,1)S(1)}, bf16[64,128]{1,0:T(8,128)(2,1)S(1)}, bf16[64,128]{1,0:T(8,128)(2,1)S(1)}, f32[32,2048]{1,0:T(8,128)S(1)}) custom-call(s32[16,4]{1,0:T(8,128)S(1)} %copy.157.cols, bf16[64,128,128]{2,1,0:T(8,128)(2,1)S(1)} %get-tuple-element.228.tiles, bf16[32,2048]{1,0:T(8,128)(2,1)} %bitcast.32.f, ...), custom_call_target="tpu_custom_call" | custom-call | flops 134217728 | bytes 2523392 | tf_op jit(solution)/shard_map/pallas_call | solution.py:30
  16.4 1.9 %collective-permute-start.10 = (bf16[64,128]{1,0:T(8,128)(2,1)S(1)}, bf16[64,128]{1,0:T(8,128)(2,1)S(1)}, u32[]{:S(2)}, u32[]{:S(2)}) collective-permute-start(bf16[64,128]{1,0:T(8,128)(2,1)S(1)} %get-tuple-element.234), channel_id=1, source_target_pairs={{0,1},{1,2},{2,3},{3,4},{4,5},{5,6},{6,7},{7,8},{8,9},{9,10},{10,1... | collective-permute-start | bytes 49160 | tf_op jit(solution)/shard_map/ppermute | solution.py:75
  18.4 4.8 %collective-permute-start.11 = (bf16[64,128]{1,0:T(8,128)(2,1)S(1)}, bf16[64,128]{1,0:T(8,128)(2,1)S(1)}, u32[]{:S(2)}, u32[]{:S(2)}) collective-permute-start(bf16[64,128]{1,0:T(8,128)(2,1)S(1)} %get-tuple-element.235), channel_id=1, source_target_pairs={{1,0},{2,1},{3,2},{4,3},{5,4},{6,5},{7,6},{8,7},{9,8},{10,9},{11,1... | collective-permute-start | bytes 49160 | tf_op jit(solution)/shard_map/ppermute | solution.py:75
  23.2 0.1 pad_maximum_fusion.4
  23.3 0.1 copy.151.bias
  23.4 1.0 shard_map.140
  24.5 3.3 %shard_map.141 = (bf16[32,2048]{1,0:T(8,128)(2,1)S(1)}, bf16[32,2048]{1,0:T(8,128)(2,1)S(1)}, bf16[64,40,128]{2,1,0:T(8,128)(2,1)S(1)}) custom-call(s32[16,4]{1,0:T(8,128)S(1)} %copy.157.cols, bf16[64,128,128]{2,1,0:T(8,128)(2,1)S(1)} %get-tuple-element.228.tiles, bf16[32,2048]{1,0:T(8,128)(2,1)} %bitcast.32.f, bf16[32,2048]{1,0:T(8,128)(2,1)} %bitcast.33.g, ...), custom_call_target="tpu_custom_call" | custom-call | flops 268435456 | bytes 2974080 | tf_op jit(solution)/shard_map/pallas_call | solution.py:30
  27.8 0.9 copy-done
  28.6 16.4 %all-to-all-start.7 = ((bf16[64,40,128]{2,1,0:T(8,128)(2,1)}), bf16[64,40,128]{2,1,0:T(8,128)(2,1)S(1)}, u32[]{:S(2)}, u32[]{:S(2)}) async-start(bf16[64,40,128]{2,1,0:T(8,128)(2,1)} %copy-done), calls=%async_computation.7 | async-start | bytes 1310720 | tf_op jit(solution)/shard_map/all_to_all | solution.py:547
  45.0 0.1 copy.153.bias
  45.1 0.1 copy.152
  45.2 19.6 %all-to-all-done.7.got = bf16[64,40,128]{2,1,0:T(8,128)(2,1)S(1)} async-done(((bf16[64,40,128]{2,1,0:T(8,128)(2,1)}), bf16[64,40,128]{2,1,0:T(8,128)(2,1)S(1)}, u32[]{:S(2)}, u32[]{:S(2)}) %all-to-all-start.7) | async-done | bytes 655392 | tf_op jit(solution)/shard_map/all_to_all | solution.py:547
  64.8 5.9 %shard_map.142 = (bf16[64,32,128]{2,1,0:T(8,128)(2,1)S(1)}, f32[64,32]{1,0:T(8,128)S(1)}) custom-call(bf16[64,40,128]{2,1,0:T(8,128)(2,1)S(1)} %all-to-all-done.7.got, bf16[32,32]{1,0:T(8,128)(2,1)S(1)} %copy-done.1, bf16[32,32]{1,0:T(8,128)(2,1)S(1)} %bitcast.100, f32[32,1]{1,0:T(8,128)S(1)} %copy.153.bias), custom_call_target="tpu_custom_call" | custom-call | bytes 659584 | tf_op jit(solution)/shard_map/pallas_call | solution.py:30
  70.8 23.1 %all_to_all.60.back = bf16[64,32,128]{2,1,0:T(8,128)(2,1)S(1)} all-to-all(bf16[64,32,128]{2,1,0:T(8,128)(2,1)S(1)} %get-tuple-element.241), channel_id=1, replica_groups=mesh['geo'=4,'region'=16,'sub'=4] {'region','sub'}, dimensions={0} | all-to-all | bytes 1048576 | tf_op jit(solution)/shard_map/all_to_all | solution.py:547
  93.9 1.4 shard_map.143.lifted
  95.3 2.1 %shard_map.144 = (bf16[32,2048]{1,0:T(8,128)(2,1)S(1)}, bf16[32,2048]{1,0:T(8,128)(2,1)S(1)}, bf16[64,128]{1,0:T(8,128)(2,1)S(1)}, bf16[64,128]{1,0:T(8,128)(2,1)S(1)}, f32[32,2048]{1,0:T(8,128)S(1)}) custom-call(s32[16,4]{1,0:T(8,128)S(1)} %copy.157.cols, bf16[64,128,128]{2,1,0:T(8,128)(2,1)S(1)} %get-tuple-element.228.tiles, ...), custom_call_target="tpu_custom_call" | custom-call | flops 67108864 | bytes 3166592 | tf_op jit(solution)/shard_map/pallas_call | solution.py:30
  97.4 1.4 shard_map.147
  98.8 12.1 %all_to_all.61 = f32[16,4,128]{2,1,0:T(4,128)S(1)} all-to-all(f32[16,4,128]{2,1,0:T(4,128)S(1)} %bitcast.95), channel_id=1, replica_groups=mesh['geo'=4,'region'=16,'sub'=4] {'region'}, dimensions={0} | all-to-all | bytes 65536 | tf_op jit(solution)/shard_map/all_to_all | solution.py:539
  111.0 0.6 broadcast_in_dim.12
  111.6 5.5 %all-to-all-start.10 = ((f32[16,4,128]{2,1,0:T(4,128)}), f32[16,4,128]{2,1,0:T(4,128)S(1)}, u32[]{:S(2)}, u32[]{:S(2)}) async-start(f32[16,4,128]{2,1,0:T(4,128)} %broadcast_in_dim.12), calls=%async_computation.10 | async-start | bytes 65536 | tf_op jit(solution)/shard_map/all_to_all | solution.py:531
  117.1 3.3 %collective-permute-start.12 = (bf16[64,128]{1,0:T(8,128)(2,1)S(1)}, bf16[64,128]{1,0:T(8,128)(2,1)S(1)}, u32[]{:S(2)}, u32[]{:S(2)}) collective-permute-start(bf16[64,128]{1,0:T(8,128)(2,1)S(1)} %get-tuple-element.246), channel_id=1, source_target_pairs={{0,1},{1,2},{2,3},{3,4},{4,5},{5,6},{6,7},{7,8},{8,9},{9,10},{10,1... | collective-permute-start | bytes 49160 | tf_op jit(solution)/shard_map/ppermute | solution.py:75
  120.3 4.0 %collective-permute-start.13 = (bf16[64,128]{1,0:T(8,128)(2,1)S(1)}, bf16[64,128]{1,0:T(8,128)(2,1)S(1)}, u32[]{:S(2)}, u32[]{:S(2)}) collective-permute-start(bf16[64,128]{1,0:T(8,128)(2,1)S(1)} %get-tuple-element.247), channel_id=1, source_target_pairs={{1,0},{2,1},{3,2},{4,3},{5,4},{6,5},{7,6},{8,7},{9,8},{10,9},{11,1... | collective-permute-start | bytes 49160 | tf_op jit(solution)/shard_map/ppermute | solution.py:75
  124.3 0.8 collective-permute-done.13.down
  125.2 1.9 %shard_map.145 = (bf16[32,2048]{1,0:T(8,128)(2,1)S(1)}, bf16[32,2048]{1,0:T(8,128)(2,1)S(1)}, bf16[64,128]{1,0:T(8,128)(2,1)S(1)}, bf16[64,128]{1,0:T(8,128)(2,1)S(1)}, f32[32,2048]{1,0:T(8,128)S(1)}) custom-call(s32[16,4]{1,0:T(8,128)S(1)} %copy.157.cols, bf16[64,128,128]{2,1,0:T(8,128)(2,1)S(1)} %get-tuple-element.228.tiles, ...), custom_call_target="tpu_custom_call" | custom-call | flops 134217728 | bytes 2523392 | tf_op jit(solution)/shard_map/pallas_call | solution.py:30
  127.1 2.8 %collective-permute-start.14 = (bf16[64,128]{1,0:T(8,128)(2,1)S(1)}, bf16[64,128]{1,0:T(8,128)(2,1)S(1)}, u32[]{:S(2)}, u32[]{:S(2)}) collective-permute-start(bf16[64,128]{1,0:T(8,128)(2,1)S(1)} %get-tuple-element.251), channel_id=1, source_target_pairs={{0,1},{1,2},{2,3},{3,4},{4,5},{5,6},{6,7},{7,8},{8,9},{9,10},{10,1... | collective-permute-start | bytes 49160 | tf_op jit(solution)/shard_map/ppermute | solution.py:75
  129.8 4.6 %collective-permute-start.15 = (bf16[64,128]{1,0:T(8,128)(2,1)S(1)}, bf16[64,128]{1,0:T(8,128)(2,1)S(1)}, u32[]{:S(2)}, u32[]{:S(2)}) collective-permute-start(bf16[64,128]{1,0:T(8,128)(2,1)S(1)} %get-tuple-element.252), channel_id=1, source_target_pairs={{1,0},{2,1},{3,2},{4,3},{5,4},{6,5},{7,6},{8,7},{9,8},{10,9},{11,1... | collective-permute-start | bytes 49160 | tf_op jit(solution)/shard_map/ppermute | solution.py:75
  134.4 0.6 broadcast_in_dim.13
  135.1 6.4 %all-to-all-start.11 = ((f32[16,4,128]{2,1,0:T(4,128)}), f32[16,4,128]{2,1,0:T(4,128)S(1)}, u32[]{:S(2)}, u32[]{:S(2)}) async-start(f32[16,4,128]{2,1,0:T(4,128)} %broadcast_in_dim.13), calls=%async_computation.11 | async-start | bytes 65536 | tf_op jit(solution)/shard_map/all_to_all | solution.py:531
  141.5 0.8 pad_maximum_fusion.6
  142.4 2.1 %shard_map.146 = (bf16[32,2048]{1,0:T(8,128)(2,1)}, bf16[32,2048]{1,0:T(8,128)(2,1)}) custom-call(s32[16,4]{1,0:T(8,128)S(1)} %copy.157.cols, bf16[64,128,128]{2,1,0:T(8,128)(2,1)S(1)} %get-tuple-element.228.tiles, bf16[32,2048]{1,0:T(8,128)(2,1)S(1)} %get-tuple-element.244.f.merged, bf16[32,2048]{1,0:T(8,128)(2,1)S(1)} %get-tuple-element.245.g.pre_grad, ...), custom_call_target="tpu_custom_call" | custom-call | flops 134217728 | bytes 2928896 | tf_op jit(solution)/shard_map/pallas_call | solution.py:30
  144.4 4.5 %all-to-all-done.11 = f32[16,4,128]{2,1,0:T(4,128)S(1)} async-done(((f32[16,4,128]{2,1,0:T(4,128)}), f32[16,4,128]{2,1,0:T(4,128)S(1)}, u32[]{:S(2)}, u32[]{:S(2)}) %all-to-all-start.11) | async-done | bytes 32800 | tf_op jit(solution)/shard_map/all_to_all | solution.py:531
  148.9 0.7 shard_map.148
  149.6 0.6 slice.79
  150.2 0.9 while.33
  (29 shorter events, 0.1 us)
Async XLA Ops:
  0.6 11.8 %copy-start.16 = (bf16[3,32,32]{2,1,0:T(8,128)(2,1)S(1)}, bf16[3,32,32]{2,1,0:T(8,128)(2,1)}, u32[]{:S(2)}) copy-start(bf16[3,32,32]{2,1,0:T(8,128)(2,1)} %param.23) | copy-start | bytes 18436
  0.6 12.5 %copy-start.3 = (bf16[3,32,32]{2,1,0:T(8,128)(2,1)S(1)}, bf16[3,32,32]{2,1,0:T(8,128)(2,1)}, u32[]{:S(2)}) copy-start(bf16[3,32,32]{2,1,0:T(8,128)(2,1)} %param.25) | copy-start | bytes 18436
  0.7 13.1 %copy-start.11 = (f32[2,32]{1,0:T(2,128)S(1)}, f32[2,32]{1,0:T(2,128)}, u32[]{:S(2)}) copy-start(f32[2,32]{1,0:T(2,128)} %param.26) | copy-start | bytes 772
  4.7 19.8 %copy-start.2 = (f32[1,2048]{1,0:T(1,128)S(1)}, f32[1,2048]{1,0:T(1,128)}, u32[]{:S(2)}) copy-start(f32[1,2048]{1,0:T(1,128)} %pool.3) | copy-start | bytes 24580
  4.7 9.6 %collective-permute-start.8 = (bf16[64,128]{1,0:T(8,128)(2,1)S(1)}, bf16[64,128]{1,0:T(8,128)(2,1)S(1)}, u32[]{:S(2)}, u32[]{:S(2)}) collective-permute-start(bf16[64,128]{1,0:T(8,128)(2,1)S(1)} %get-tuple-element.229), channel_id=1, source_target_pairs={{0,1},{1,2},{2,3},{3,4},{4,5},{5,6},{6,7},{7,8},{8,9},{9,10},{10,1... | collective-permute-start | bytes 49160 | tf_op jit(solution)/shard_map/ppermute | solution.py:75
  8.6 5.7 %collective-permute-start.9 = (bf16[64,128]{1,0:T(8,128)(2,1)S(1)}, bf16[64,128]{1,0:T(8,128)(2,1)S(1)}, u32[]{:S(2)}, u32[]{:S(2)}) collective-permute-start(bf16[64,128]{1,0:T(8,128)(2,1)S(1)} %get-tuple-element.230), channel_id=1, source_target_pairs={{1,0},{2,1},{3,2},{4,3},{5,4},{6,5},{7,6},{8,7},{9,8},{10,9},{11,1... | collective-permute-start | bytes 49160 | tf_op jit(solution)/shard_map/ppermute | solution.py:75
  16.4 8.0 %collective-permute-start.10 = (bf16[64,128]{1,0:T(8,128)(2,1)S(1)}, bf16[64,128]{1,0:T(8,128)(2,1)S(1)}, u32[]{:S(2)}, u32[]{:S(2)}) collective-permute-start(bf16[64,128]{1,0:T(8,128)(2,1)S(1)} %get-tuple-element.234), channel_id=1, source_target_pairs={{0,1},{1,2},{2,3},{3,4},{4,5},{5,6},{6,7},{7,8},{8,9},{9,10},{10,1... | collective-permute-start | bytes 49160 | tf_op jit(solution)/shard_map/ppermute | solution.py:75
  18.4 6.1 %collective-permute-start.11 = (bf16[64,128]{1,0:T(8,128)(2,1)S(1)}, bf16[64,128]{1,0:T(8,128)(2,1)S(1)}, u32[]{:S(2)}, u32[]{:S(2)}) collective-permute-start(bf16[64,128]{1,0:T(8,128)(2,1)S(1)} %get-tuple-element.235), channel_id=1, source_target_pairs={{1,0},{2,1},{3,2},{4,3},{5,4},{6,5},{7,6},{8,7},{9,8},{10,9},{11,1... | collective-permute-start | bytes 49160 | tf_op jit(solution)/shard_map/ppermute | solution.py:75
  24.5 20.7 %copy-start.1 = (bf16[32,32]{1,0:T(8,128)(2,1)S(1)}, bf16[32,32]{1,0:T(8,128)(2,1)}, u32[]{:S(2)}) copy-start(bf16[32,32]{1,0:T(8,128)(2,1)} %weight.1) | copy-start | bytes 6148
  27.8 0.9 copy-start
  28.6 36.2 %all-to-all-start.7 = ((bf16[64,40,128]{2,1,0:T(8,128)(2,1)}), bf16[64,40,128]{2,1,0:T(8,128)(2,1)S(1)}, u32[]{:S(2)}, u32[]{:S(2)}) async-start(bf16[64,40,128]{2,1,0:T(8,128)(2,1)} %copy-done), calls=%async_computation.7 | async-start | bytes 1310720 | tf_op jit(solution)/shard_map/all_to_all | solution.py:547
  97.4 44.1 %copy-start.14 = (bf16[32,32]{1,0:T(8,128)(2,1)S(1)}, bf16[32,32]{1,0:T(8,128)(2,1)}, u32[]{:S(2)}) copy-start(bf16[32,32]{1,0:T(8,128)(2,1)} %get-tuple-element.408) | copy-start | bytes 6148
  97.4 44.1 %copy-start.15 = (bf16[32,32]{1,0:T(8,128)(2,1)S(1)}, bf16[32,32]{1,0:T(8,128)(2,1)}, u32[]{:S(2)}) copy-start(bf16[32,32]{1,0:T(8,128)(2,1)} %get-tuple-element.409) | copy-start | bytes 6148
  111.6 22.8 %all-to-all-start.10 = ((f32[16,4,128]{2,1,0:T(4,128)}), f32[16,4,128]{2,1,0:T(4,128)S(1)}, u32[]{:S(2)}, u32[]{:S(2)}) async-start(f32[16,4,128]{2,1,0:T(4,128)} %broadcast_in_dim.12), calls=%async_computation.10 | async-start | bytes 65536 | tf_op jit(solution)/shard_map/all_to_all | solution.py:531
  117.1 7.3 %collective-permute-start.12 = (bf16[64,128]{1,0:T(8,128)(2,1)S(1)}, bf16[64,128]{1,0:T(8,128)(2,1)S(1)}, u32[]{:S(2)}, u32[]{:S(2)}) collective-permute-start(bf16[64,128]{1,0:T(8,128)(2,1)S(1)} %get-tuple-element.246), channel_id=1, source_target_pairs={{0,1},{1,2},{2,3},{3,4},{4,5},{5,6},{6,7},{7,8},{8,9},{9,10},{10,1... | collective-permute-start | bytes 49160 | tf_op jit(solution)/shard_map/ppermute | solution.py:75
  120.3 4.8 %collective-permute-start.13 = (bf16[64,128]{1,0:T(8,128)(2,1)S(1)}, bf16[64,128]{1,0:T(8,128)(2,1)S(1)}, u32[]{:S(2)}, u32[]{:S(2)}) collective-permute-start(bf16[64,128]{1,0:T(8,128)(2,1)S(1)} %get-tuple-element.247), channel_id=1, source_target_pairs={{1,0},{2,1},{3,2},{4,3},{5,4},{6,5},{7,6},{8,7},{9,8},{10,9},{11,1... | collective-permute-start | bytes 49160 | tf_op jit(solution)/shard_map/ppermute | solution.py:75
  127.0 23.2 %copy-start.10 = (s32[1,16,4]{1,2,0:T(4,128)S(1)}, s32[1,16,4]{1,2,0:T(4,128)}, u32[]{:S(2)}) copy-start(s32[1,16,4]{1,2,0:T(4,128)} %param.19) | copy-start | bytes 772
  127.1 23.2 %copy-start.12 = (f32[2,32]{1,0:T(2,128)S(1)}, f32[2,32]{1,0:T(2,128)}, u32[]{:S(2)}) copy-start(f32[2,32]{1,0:T(2,128)} %param.26) | copy-start | bytes 772
  127.1 15.3 %collective-permute-start.14 = (bf16[64,128]{1,0:T(8,128)(2,1)S(1)}, bf16[64,128]{1,0:T(8,128)(2,1)S(1)}, u32[]{:S(2)}, u32[]{:S(2)}) collective-permute-start(bf16[64,128]{1,0:T(8,128)(2,1)S(1)} %get-tuple-element.251), channel_id=1, source_target_pairs={{0,1},{1,2},{2,3},{3,4},{4,5},{5,6},{6,7},{7,8},{8,9},{9,10},{10,1... | collective-permute-start | bytes 49160 | tf_op jit(solution)/shard_map/ppermute | solution.py:75
  129.8 12.5 %collective-permute-start.15 = (bf16[64,128]{1,0:T(8,128)(2,1)S(1)}, bf16[64,128]{1,0:T(8,128)(2,1)S(1)}, u32[]{:S(2)}, u32[]{:S(2)}) collective-permute-start(bf16[64,128]{1,0:T(8,128)(2,1)S(1)} %get-tuple-element.252), channel_id=1, source_target_pairs={{1,0},{2,1},{3,2},{4,3},{5,4},{6,5},{7,6},{8,7},{9,8},{10,9},{11,1... | collective-permute-start | bytes 49160 | tf_op jit(solution)/shard_map/ppermute | solution.py:75
  135.1 13.8 %all-to-all-start.11 = ((f32[16,4,128]{2,1,0:T(4,128)}), f32[16,4,128]{2,1,0:T(4,128)S(1)}, u32[]{:S(2)}, u32[]{:S(2)}) async-start(f32[16,4,128]{2,1,0:T(4,128)} %broadcast_in_dim.13), calls=%async_computation.11 | async-start | bytes 65536 | tf_op jit(solution)/shard_map/all_to_all | solution.py:531

commit v5 on v4

--- a/solution.py
+++ b/solution.py
@@ -22,7 +22,7 @@
 SM = pl.BlockSpec(memory_space=pltpu.SMEM)
 
 
-def call(body, outs, scratch, args, smem=0, flops=0, limit=24, far=()):
+def call(body, outs, scratch, args, smem=0, flops=0, limit=24, far=(), smem_out=()):
     specs = [SM] * smem + [VM] * (len(args) - smem)
     for i in far:
         specs[i] = pl.BlockSpec(memory_space=pl.ANY)
@@ -31,7 +31,7 @@
         body,
         out_shape=tuple(jax.ShapeDtypeStruct(s, d) for s, d in outs),
         in_specs=specs,
-        out_specs=tuple(VM for _ in outs),
+        out_specs=tuple(SM if i in smem_out else VM for i in range(len(outs))),
         scratch_shapes=scratch,
         cost_estimate=pl.CostEstimate(flops=flops, bytes_accessed=moved, transcendentals=0),
         compiler_params=pltpu.CompilerParams(vmem_limit_bytes=limit << 20),
@@ -81,7 +81,7 @@
     def one(k):
         y = dot_nt(grad_of(k), row_tiles(tiles, k, nonzero))
         for n in range(nonzero):
-            ext[cols[k, n]] += y[:, n * LANES : (n + 1) * LANES]
+            ext[cols[n, k]] += y[:, n * LANES : (n + 1) * LANES]
 
     each(count, one, compact)
 
@@ -91,7 +91,7 @@
 
 
 def row_product(cols, tiles, blocks, k, nonzero):
-    picked = [blocks[cols[k, n]] for n in range(nonzero)]
+    picked = [blocks[cols[n, k]] for n in range(nonzero)]
     return dot(jnp.concatenate(picked, axis=1), row_tiles(tiles, k, nonzero))
 
 
@@ -191,6 +191,21 @@
         g2[:, at] = (2.0 * z - g[:, at].astype(F32)).astype(BF)
 
     each(count, one, compact)
+
+
+def prepare_body(
+    w_in, w_mid, w_out, biases, mix_in, mix_in_t, mix_out, mix_out_t, mid, mid_t, bias_in, bias_mid,
+    *, chans
+):
+    flip = lambda w: w.astype(F32).T.astype(BF)
+    for source, plain, turned in ((w_in, mix_in, mix_in_t), (w_out, mix_out, mix_out_t)):
+        plain[...] = jnp.concatenate([source[k] for k in range(3)], axis=1)
+        turned[...] = jnp.concatenate([flip(source[k]) for k in range(3)], axis=1)
+    mid[...] = w_mid[...]
+    mid_t[...] = flip(w_mid[...])
+    same = lax.broadcasted_iota(I32, (chans, chans), 0) == lax.broadcasted_iota(I32, (chans, chans), 1)
+    for row, column in ((0, bias_in), (1, bias_mid)):
+        column[...] = jnp.sum(jnp.where(same, biases[row : row + 1, :], 0.0), axis=1, keepdims=True)
 
 
 def place_body(owner, slot, dest, rank, most, *, peers, rows):
@@ -333,7 +348,7 @@
 
 
 def coarse_totals(hot, masked, chans, parts):
-    acc = dot_nt(masked[...], hot[...])
+    acc = dot_nt(hot[...], masked[...]).T
     split = [acc[h * chans : (h + 1) * chans] for h in range(parts)]
     low = jnp.concatenate([s[:, 0:LANES] for s in split], axis=1)
     top = jnp.concatenate([s[:, LANES:] for s in split], axis=1)
@@ -490,13 +505,16 @@
     p, m = pre_grad[...], merged[...]
     gin = [dot_nt(p, t[...]) for t in (f, f1, f2)]
     gout = [dot_nt(t[...], m) for t in (g, g1, g2)]
-    local[0:chans, :] = jnp.concatenate(gin + [mid[0:chans, :]], axis=1)
     total = dot_nt(jnp.ones(p.shape, BF), p)
     row = lax.broadcasted_iota(I32, (chans, chans), 0)
     sums = jnp.where(row == 0, total, mid[chans : 2 * chans, :])
     over = jnp.where(most[0:1, 0:1] > cap, 1.0, 0.0)
     sums = jnp.where(row == 2, over, sums)
-    local[chans : 2 * chans, :] = jnp.concatenate(gout + [sums], axis=1)
+    upper = jnp.concatenate(gin + [mid[0:chans, :]], axis=1).astype(BF)
+    lower = jnp.concatenate(gout + [sums], axis=1).astype(BF)
+    for i in range(local.shape[0]):
+        local[i, 0:chans, :] = upper
+        local[i, chans : 2 * chans, :] = lower
 
 
 def second_end_body(
@@ -518,29 +536,27 @@
     each(count, one, compact)
 
 
-def last_body(total, weights, biases, *, chans, factor):
+def total_of(got):
+    total = got[0].astype(F32)
+    for i in range(1, got.shape[0]):
+        total = total + got[i].astype(F32)
+    return total
+
+
+def relay_body(got, spread):
+    total = total_of(got).astype(BF)
+    for i in range(spread.shape[0]):
+        spread[i] = total
+
+
+def last_body(got, weights, biases, over, total, *, chans, factor):
+    total[...] = total_of(got)
+    over[0] = jnp.sum(total[chans + 2 : chans + 3, 3 * chans : 3 * chans + 1])
     for k in range(7):
         low = k // 4 * chans
         at = slice(k % 4 * chans, (k % 4 + 1) * chans)
         weights[k] = total[low : low + chans, at] * factor
     biases[...] = total[chans : chans + 2, 3 * chans : 4 * chans] * factor
-
-
-def spread(values, axes):
-    peers = lax.axis_size(axes)
-    return lax.all_to_all(
-        jnp.broadcast_to(values[None], (peers, *values.shape)), axes, 0, 0, tiled=True
-    )
-
-
-def summed_everywhere(local):
-    regions = lax.axis_size("region")
-    parts = local.reshape(regions, -1, LANES)
-    mine = lax.all_to_all(parts, "region", 0, 0, tiled=True)
-    mine = jnp.sum(mine, axis=0)
-    mine = spread(mine, ("geo", "sub"))
-    mine = jnp.sum(mine, axis=0)
-    return spread(mine, "region").reshape(local.shape)
 
 
 def exchanged(buffer):
@@ -583,12 +599,10 @@
     parts = coarse_rows // LANES
     f, g = features[0], out_grad[0]
     tiles = lap_tiles[0].reshape(count * nonzero, LANES, LANES)
-    cols = tile_cols[0]
+    cols = tile_cols[0].T
     owner = coarse_owner[0].reshape(1, rows)
     slot = coarse_slot
     pool = pool_weight
-    side = lambda w: jnp.concatenate([w[k] for k in range(3)], axis=1)
-    side_t = lambda w: jnp.concatenate([w[k].T for k in range(3)], axis=1)
     line = dict(chans=chans, count=count, nonzero=nonzero, compact=several)
     ways = dict(chans=chans, peers=peers, cap=cap, go=go, rows=rows, compact=several)
     sizes = dict(chans=chans, peers=peers, cap=cap, parts=parts)
@@ -607,8 +621,15 @@
         pltpu.VMEM((peers // go * 2 * chans, go * cap), BF),
         pltpu.VMEM((go * cap, rows), BF),
     ]
-    bias_mid = biases[1][:, None]
-    weight_mid_t = weight_mid.T
+    small = (chans, chans)
+    wide = (chans, 3 * chans)
+    mix_in, mix_in_t, mix_out, mix_out_t, mid_w, mid_t, bias_in, bias_mid = call(
+        functools.partial(prepare_body, chans=chans),
+        [(wide, BF)] * 4 + [(small, BF)] * 2 + [((chans, 1), F32)] * 2,
+        [],
+        (weight_in, weight_mid, weight_out, biases),
+        flops=2 * work,
+    )
 
     def passed(up, down):
         up = shifted(up, 1)
@@ -645,7 +666,7 @@
     )
     f1, g1, up, down, inner = middle(f, up, down, inner)
     up, down = passed(up, down)
-    mixes = (side(weight_in), side_t(weight_out), biases[0][:, None])
+    mixes = (mix_in, mix_out_t, bias_in)
     packed = (2 * chans + PAD, rows)
     ended = call(
         functools.partial(first_end_body, **line, peers=peers, cap=cap, go=go, rows=rows),
@@ -700,7 +721,7 @@
             math_body,
             [((2 * chans, coarse_rows), BF), ((2 * chans, chans), F32)],
             [],
-            (totals, weight_mid, weight_mid_t, bias_mid),
+            (totals, mid_w, mid_t, bias_mid),
         )
 
         def fetch(step, lifted):
@@ -719,7 +740,7 @@
             functools.partial(coarse_body, **sizes),
             [(reply, BF), ((2 * chans, chans), F32)],
             [hot_s, masked_s],
-            (got, weight_mid, weight_mid_t, bias_mid),
+            (got, mid_w, mid_t, bias_mid),
             limit=32,
         )
         lifted = unpacked(exchanged(back), jnp.zeros((1,), I32))
@@ -735,7 +756,7 @@
     up, down = passed(up, down)
     local = call(
         functools.partial(weights_body, chans=chans, cap=cap),
-        [((2 * chans, LANES), F32)],
+        [((lax.axis_size("region"), 2 * chans, LANES), BF)],
         [],
         (merged, pre_grad, f, f1, f2, g, g1, g2, mid, most),
         flops=work,
@@ -748,20 +769,24 @@
         [pltpu.VMEM(full, BF), pltpu.VMEM(full, BF), blocks],
         (
             cols, tiles, merged, pre_grad, m1, p1, up, down, inner,
-            side(weight_out), side_t(weight_in),
+            mix_out, mix_in_t,
         ),
         smem=1,
         flops=2 * work,
     )
     factor = 1.0 / math.sqrt(lax.axis_size("geo") * rows * peers)
-    summed = summed_everywhere(local)
-    sum_weights, sum_biases = call(
+    got = lax.all_to_all(local, "region", 0, 0, tiled=True)
+    rest = lax.axis_size("geo") * lax.axis_size("sub")
+    spread = call(relay_body, [((rest, 2 * chans, LANES), BF)], [], (got,))[0]
+    got = lax.all_to_all(spread, ("geo", "sub"), 0, 0, tiled=True)
+    sum_weights, sum_biases, over = call(
         functools.partial(last_body, chans=chans, factor=factor),
-        [((7, chans, chans), F32), ((2, chans), F32)],
-        [],
-        (summed,),
-    )
-    return result, input_grad, sum_weights, sum_biases, summed[chans + 2, 3 * chans]
+        [((7, chans, chans), F32), ((2, chans), F32), ((1,), F32)],
+        [pltpu.VMEM((2 * chans, LANES), F32)],
+        (got,),
+        smem_out=(2,),
+    )
+    return result, input_grad, sum_weights, sum_biases, over.reshape(())
 
 
 def solution(mesh):

time: 152 us -> 143 us (0.941); the launches traced: 151 us -> 140 us
  blocking collectives: 35.2 us -> 74.6 us
  starting transfers between devices: 57.3 us -> 34.3 us
  waiting for transfers between devices: 25 us -> 2.94 us
  local copies, waits for them, and re-layouts: 5.66 us -> 0.01 us
    all_to_all x1 -> x2, blocking collectives: 23.1 us -> 58.3 us  [exchanged(): return lax.all_to_all(buffer, LINE, 0, 0, tiled=True)]
    all_to_all x3 -> x1, waiting for transfers between devices: 24.1 us -> 0.01 us  [level(): got = lax.all_to_all(spread, ('geo', 'sub'), 0, 0, tiled=True)]
    all_to_all x3 -> x1, starting transfers between devices: 28.3 us -> 5.58 us  [level(): got = lax.all_to_all(spread, ('geo', 'sub'), 0, 0, tiled=True)]
    all_to_all x1, blocking collectives: 12.1 us -> 16.3 us  [level(): got = lax.all_to_all(local, 'region', 0, 0, tiled=True)]
    ppermute x8, waiting for transfers between devices: 0.87 us -> 2.94 us  [shifted(): return lax.ppermute(value, LINE, pairs)]
    squeeze x5 -> x0, local copies, waits for them, and re-layouts: 1.66 us -> none  [the longest x1 0.77 us: level(): cols = tile_cols[0]]
    pallas_call x11 -> x13, Pallas kernels: 25.2 us -> 26.4 us  [call(): pl.pallas_call(body, out_shape=tuple((jax.ShapeDtypeStruct(s, d) for s, d...]
  transfers between devices with their start and end apart: 11 -> 9, of which waited for: 3 -> 3; matrix products, arithmetic and copies ran while one was open for 2% -> 0% of each run, Pallas kernels for 3% -> 4%
where the time goes in v5:
time: 143 us; the launch traced here: 140 us
  blocking collectives  74.6 us (52%)
  starting transfers between devices  34.3 us (24%)
  Pallas kernels  26.4 us (18%)
  waiting for transfers between devices  2.94 us (2%)
    all_to_all x2, blocking collectives, exchanged(): return lax.all_to_all(buffer, LINE, 0, 0, tiled=True)  58.3 us
    ppermute x8, starting transfers between devices, shifted(): return lax.ppermute(value, LINE, pairs)  28.7 us
    pallas_call x13, Pallas kernels, call(): pl.pallas_call(body, out_shape=tuple((jax.ShapeDtypeStruct(s, d) for s, d...  26.4 us
    all_to_all x1, blocking collectives, level(): got = lax.all_to_all(local, 'region', 0, 0, tiled=True)  16.3 us
    all_to_all x1, starting transfers between devices, level(): got = lax.all_to_all(spread, ('geo', 'sub'), 0, 0, tiled=True)  5.58 us
    ppermute x8, waiting for transfers between devices, shifted(): return lax.ppermute(value, LINE, pairs)  2.94 us
  transfers between devices with their start and end apart: 9, of which 3 were waited for; matrix products, arithmetic and copies ran while one was open for 0% of the time, Pallas kernels for 4%

profile of v5, /device:TPU:1, one launch (start us, length us, event | category | flops | bytes accessed | tf_op | source)
XLA Modules:
  0.0 140.1 jit_solution(8695719739967904627)
XLA Ops:
  0.6 0.0 copy-start.2
  0.6 3.2 %shard_map.138 = (bf16[64,128]{1,0:T(8,128)(2,1)S(1)}, bf16[64,128]{1,0:T(8,128)(2,1)S(1)}, f32[32,2048]{1,0:T(8,128)S(1)}, bf16[64,128,128]{2,1,0:T(8,128)(2,1)S(1)}) custom-call(s32[4,16]{1,0:T(4,128)} %bitcast.25, bf16[64,128,128]{2,1,0:T(8,128)(2,1)} %bitcast.23, bf16[32,2048]{1,0:T(8,128)(2,1)} %bitcast.13.f, bf16[32,2048]{1,0:T(8,128)(2,1)} %bitcast.14.g), custom_call_target="tpu_custom_call" | custom-call | flops 67108864 | bytes 2359552 | tf_op jit(solution)/shard_map/pallas_call | solution.py:30
  3.9 0.0 copy-start.3
  3.9 3.9 %collective-permute-start.8 = (bf16[64,128]{1,0:T(8,128)(2,1)S(1)}, bf16[64,128]{1,0:T(8,128)(2,1)S(1)}, u32[]{:S(2)}, u32[]{:S(2)}) collective-permute-start(bf16[64,128]{1,0:T(8,128)(2,1)S(1)} %get-tuple-element.246), channel_id=1, source_target_pairs={{0,1},{1,2},{2,3},{3,4},{4,5},{5,6},{6,7},{7,8},{8,9},{9,10},{10,1... | collective-permute-start | bytes 49160 | tf_op jit(solution)/shard_map/ppermute | solution.py:75
  7.8 3.7 %collective-permute-start.9 = (bf16[64,128]{1,0:T(8,128)(2,1)S(1)}, bf16[64,128]{1,0:T(8,128)(2,1)S(1)}, u32[]{:S(2)}, u32[]{:S(2)}) collective-permute-start(bf16[64,128]{1,0:T(8,128)(2,1)S(1)} %get-tuple-element.247), channel_id=1, source_target_pairs={{1,0},{2,1},{3,2},{4,3},{5,4},{6,5},{7,6},{8,7},{9,8},{10,9},{11,1... | collective-permute-start | bytes 49160 | tf_op jit(solution)/shard_map/ppermute | solution.py:75
  11.6 0.0 collective-permute-done.8.up
  11.6 0.8 collective-permute-done.9.down
  12.5 0.0 copy-done.2
  12.5 2.1 %shard_map.139 = (bf16[32,2048]{1,0:T(8,128)(2,1)S(1)}, bf16[32,2048]{1,0:T(8,128)(2,1)S(1)}, bf16[64,128]{1,0:T(8,128)(2,1)S(1)}, bf16[64,128]{1,0:T(8,128)(2,1)S(1)}, f32[32,2048]{1,0:T(8,128)S(1)}) custom-call(s32[4,16]{1,0:T(4,128)S(1)} %bitcast.26, bf16[64,128,128]{2,1,0:T(8,128)(2,1)S(1)} %get-tuple-element.245.tiles, bf16[32,2048]{1,0:T(8,128)(2,1)} %bitcast.13.f, ...), custom_call_target="tpu_custom_call" | custom-call | flops 134217728 | bytes 2523392 | tf_op jit(solution)/shard_map/pallas_call | solution.py:30
  14.6 3.0 %collective-permute-start.10 = (bf16[64,128]{1,0:T(8,128)(2,1)S(1)}, bf16[64,128]{1,0:T(8,128)(2,1)S(1)}, u32[]{:S(2)}, u32[]{:S(2)}) collective-permute-start(bf16[64,128]{1,0:T(8,128)(2,1)S(1)} %get-tuple-element.251), channel_id=1, source_target_pairs={{0,1},{1,2},{2,3},{3,4},{4,5},{5,6},{6,7},{7,8},{8,9},{9,10},{10,1... | collective-permute-start | bytes 49160 | tf_op jit(solution)/shard_map/ppermute | solution.py:75
  17.6 4.3 %collective-permute-start.11 = (bf16[64,128]{1,0:T(8,128)(2,1)S(1)}, bf16[64,128]{1,0:T(8,128)(2,1)S(1)}, u32[]{:S(2)}, u32[]{:S(2)}) collective-permute-start(bf16[64,128]{1,0:T(8,128)(2,1)S(1)} %get-tuple-element.252), channel_id=1, source_target_pairs={{1,0},{2,1},{3,2},{4,3},{5,4},{6,5},{7,6},{8,7},{9,8},{10,9},{11,1... | collective-permute-start | bytes 49160 | tf_op jit(solution)/shard_map/ppermute | solution.py:75
  21.9 1.0 shard_map.141
  22.9 1.0 shard_map.140
  23.9 0.0 collective-permute-done.10.up
  23.9 0.0 collective-permute-done.11.down
  23.9 0.0 copy-done.3
  23.9 3.3 %shard_map.142 = (bf16[32,2048]{1,0:T(8,128)(2,1)S(1)}, bf16[32,2048]{1,0:T(8,128)(2,1)S(1)}, bf16[64,40,128]{2,1,0:T(8,128)(2,1)S(1)}) custom-call(s32[4,16]{1,0:T(4,128)S(1)} %bitcast.27, bf16[64,128,128]{2,1,0:T(8,128)(2,1)S(1)} %get-tuple-element.245.tiles, bf16[32,2048]{1,0:T(8,128)(2,1)} %bitcast.13.f, bf16[32,2048]{1,0:T(8,128)(2,1)} %bitcast.14.g, ...), custom_call_target="tpu_custom_call" | custom-call | flops 268435456 | bytes 2974080 | tf_op jit(solution)/shard_map/pallas_call | solution.py:30
  27.2 35.2 %all_to_all.51.got = bf16[64,40,128]{2,1,0:T(8,128)(2,1)S(1)} all-to-all(bf16[64,40,128]{2,1,0:T(8,128)(2,1)S(1)} %get-tuple-element.260), channel_id=1, replica_groups=mesh['geo'=4,'region'=16,'sub'=4] {'region','sub'}, dimensions={0} | all-to-all | bytes 1310720 | tf_op jit(solution)/shard_map/all_to_all | solution.py:563
  62.5 5.7 %shard_map.143 = (bf16[64,32,128]{2,1,0:T(8,128)(2,1)S(1)}, f32[64,32]{1,0:T(8,128)S(1)}) custom-call(bf16[64,40,128]{2,1,0:T(8,128)(2,1)S(1)} %all_to_all.51.got, bf16[32,32]{1,0:T(8,128)(2,1)S(1)} %get-tuple-element.261.weight, bf16[32,32]{1,0:T(8,128)(2,1)S(1)} %get-tuple-element.262.weight_t, f32[32,1]{1,0:T(8,128)S(1)} %get-tuple-element.263.bias), custom_call_target="tpu_custom_call" | custom-call | bytes 659584 | tf_op jit(solution)/shard_map/pallas_call | solution.py:30
  68.1 23.1 %all_to_all.52.back = bf16[64,32,128]{2,1,0:T(8,128)(2,1)S(1)} all-to-all(bf16[64,32,128]{2,1,0:T(8,128)(2,1)S(1)} %get-tuple-element.264), channel_id=1, replica_groups=mesh['geo'=4,'region'=16,'sub'=4] {'region','sub'}, dimensions={0} | all-to-all | bytes 1048576 | tf_op jit(solution)/shard_map/all_to_all | solution.py:563
  91.2 1.4 shard_map.144.lifted
  92.6 2.1 %shard_map.145 = (bf16[32,2048]{1,0:T(8,128)(2,1)S(1)}, bf16[32,2048]{1,0:T(8,128)(2,1)S(1)}, bf16[64,128]{1,0:T(8,128)(2,1)S(1)}, bf16[64,128]{1,0:T(8,128)(2,1)S(1)}, f32[32,2048]{1,0:T(8,128)S(1)}) custom-call(s32[4,16]{1,0:T(4,128)S(1)} %bitcast.28, bf16[64,128,128]{2,1,0:T(8,128)(2,1)S(1)} %get-tuple-element.245.tiles, ...), custom_call_target="tpu_custom_call" | custom-call | flops 67108864 | bytes 3166592 | tf_op jit(solution)/shard_map/pallas_call | solution.py:30
  94.7 1.4 %shard_map.148 = bf16[16,64,128]{2,1,0:T(8,128)(2,1)S(1)} custom-call(bf16[32,2048]{1,0:T(8,128)(2,1)S(1)} %get-tuple-element.267.f.merged, bf16[32,2048]{1,0:T(8,128)(2,1)S(1)} %get-tuple-element.268.g.pre_grad, bf16[32,2048]{1,0:T(8,128)(2,1)} %bitcast.13.f, bf16[32,2048]{1,0:T(8,128)(2,1)S(1)} %get-tuple-element.249.f1, ...), custom_call_target="tpu_custom_call" | custom-call | flops 67108864 | bytes 1060864 | tf_op jit(solution)/shard_map/pallas_call | solution.py:30
  96.2 16.3 %all_to_all.53.got = bf16[16,64,128]{2,1,0:T(8,128)(2,1)S(1)} all-to-all(bf16[16,64,128]{2,1,0:T(8,128)(2,1)S(1)} %shard_map.148), channel_id=1, replica_groups=mesh['geo'=4,'region'=16,'sub'=4] {'region'}, dimensions={0} | all-to-all | bytes 524288 | tf_op jit(solution)/shard_map/all_to_all | solution.py:778
  112.4 0.8 shard_map.149
  113.2 5.6 %all-to-all-start.9 = ((bf16[16,64,128]{2,1,0:T(8,128)(2,1)}), bf16[16,64,128]{2,1,0:T(8,128)(2,1)S(1)}, u32[]{:S(2)}, u32[]{:S(2)}) async-start(bf16[16,64,128]{2,1,0:T(8,128)(2,1)} %shard_map.149), calls=%async_computation.9 | async-start | bytes 524288 | tf_op jit(solution)/shard_map/all_to_all | solution.py:781
  118.8 3.3 %collective-permute-start.12 = (bf16[64,128]{1,0:T(8,128)(2,1)S(1)}, bf16[64,128]{1,0:T(8,128)(2,1)S(1)}, u32[]{:S(2)}, u32[]{:S(2)}) collective-permute-start(bf16[64,128]{1,0:T(8,128)(2,1)S(1)} %get-tuple-element.269), channel_id=1, source_target_pairs={{0,1},{1,2},{2,3},{3,4},{4,5},{5,6},{6,7},{7,8},{8,9},{9,10},{10,1... | collective-permute-start | bytes 49160 | tf_op jit(solution)/shard_map/ppermute | solution.py:75
  122.0 3.5 %collective-permute-start.13 = (bf16[64,128]{1,0:T(8,128)(2,1)S(1)}, bf16[64,128]{1,0:T(8,128)(2,1)S(1)}, u32[]{:S(2)}, u32[]{:S(2)}) collective-permute-start(bf16[64,128]{1,0:T(8,128)(2,1)S(1)} %get-tuple-element.270), channel_id=1, source_target_pairs={{1,0},{2,1},{3,2},{4,3},{5,4},{6,5},{7,6},{8,7},{9,8},{10,9},{11,1... | collective-permute-start | bytes 49160 | tf_op jit(solution)/shard_map/ppermute | solution.py:75
  125.6 0.0 collective-permute-done.12.up
  125.6 1.2 collective-permute-done.13.down
  126.8 1.8 %shard_map.146 = (bf16[32,2048]{1,0:T(8,128)(2,1)S(1)}, bf16[32,2048]{1,0:T(8,128)(2,1)S(1)}, bf16[64,128]{1,0:T(8,128)(2,1)S(1)}, bf16[64,128]{1,0:T(8,128)(2,1)S(1)}, f32[32,2048]{1,0:T(8,128)S(1)}) custom-call(s32[4,16]{1,0:T(4,128)S(1)} %bitcast.29, bf16[64,128,128]{2,1,0:T(8,128)(2,1)S(1)} %get-tuple-element.245.tiles, ...), custom_call_target="tpu_custom_call" | custom-call | flops 134217728 | bytes 2523392 | tf_op jit(solution)/shard_map/pallas_call | solution.py:30
  128.6 3.1 %collective-permute-start.14 = (bf16[64,128]{1,0:T(8,128)(2,1)S(1)}, bf16[64,128]{1,0:T(8,128)(2,1)S(1)}, u32[]{:S(2)}, u32[]{:S(2)}) collective-permute-start(bf16[64,128]{1,0:T(8,128)(2,1)S(1)} %get-tuple-element.274), channel_id=1, source_target_pairs={{0,1},{1,2},{2,3},{3,4},{4,5},{5,6},{6,7},{7,8},{8,9},{9,10},{10,1... | collective-permute-start | bytes 49160 | tf_op jit(solution)/shard_map/ppermute | solution.py:75
  131.7 3.8 %collective-permute-start.15 = (bf16[64,128]{1,0:T(8,128)(2,1)S(1)}, bf16[64,128]{1,0:T(8,128)(2,1)S(1)}, u32[]{:S(2)}, u32[]{:S(2)}) collective-permute-start(bf16[64,128]{1,0:T(8,128)(2,1)S(1)} %get-tuple-element.275), channel_id=1, source_target_pairs={{1,0},{2,1},{3,2},{4,3},{5,4},{6,5},{7,6},{8,7},{9,8},{10,9},{11,1... | collective-permute-start | bytes 49160 | tf_op jit(solution)/shard_map/ppermute | solution.py:75
  135.5 0.0 collective-permute-done.14.up
  135.5 0.8 collective-permute-done.15.down
  136.4 1.9 %shard_map.147 = (bf16[32,2048]{1,0:T(8,128)(2,1)}, bf16[32,2048]{1,0:T(8,128)(2,1)}) custom-call(s32[4,16]{1,0:T(4,128)S(1)} %bitcast.30, bf16[64,128,128]{2,1,0:T(8,128)(2,1)S(1)} %get-tuple-element.245.tiles, bf16[32,2048]{1,0:T(8,128)(2,1)S(1)} %get-tuple-element.267.f.merged, bf16[32,2048]{1,0:T(8,128)(2,1)S(1)} %get-tuple-element.268.g.pre_grad, ...), custom_call_target="tpu_custom_call" | custom-call | flops 134217728 | bytes 2928896 | tf_op jit(solution)/shard_map/pallas_call | solution.py:30
  138.3 0.0 all-to-all-done.9.got
  138.3 0.8 shard_map.150
  139.1 0.8 while.33
Async XLA Ops:
  0.6 11.8 %copy-start.2 = (s32[1,16,4]{1,2,0:T(4,128)S(1)}, s32[1,16,4]{1,2,0:T(4,128)}, u32[]{:S(2)}) copy-start(s32[1,16,4]{1,2,0:T(4,128)} %param.19) | copy-start | bytes 772
  3.9 20.0 %copy-start.3 = (f32[1,2048]{1,0:T(1,128)S(1)}, f32[1,2048]{1,0:T(1,128)}, u32[]{:S(2)}) copy-start(f32[1,2048]{1,0:T(1,128)} %pool.3) | copy-start | bytes 24580
  3.9 7.7 %collective-permute-start.8 = (bf16[64,128]{1,0:T(8,128)(2,1)S(1)}, bf16[64,128]{1,0:T(8,128)(2,1)S(1)}, u32[]{:S(2)}, u32[]{:S(2)}) collective-permute-start(bf16[64,128]{1,0:T(8,128)(2,1)S(1)} %get-tuple-element.246), channel_id=1, source_target_pairs={{0,1},{1,2},{2,3},{3,4},{4,5},{5,6},{6,7},{7,8},{8,9},{9,10},{10,1... | collective-permute-start | bytes 49160 | tf_op jit(solution)/shard_map/ppermute | solution.py:75
  7.8 4.6 %collective-permute-start.9 = (bf16[64,128]{1,0:T(8,128)(2,1)S(1)}, bf16[64,128]{1,0:T(8,128)(2,1)S(1)}, u32[]{:S(2)}, u32[]{:S(2)}) collective-permute-start(bf16[64,128]{1,0:T(8,128)(2,1)S(1)} %get-tuple-element.247), channel_id=1, source_target_pairs={{1,0},{2,1},{3,2},{4,3},{5,4},{6,5},{7,6},{8,7},{9,8},{10,9},{11,1... | collective-permute-start | bytes 49160 | tf_op jit(solution)/shard_map/ppermute | solution.py:75
  14.6 9.3 %collective-permute-start.10 = (bf16[64,128]{1,0:T(8,128)(2,1)S(1)}, bf16[64,128]{1,0:T(8,128)(2,1)S(1)}, u32[]{:S(2)}, u32[]{:S(2)}) collective-permute-start(bf16[64,128]{1,0:T(8,128)(2,1)S(1)} %get-tuple-element.251), channel_id=1, source_target_pairs={{0,1},{1,2},{2,3},{3,4},{4,5},{5,6},{6,7},{7,8},{8,9},{9,10},{10,1... | collective-permute-start | bytes 49160 | tf_op jit(solution)/shard_map/ppermute | solution.py:75
  17.6 6.4 %collective-permute-start.11 = (bf16[64,128]{1,0:T(8,128)(2,1)S(1)}, bf16[64,128]{1,0:T(8,128)(2,1)S(1)}, u32[]{:S(2)}, u32[]{:S(2)}) collective-permute-start(bf16[64,128]{1,0:T(8,128)(2,1)S(1)} %get-tuple-element.252), channel_id=1, source_target_pairs={{1,0},{2,1},{3,2},{4,3},{5,4},{6,5},{7,6},{8,7},{9,8},{10,9},{11,1... | collective-permute-start | bytes 49160 | tf_op jit(solution)/shard_map/ppermute | solution.py:75
  113.2 25.1 %all-to-all-start.9 = ((bf16[16,64,128]{2,1,0:T(8,128)(2,1)}), bf16[16,64,128]{2,1,0:T(8,128)(2,1)S(1)}, u32[]{:S(2)}, u32[]{:S(2)}) async-start(bf16[16,64,128]{2,1,0:T(8,128)(2,1)} %shard_map.149), calls=%async_computation.9 | async-start | bytes 524288 | tf_op jit(solution)/shard_map/all_to_all | solution.py:781
  118.8 6.8 %collective-permute-start.12 = (bf16[64,128]{1,0:T(8,128)(2,1)S(1)}, bf16[64,128]{1,0:T(8,128)(2,1)S(1)}, u32[]{:S(2)}, u32[]{:S(2)}) collective-permute-start(bf16[64,128]{1,0:T(8,128)(2,1)S(1)} %get-tuple-element.269), channel_id=1, source_target_pairs={{0,1},{1,2},{2,3},{3,4},{4,5},{5,6},{6,7},{7,8},{8,9},{9,10},{10,1... | collective-permute-start | bytes 49160 | tf_op jit(solution)/shard_map/ppermute | solution.py:75
  122.0 4.8 %collective-permute-start.13 = (bf16[64,128]{1,0:T(8,128)(2,1)S(1)}, bf16[64,128]{1,0:T(8,128)(2,1)S(1)}, u32[]{:S(2)}, u32[]{:S(2)}) collective-permute-start(bf16[64,128]{1,0:T(8,128)(2,1)S(1)} %get-tuple-element.270), channel_id=1, source_target_pairs={{1,0},{2,1},{3,2},{4,3},{5,4},{6,5},{7,6},{8,7},{9,8},{10,9},{11,1... | collective-permute-start | bytes 49160 | tf_op jit(solution)/shard_map/ppermute | solution.py:75
  128.6 6.9 %collective-permute-start.14 = (bf16[64,128]{1,0:T(8,128)(2,1)S(1)}, bf16[64,128]{1,0:T(8,128)(2,1)S(1)}, u32[]{:S(2)}, u32[]{:S(2)}) collective-permute-start(bf16[64,128]{1,0:T(8,128)(2,1)S(1)} %get-tuple-element.274), channel_id=1, source_target_pairs={{0,1},{1,2},{2,3},{3,4},{4,5},{5,6},{6,7},{7,8},{8,9},{9,10},{10,1... | collective-permute-start | bytes 49160 | tf_op jit(solution)/shard_map/ppermute | solution.py:75
  131.7 4.7 %collective-permute-start.15 = (bf16[64,128]{1,0:T(8,128)(2,1)S(1)}, bf16[64,128]{1,0:T(8,128)(2,1)S(1)}, u32[]{:S(2)}, u32[]{:S(2)}) collective-permute-start(bf16[64,128]{1,0:T(8,128)(2,1)S(1)} %get-tuple-element.275), channel_id=1, source_target_pairs={{1,0},{2,1},{3,2},{4,3},{5,4},{6,5},{7,6},{8,7},{9,8},{10,9},{11,1... | collective-permute-start | bytes 49160 | tf_op jit(solution)/shard_map/ppermute | solution.py:75

commit v6 on v5

--- a/solution.py
+++ b/solution.py
@@ -127,15 +127,24 @@
 
 
 def start_body(
-    cols, tiles_h, f, g, up, down, inner, tiles, ext, sems, *, chans, count, nonzero, compact
+    cols, tiles_h, f_h, g_h, up, down, inner, tiles, ext, g, edges, sems,
+    *, chans, count, nonzero, compact
 ):
     pieces = 4 if count % 4 == 0 else 1
     size = count // pieces
+    ends = [slice(0, LANES), slice((count - 1) * LANES, count * LANES)]
+    others = [pltpu.make_async_copy(g_h, g, sems.at[pieces])]
+    for i, at in enumerate(ends):
+        others.append(pltpu.make_async_copy(f_h.at[:, at], edges.at[i], sems.at[pieces + 1 + i]))
+    for c in others:
+        c.start()
     copies = []
     for i in range(pieces):
         at = slice(i * size * nonzero, (i + 1) * size * nonzero)
         copies.append(pltpu.make_async_copy(tiles_h.at[at], tiles.at[at], sems.at[i]))
         copies[-1].start()
+    for c in others:
+        c.wait()
     if compact:
         for c in copies:
             c.wait()
@@ -146,7 +155,7 @@
         return tile(g, k)
 
     add_transposed(cols, tiles, grad_of, ext, count, nonzero, compact)
-    write_sends(up, down, tile(f, 0), tile(f, count - 1), ext, chans, count)
+    write_sends(up, down, edges[0], edges[1], ext, chans, count)
 
     def one(k):
         inner[:, lanes(k)] = ext[k + 1]
@@ -327,7 +336,7 @@
     lax.fori_loop(0, rows // width, select, 0, unroll=1 if compact else rows // width)
 
 
-def coarse_hot(got, hot, masked, *, chans, peers, cap, parts):
+def coarse_hot(got, hot, masked, *, chans, peers, cap, parts, compact):
     wide = 2 * cap
 
     def one(p, carry):
@@ -344,7 +353,7 @@
                 ).astype(BF)
         return carry
 
-    lax.fori_loop(0, peers, one, 0, unroll=4)
+    lax.fori_loop(0, peers, one, 0, unroll=4 if compact else 16)
 
 
 def coarse_totals(hot, masked, chans, parts):
@@ -372,7 +381,7 @@
     return out, dot(weight_t[...], mid_grad).astype(BF)
 
 
-def coarse_gather(back, got, hot, out, behind, *, chans, peers, cap, parts):
+def coarse_gather(back, got, hot, out, behind, *, chans, peers, cap, parts, compact):
     wide = 2 * cap
     stacked = [
         jnp.concatenate(
@@ -399,7 +408,7 @@
             back[p] = total.astype(BF)
         return carry
 
-    lax.fori_loop(0, peers // step, one, 0, unroll=2)
+    lax.fori_loop(0, peers // step, one, 0, unroll=1 if compact else peers // step)
 
 
 def coarse_body(got, weight, weight_t, bias, back, grads, hot, masked, **sizes):
@@ -499,6 +508,22 @@
         inner[:, lanes(k)] = ext[k + 1]
 
     each(count, one, compact)
+
+
+def joined_body(
+    cols, tiles, back, dest, rank, f, f1, f2, g, g1, g2, pool, mix_in, mix_out_t, bias,
+    merged, pre_grad, up, down, inner, ext, lifted, big, hot,
+    *, chans, count, nonzero, compact, peers, cap, go, rows
+):
+    unpack_body(
+        (0,), back, dest, rank, lifted, big, hot,
+        chans=chans, peers=peers, cap=cap, go=go, rows=rows, compact=compact,
+    )
+    second_start_body(
+        cols, tiles, lifted, f, f1, f2, g, g1, g2, pool, mix_in, mix_out_t, bias,
+        merged, pre_grad, up, down, inner, ext,
+        chans=chans, count=count, nonzero=nonzero, compact=compact,
+    )
 
 
 def weights_body(merged, pre_grad, f, f1, f2, g, g1, g2, mid, most, local, *, chans, cap):
@@ -605,7 +630,7 @@
     pool = pool_weight
     line = dict(chans=chans, count=count, nonzero=nonzero, compact=several)
     ways = dict(chans=chans, peers=peers, cap=cap, go=go, rows=rows, compact=several)
-    sizes = dict(chans=chans, peers=peers, cap=cap, parts=parts)
+    sizes = dict(chans=chans, peers=peers, cap=cap, parts=parts, compact=several)
     full = (chans, rows)
     halo = (2 * chans, LANES)
     ext = pltpu.VMEM((count + 2, chans, LANES), F32)
@@ -649,10 +674,15 @@
     up, down, inner, tiles = call(
         functools.partial(start_body, **line),
         [(halo, BF), (halo, BF), (full, F32), (tiles.shape, BF)],
-        [ext, pltpu.SemaphoreType.DMA((4,))],
+        [
+            ext,
+            pltpu.VMEM(full, BF),
+            pltpu.VMEM((2, chans, LANES), BF),
+            pltpu.SemaphoreType.DMA((7,)),
+        ],
         (cols, tiles, f, g),
         smem=1,
-        far=(1,),
+        far=(1, 2, 3),
         limit=START_LIMIT,
         flops=work,
     )
@@ -743,13 +773,20 @@
             (got, mid_w, mid_t, bias_mid),
             limit=32,
         )
-        lifted = unpacked(exchanged(back), jnp.zeros((1,), I32))
-
+        back = exchanged(back)
+
+    body, first, extra = functools.partial(second_start_body, **line), [], []
+    if several:
+        first = [lifted]
+    else:
+        body = functools.partial(joined_body, **line, peers=peers, cap=cap, go=go, rows=rows)
+        first = [back, dest, rank]
+        extra = [pltpu.VMEM((2 * chans, rows), BF), *lift_s]
     merged, pre_grad, up, down, inner = call(
-        functools.partial(second_start_body, **line),
+        body,
         [(full, BF), (full, BF), (halo, BF), (halo, BF), (full, F32)],
-        [ext],
-        (cols, tiles, lifted, f, f1, f2, g, g1, g2, pool, *mixes),
+        [ext, *extra],
+        (cols, tiles, *first, f, f1, f2, g, g1, g2, pool, *mixes),
         smem=1,
         flops=work,
     )

time: 143 us -> 142 us (level)
    pallas_call x13 -> x12, Pallas kernels: 26.4 us -> 26.2 us  [call(): pl.pallas_call(body, out_shape=tuple((jax.ShapeDtypeStruct(s, d) for s, d...]
where the time goes in v6:
time: 142 us; the launch traced here: 140 us
  blocking collectives  74.6 us (53%)
  starting transfers between devices  34.3 us (24%)
  Pallas kernels  26.2 us (18%)
  waiting for transfers between devices  2.94 us (2%)
    all_to_all x2, blocking collectives, exchanged(): return lax.all_to_all(buffer, LINE, 0, 0, tiled=True)  58.3 us
    ppermute x8, starting transfers between devices, shifted(): return lax.ppermute(value, LINE, pairs)  28.7 us
    pallas_call x12, Pallas kernels, call(): pl.pallas_call(body, out_shape=tuple((jax.ShapeDtypeStruct(s, d) for s, d...  26.2 us
    all_to_all x1, blocking collectives, level(): got = lax.all_to_all(local, 'region', 0, 0, tiled=True)  16.3 us
    all_to_all x1, starting transfers between devices, level(): got = lax.all_to_all(spread, ('geo', 'sub'), 0, 0, tiled=True)  5.57 us
    ppermute x8, waiting for transfers between devices, shifted(): return lax.ppermute(value, LINE, pairs)  2.94 us
  transfers between devices with their start and end apart: 9, of which 3 were waited for; matrix products, arithmetic and copies ran while one was open for 0% of the time, Pallas kernels for 4%

profile of v6, /device:TPU:1, one launch (start us, length us, event | category | flops | bytes accessed | tf_op | source)
XLA Modules:
  0.0 139.8 jit_solution(11185402124386384006)
XLA Ops:
  0.6 0.0 copy-start.2
  0.6 3.2 %shard_map.138 = (bf16[64,128]{1,0:T(8,128)(2,1)S(1)}, bf16[64,128]{1,0:T(8,128)(2,1)S(1)}, f32[32,2048]{1,0:T(8,128)S(1)}, bf16[64,128,128]{2,1,0:T(8,128)(2,1)S(1)}) custom-call(s32[4,16]{1,0:T(4,128)} %bitcast.25, bf16[64,128,128]{2,1,0:T(8,128)(2,1)} %bitcast.23, bf16[32,2048]{1,0:T(8,128)(2,1)} %bitcast.13.f_h.f, bf16[32,2048]{1,0:T(8,128)(2,1)} %bitcast.14.g_h.g), custom_call_target="tpu_custom_call" | custom-call | flops 67108864 | bytes 2359552 | tf_op jit(solution)/shard_map/pallas_call | solution.py:30
  3.9 0.0 copy-start.3
  3.9 3.9 %collective-permute-start.8 = (bf16[64,128]{1,0:T(8,128)(2,1)S(1)}, bf16[64,128]{1,0:T(8,128)(2,1)S(1)}, u32[]{:S(2)}, u32[]{:S(2)}) collective-permute-start(bf16[64,128]{1,0:T(8,128)(2,1)S(1)} %get-tuple-element.246), channel_id=1, source_target_pairs={{0,1},{1,2},{2,3},{3,4},{4,5},{5,6},{6,7},{7,8},{8,9},{9,10},{10,1... | collective-permute-start | bytes 49160 | tf_op jit(solution)/shard_map/ppermute | solution.py:75
  7.8 3.7 %collective-permute-start.9 = (bf16[64,128]{1,0:T(8,128)(2,1)S(1)}, bf16[64,128]{1,0:T(8,128)(2,1)S(1)}, u32[]{:S(2)}, u32[]{:S(2)}) collective-permute-start(bf16[64,128]{1,0:T(8,128)(2,1)S(1)} %get-tuple-element.247), channel_id=1, source_target_pairs={{1,0},{2,1},{3,2},{4,3},{5,4},{6,5},{7,6},{8,7},{9,8},{10,9},{11,1... | collective-permute-start | bytes 49160 | tf_op jit(solution)/shard_map/ppermute | solution.py:75
  11.6 0.0 collective-permute-done.8.up
  11.6 0.8 collective-permute-done.9.down
  12.4 0.0 copy-done.2
  12.4 2.1 %shard_map.139 = (bf16[32,2048]{1,0:T(8,128)(2,1)S(1)}, bf16[32,2048]{1,0:T(8,128)(2,1)S(1)}, bf16[64,128]{1,0:T(8,128)(2,1)S(1)}, bf16[64,128]{1,0:T(8,128)(2,1)S(1)}, f32[32,2048]{1,0:T(8,128)S(1)}) custom-call(s32[4,16]{1,0:T(4,128)S(1)} %bitcast.26, bf16[64,128,128]{2,1,0:T(8,128)(2,1)S(1)} %get-tuple-element.245.tiles, bf16[32,2048]{1,0:T(8,128)(2,1)} %bitcast.13.f_h.f, ...), custom_call_target="tpu_custom_call" | custom-call | flops 134217728 | bytes 2523392 | tf_op jit(solution)/shard_map/pallas_call | solution.py:30
  14.5 3.0 %collective-permute-start.10 = (bf16[64,128]{1,0:T(8,128)(2,1)S(1)}, bf16[64,128]{1,0:T(8,128)(2,1)S(1)}, u32[]{:S(2)}, u32[]{:S(2)}) collective-permute-start(bf16[64,128]{1,0:T(8,128)(2,1)S(1)} %get-tuple-element.251), channel_id=1, source_target_pairs={{0,1},{1,2},{2,3},{3,4},{4,5},{5,6},{6,7},{7,8},{8,9},{9,10},{10,1... | collective-permute-start | bytes 49160 | tf_op jit(solution)/shard_map/ppermute | solution.py:75
  17.6 4.3 %collective-permute-start.11 = (bf16[64,128]{1,0:T(8,128)(2,1)S(1)}, bf16[64,128]{1,0:T(8,128)(2,1)S(1)}, u32[]{:S(2)}, u32[]{:S(2)}) collective-permute-start(bf16[64,128]{1,0:T(8,128)(2,1)S(1)} %get-tuple-element.252), channel_id=1, source_target_pairs={{1,0},{2,1},{3,2},{4,3},{5,4},{6,5},{7,6},{8,7},{9,8},{10,9},{11,1... | collective-permute-start | bytes 49160 | tf_op jit(solution)/shard_map/ppermute | solution.py:75
  21.9 1.0 shard_map.141
  22.9 1.0 shard_map.140
  23.9 0.0 collective-permute-done.10.up
  23.9 0.0 collective-permute-done.11.down
  23.9 0.0 copy-done.3
  23.9 3.3 %shard_map.142 = (bf16[32,2048]{1,0:T(8,128)(2,1)S(1)}, bf16[32,2048]{1,0:T(8,128)(2,1)S(1)}, bf16[64,40,128]{2,1,0:T(8,128)(2,1)S(1)}) custom-call(s32[4,16]{1,0:T(4,128)S(1)} %bitcast.27, bf16[64,128,128]{2,1,0:T(8,128)(2,1)S(1)} %get-tuple-element.245.tiles, bf16[32,2048]{1,0:T(8,128)(2,1)} %bitcast.13.f_h.f, bf16[32,2048]{1,0:T(8,128)(2,1)} %bitcast.14.g_h.g, ...), custom_call_target="tpu_custom_call" | custom-call | flops 268435456 | bytes 2974080 | tf_op jit(solution)/shard_map/pallas_call | solution.py:30
  27.2 35.2 %all_to_all.51.got = bf16[64,40,128]{2,1,0:T(8,128)(2,1)S(1)} all-to-all(bf16[64,40,128]{2,1,0:T(8,128)(2,1)S(1)} %get-tuple-element.260), channel_id=1, replica_groups=mesh['geo'=4,'region'=16,'sub'=4] {'region','sub'}, dimensions={0} | all-to-all | bytes 1310720 | tf_op jit(solution)/shard_map/all_to_all | solution.py:588
  62.4 5.6 %shard_map.143 = (bf16[64,32,128]{2,1,0:T(8,128)(2,1)S(1)}, f32[64,32]{1,0:T(8,128)S(1)}) custom-call(bf16[64,40,128]{2,1,0:T(8,128)(2,1)S(1)} %all_to_all.51.got, bf16[32,32]{1,0:T(8,128)(2,1)S(1)} %get-tuple-element.261.weight, bf16[32,32]{1,0:T(8,128)(2,1)S(1)} %get-tuple-element.262.weight_t, f32[32,1]{1,0:T(8,128)S(1)} %get-tuple-element.263.bias), custom_call_target="tpu_custom_call" | custom-call | bytes 659584 | tf_op jit(solution)/shard_map/pallas_call | solution.py:30
  68.0 23.1 %all_to_all.52.back = bf16[64,32,128]{2,1,0:T(8,128)(2,1)S(1)} all-to-all(bf16[64,32,128]{2,1,0:T(8,128)(2,1)S(1)} %get-tuple-element.264), channel_id=1, replica_groups=mesh['geo'=4,'region'=16,'sub'=4] {'region','sub'}, dimensions={0} | all-to-all | bytes 1048576 | tf_op jit(solution)/shard_map/all_to_all | solution.py:588
  91.1 3.3 %shard_map.144 = (bf16[32,2048]{1,0:T(8,128)(2,1)S(1)}, bf16[32,2048]{1,0:T(8,128)(2,1)S(1)}, bf16[64,128]{1,0:T(8,128)(2,1)S(1)}, bf16[64,128]{1,0:T(8,128)(2,1)S(1)}, f32[32,2048]{1,0:T(8,128)S(1)}) custom-call(s32[4,16]{1,0:T(4,128)S(1)} %bitcast.28, bf16[64,128,128]{2,1,0:T(8,128)(2,1)S(1)} %get-tuple-element.245.tiles, ...), custom_call_target="tpu_custom_call" | custom-call | flops 67108864 | bytes 3445120 | tf_op jit(solution)/shard_map/pallas_call | solution.py:30
  94.5 1.4 %shard_map.147 = bf16[16,64,128]{2,1,0:T(8,128)(2,1)S(1)} custom-call(bf16[32,2048]{1,0:T(8,128)(2,1)S(1)} %get-tuple-element.267.f.merged, bf16[32,2048]{1,0:T(8,128)(2,1)S(1)} %get-tuple-element.268.g.pre_grad, bf16[32,2048]{1,0:T(8,128)(2,1)} %bitcast.13.f_h.f, bf16[32,2048]{1,0:T(8,128)(2,1)S(1)} %get-tuple-element.249.f1, ...), custom_call_target="tpu_custom_call" | custom-call | flops 67108864 | bytes 1060864 | tf_op jit(solution)/shard_map/pallas_call | solution.py:30
  95.9 16.3 %all_to_all.53.got = bf16[16,64,128]{2,1,0:T(8,128)(2,1)S(1)} all-to-all(bf16[16,64,128]{2,1,0:T(8,128)(2,1)S(1)} %shard_map.147), channel_id=1, replica_groups=mesh['geo'=4,'region'=16,'sub'=4] {'region'}, dimensions={0} | all-to-all | bytes 524288 | tf_op jit(solution)/shard_map/all_to_all | solution.py:815
  112.2 0.8 shard_map.148
  113.0 5.6 %all-to-all-start.9 = ((bf16[16,64,128]{2,1,0:T(8,128)(2,1)}), bf16[16,64,128]{2,1,0:T(8,128)(2,1)S(1)}, u32[]{:S(2)}, u32[]{:S(2)}) async-start(bf16[16,64,128]{2,1,0:T(8,128)(2,1)} %shard_map.148), calls=%async_computation.9 | async-start | bytes 524288 | tf_op jit(solution)/shard_map/all_to_all | solution.py:818
  118.5 3.3 %collective-permute-start.12 = (bf16[64,128]{1,0:T(8,128)(2,1)S(1)}, bf16[64,128]{1,0:T(8,128)(2,1)S(1)}, u32[]{:S(2)}, u32[]{:S(2)}) collective-permute-start(bf16[64,128]{1,0:T(8,128)(2,1)S(1)} %get-tuple-element.269), channel_id=1, source_target_pairs={{0,1},{1,2},{2,3},{3,4},{4,5},{5,6},{6,7},{7,8},{8,9},{9,10},{10,1... | collective-permute-start | bytes 49160 | tf_op jit(solution)/shard_map/ppermute | solution.py:75
  121.8 3.5 %collective-permute-start.13 = (bf16[64,128]{1,0:T(8,128)(2,1)S(1)}, bf16[64,128]{1,0:T(8,128)(2,1)S(1)}, u32[]{:S(2)}, u32[]{:S(2)}) collective-permute-start(bf16[64,128]{1,0:T(8,128)(2,1)S(1)} %get-tuple-element.270), channel_id=1, source_target_pairs={{1,0},{2,1},{3,2},{4,3},{5,4},{6,5},{7,6},{8,7},{9,8},{10,9},{11,1... | collective-permute-start | bytes 49160 | tf_op jit(solution)/shard_map/ppermute | solution.py:75
  125.3 0.0 collective-permute-done.12.up
  125.3 1.2 collective-permute-done.13.down
  126.6 1.8 %shard_map.145 = (bf16[32,2048]{1,0:T(8,128)(2,1)S(1)}, bf16[32,2048]{1,0:T(8,128)(2,1)S(1)}, bf16[64,128]{1,0:T(8,128)(2,1)S(1)}, bf16[64,128]{1,0:T(8,128)(2,1)S(1)}, f32[32,2048]{1,0:T(8,128)S(1)}) custom-call(s32[4,16]{1,0:T(4,128)S(1)} %bitcast.29, bf16[64,128,128]{2,1,0:T(8,128)(2,1)S(1)} %get-tuple-element.245.tiles, ...), custom_call_target="tpu_custom_call" | custom-call | flops 134217728 | bytes 2523392 | tf_op jit(solution)/shard_map/pallas_call | solution.py:30
  128.3 3.1 %collective-permute-start.14 = (bf16[64,128]{1,0:T(8,128)(2,1)S(1)}, bf16[64,128]{1,0:T(8,128)(2,1)S(1)}, u32[]{:S(2)}, u32[]{:S(2)}) collective-permute-start(bf16[64,128]{1,0:T(8,128)(2,1)S(1)} %get-tuple-element.274), channel_id=1, source_target_pairs={{0,1},{1,2},{2,3},{3,4},{4,5},{5,6},{6,7},{7,8},{8,9},{9,10},{10,1... | collective-permute-start | bytes 49160 | tf_op jit(solution)/shard_map/ppermute | solution.py:75
  131.4 3.8 %collective-permute-start.15 = (bf16[64,128]{1,0:T(8,128)(2,1)S(1)}, bf16[64,128]{1,0:T(8,128)(2,1)S(1)}, u32[]{:S(2)}, u32[]{:S(2)}) collective-permute-start(bf16[64,128]{1,0:T(8,128)(2,1)S(1)} %get-tuple-element.275), channel_id=1, source_target_pairs={{1,0},{2,1},{3,2},{4,3},{5,4},{6,5},{7,6},{8,7},{9,8},{10,9},{11,1... | collective-permute-start | bytes 49160 | tf_op jit(solution)/shard_map/ppermute | solution.py:75
  135.3 0.0 collective-permute-done.14.up
  135.3 0.8 collective-permute-done.15.down
  136.1 1.9 %shard_map.146 = (bf16[32,2048]{1,0:T(8,128)(2,1)}, bf16[32,2048]{1,0:T(8,128)(2,1)}) custom-call(s32[4,16]{1,0:T(4,128)S(1)} %bitcast.30, bf16[64,128,128]{2,1,0:T(8,128)(2,1)S(1)} %get-tuple-element.245.tiles, bf16[32,2048]{1,0:T(8,128)(2,1)S(1)} %get-tuple-element.267.f.merged, bf16[32,2048]{1,0:T(8,128)(2,1)S(1)} %get-tuple-element.268.g.pre_grad, ...), custom_call_target="tpu_custom_call" | custom-call | flops 134217728 | bytes 2928896 | tf_op jit(solution)/shard_map/pallas_call | solution.py:30
  138.1 0.0 all-to-all-done.9.got
  138.1 0.8 shard_map.149
  138.9 0.8 while.33
Async XLA Ops:
  0.6 11.8 %copy-start.2 = (s32[1,16,4]{1,2,0:T(4,128)S(1)}, s32[1,16,4]{1,2,0:T(4,128)}, u32[]{:S(2)}) copy-start(s32[1,16,4]{1,2,0:T(4,128)} %param.19) | copy-start | bytes 772
  3.9 20.0 %copy-start.3 = (f32[1,2048]{1,0:T(1,128)S(1)}, f32[1,2048]{1,0:T(1,128)}, u32[]{:S(2)}) copy-start(f32[1,2048]{1,0:T(1,128)} %pool.3) | copy-start | bytes 24580
  3.9 7.7 %collective-permute-start.8 = (bf16[64,128]{1,0:T(8,128)(2,1)S(1)}, bf16[64,128]{1,0:T(8,128)(2,1)S(1)}, u32[]{:S(2)}, u32[]{:S(2)}) collective-permute-start(bf16[64,128]{1,0:T(8,128)(2,1)S(1)} %get-tuple-element.246), channel_id=1, source_target_pairs={{0,1},{1,2},{2,3},{3,4},{4,5},{5,6},{6,7},{7,8},{8,9},{9,10},{10,1... | collective-permute-start | bytes 49160 | tf_op jit(solution)/shard_map/ppermute | solution.py:75
  7.8 4.6 %collective-permute-start.9 = (bf16[64,128]{1,0:T(8,128)(2,1)S(1)}, bf16[64,128]{1,0:T(8,128)(2,1)S(1)}, u32[]{:S(2)}, u32[]{:S(2)}) collective-permute-start(bf16[64,128]{1,0:T(8,128)(2,1)S(1)} %get-tuple-element.247), channel_id=1, source_target_pairs={{1,0},{2,1},{3,2},{4,3},{5,4},{6,5},{7,6},{8,7},{9,8},{10,9},{11,1... | collective-permute-start | bytes 49160 | tf_op jit(solution)/shard_map/ppermute | solution.py:75
  14.5 9.3 %collective-permute-start.10 = (bf16[64,128]{1,0:T(8,128)(2,1)S(1)}, bf16[64,128]{1,0:T(8,128)(2,1)S(1)}, u32[]{:S(2)}, u32[]{:S(2)}) collective-permute-start(bf16[64,128]{1,0:T(8,128)(2,1)S(1)} %get-tuple-element.251), channel_id=1, source_target_pairs={{0,1},{1,2},{2,3},{3,4},{4,5},{5,6},{6,7},{7,8},{8,9},{9,10},{10,1... | collective-permute-start | bytes 49160 | tf_op jit(solution)/shard_map/ppermute | solution.py:75
  17.6 6.3 %collective-permute-start.11 = (bf16[64,128]{1,0:T(8,128)(2,1)S(1)}, bf16[64,128]{1,0:T(8,128)(2,1)S(1)}, u32[]{:S(2)}, u32[]{:S(2)}) collective-permute-start(bf16[64,128]{1,0:T(8,128)(2,1)S(1)} %get-tuple-element.252), channel_id=1, source_target_pairs={{1,0},{2,1},{3,2},{4,3},{5,4},{6,5},{7,6},{8,7},{9,8},{10,9},{11,1... | collective-permute-start | bytes 49160 | tf_op jit(solution)/shard_map/ppermute | solution.py:75
  113.0 25.1 %all-to-all-start.9 = ((bf16[16,64,128]{2,1,0:T(8,128)(2,1)}), bf16[16,64,128]{2,1,0:T(8,128)(2,1)S(1)}, u32[]{:S(2)}, u32[]{:S(2)}) async-start(bf16[16,64,128]{2,1,0:T(8,128)(2,1)} %shard_map.148), calls=%async_computation.9 | async-start | bytes 524288 | tf_op jit(solution)/shard_map/all_to_all | solution.py:818
  118.5 6.8 %collective-permute-start.12 = (bf16[64,128]{1,0:T(8,128)(2,1)S(1)}, bf16[64,128]{1,0:T(8,128)(2,1)S(1)}, u32[]{:S(2)}, u32[]{:S(2)}) collective-permute-start(bf16[64,128]{1,0:T(8,128)(2,1)S(1)} %get-tuple-element.269), channel_id=1, source_target_pairs={{0,1},{1,2},{2,3},{3,4},{4,5},{5,6},{6,7},{7,8},{8,9},{9,10},{10,1... | collective-permute-start | bytes 49160 | tf_op jit(solution)/shard_map/ppermute | solution.py:75
  121.8 4.8 %collective-permute-start.13 = (bf16[64,128]{1,0:T(8,128)(2,1)S(1)}, bf16[64,128]{1,0:T(8,128)(2,1)S(1)}, u32[]{:S(2)}, u32[]{:S(2)}) collective-permute-start(bf16[64,128]{1,0:T(8,128)(2,1)S(1)} %get-tuple-element.270), channel_id=1, source_target_pairs={{1,0},{2,1},{3,2},{4,3},{5,4},{6,5},{7,6},{8,7},{9,8},{10,9},{11,1... | collective-permute-start | bytes 49160 | tf_op jit(solution)/shard_map/ppermute | solution.py:75
  128.3 6.9 %collective-permute-start.14 = (bf16[64,128]{1,0:T(8,128)(2,1)S(1)}, bf16[64,128]{1,0:T(8,128)(2,1)S(1)}, u32[]{:S(2)}, u32[]{:S(2)}) collective-permute-start(bf16[64,128]{1,0:T(8,128)(2,1)S(1)} %get-tuple-element.274), channel_id=1, source_target_pairs={{0,1},{1,2},{2,3},{3,4},{4,5},{5,6},{6,7},{7,8},{8,9},{9,10},{10,1... | collective-permute-start | bytes 49160 | tf_op jit(solution)/shard_map/ppermute | solution.py:75
  131.4 4.7 %collective-permute-start.15 = (bf16[64,128]{1,0:T(8,128)(2,1)S(1)}, bf16[64,128]{1,0:T(8,128)(2,1)S(1)}, u32[]{:S(2)}, u32[]{:S(2)}) collective-permute-start(bf16[64,128]{1,0:T(8,128)(2,1)S(1)} %get-tuple-element.275), channel_id=1, source_target_pairs={{1,0},{2,1},{3,2},{4,3},{5,4},{6,5},{7,6},{8,7},{9,8},{10,9},{11,1... | collective-permute-start | bytes 49160 | tf_op jit(solution)/shard_map/ppermute | solution.py:75
